TPU v7x, 32 devices: a whole 2x2x4 slice. The times are simulated.
32 devices in a mesh: fsdp: 8 (over y, x, core), tp: 4 (over z).
Axes of the slice: x: 2, y: 2, z: 4, core: 2. Of those that a mesh axis runs over, the one named last changes fastest.
Arguments:
- layer_input: bfloat16 [8192, 2048], P(('fsdp', 'tp')), may hold values from -6 to 6
- teacher: bfloat16 [8192, 2048], P(('fsdp', 'tp')), may hold values from -6 to 6
- out_grad: bfloat16 [8192, 2048], P(('fsdp', 'tp')), may hold values from -6 to 6
- lengths: int32 [8], P('fsdp'), may hold values from 512 to 1024, as said below
- norm_gain: float32 [2048], P(('fsdp', 'tp')), may hold values from 0.5 to 1.5
- norm_bias: float32 [2048], P(('fsdp', 'tp')), may hold values from -4 to 4
- qkv_weight: bfloat16 [3, 2048, 2048], P(None, 'fsdp', 'tp'), may hold values from -0.125 to 0.125
- qkv_bias: bfloat16 [3, 2048], P(None, ('tp', 'fsdp')), may hold values from -4 to 4
- out_weight: bfloat16 [2048, 2048], P('tp', 'fsdp'), may hold values from -1 to 1
- gate_up_weight: bfloat16 [2, 2048, 5632], P(None, 'fsdp', 'tp'), may hold values from -0.125 to 0.125
- down_weight: bfloat16 [5632, 2048], P('tp', 'fsdp'), may hold values from -0.078125 to 0.078125
Outputs:
- output: bfloat16 [8192, 2048], P(('fsdp', 'tp'))
- loss: float32 [], replicated
- input_grad: bfloat16 [8192, 2048], P(('fsdp', 'tp'))
- norm_gain_grad: float32 [2048], P(('fsdp', 'tp'))
- norm_bias_grad: float32 [2048], P(('fsdp', 'tp'))
- qkv_weight_grad: float32 [3, 2048, 2048], P(None, 'fsdp', 'tp')
- qkv_bias_grad: float32 [3, 2048], P(None, ('tp', 'fsdp'))
- out_weight_grad: float32 [2048, 2048], P('tp', 'fsdp')
- gate_up_weight_grad: float32 [2, 2048, 5632], P(None, 'fsdp', 'tp')
- down_weight_grad: float32 [5632, 2048], P('tp', 'fsdp')
Inputs may be any that keep to these rules, and one draw needn't show every extreme that they name: `lengths`: each slot holds at least half of its 1024 positions; some slot is full in every draw.
All inputs are finite; a program needn't handle non-finite values.
Results may differ from a plain program's by a relative error of at most 0.0084.
Values may be sent and summed in bfloat16 or wider, within the bound.
No kernel may reach another device: no remote copies, remote signals or barrier semaphores. Data moves between devices by JAX's collectives and lax.ppermute only.
A program may use at most 256 MiB of HBM per device.

v0:
```python
import jax
import jax.numpy as jnp
from jax import lax
from jax.sharding import PartitionSpec as P

D = 2048
HD = 64
ROT = 16
SEQ = 1024
SEQS_DEV = 1


epsilon = 1e-05


def rotary_tables(row_total):
    half_rot = ROT // 2
    positions = (jnp.arange(row_total, dtype=jnp.int32) % SEQ).astype(jnp.float32)
    frequency = 10000.0 ** (-2.0 * jnp.arange(half_rot, dtype=jnp.float32) / ROT)
    angles = positions[:, None] * frequency[None, :]
    angles = jnp.concatenate([angles, angles], -1)[:, None, :]
    return (jnp.cos(angles), jnp.sin(angles))


def turn_heads(vectors, cos_tab, sine_tab):
    half_rot = ROT // 2
    head_part = vectors[..., :ROT]
    turned = jnp.concatenate([-head_part[..., half_rot:], head_part[..., :half_rot]], -1)
    return jnp.concatenate([head_part * cos_tab + turned * sine_tab, vectors[..., ROT:]], -1)


def unturn_heads(vectors, cos_tab, sine_tab):
    half_rot = ROT // 2
    head_part = vectors[..., :ROT]
    by_sine = head_part * sine_tab
    back_part = jnp.concatenate([by_sine[..., half_rot:], -by_sine[..., :half_rot]], -1)
    return jnp.concatenate([head_part * cos_tab + back_part, vectors[..., ROT:]], -1)


def per_device(
    layer_input,
    teacher,
    out_grad,
    lengths,
    norm_gain,
    norm_bias,
    qkv_weight,
    qkv_bias,
    out_weight,
    gate_up_weight,
    down_weight,
):
    local_rows = layer_input.shape[0]
    group_rows = SEQS_DEV * SEQ
    gain_vec, shift_vec = (
        lax.all_gather(norm_gain, ("fsdp", "tp"), axis=0, tiled=True),
        lax.all_gather(norm_bias, ("fsdp", "tp"), axis=0, tiled=True),
    )
    w_qkv, b_qkv, w_out, w_gu, w_down = (
        lax.all_gather(qkv_weight, "fsdp", axis=1, tiled=True),
        lax.all_gather(qkv_bias, "fsdp", axis=1, tiled=True),
        lax.all_gather(out_weight, "fsdp", axis=1, tiled=True),
        lax.all_gather(gate_up_weight, "fsdp", axis=1, tiled=True),
        lax.all_gather(down_weight, "fsdp", axis=1, tiled=True),
    )
    row_ids = lax.axis_index("tp") * local_rows + jnp.arange(local_rows, dtype=jnp.int32)
    row_pick = (row_ids // SEQ)[:, None] == jnp.arange(SEQS_DEV, dtype=jnp.int32)[None, :]
    row_length = jnp.sum(jnp.where(row_pick, lengths[None, :], 0), 1)
    valid_rows = (row_ids % SEQ < row_length).astype(jnp.float32)
    inputs = layer_input.astype(jnp.float32)
    center = inputs - jnp.mean(inputs, -1, keepdims=True)
    inv_std = lax.rsqrt(jnp.mean(center * center, -1, keepdims=True) + epsilon)
    unit_rows = center * inv_std
    normed = (unit_rows * gain_vec + shift_vec).astype(jnp.bfloat16)
    all_normed = lax.all_gather(normed, "tp", axis=0, tiled=True)
    local_width = w_qkv.shape[2]
    local_heads = local_width // HD
    cos_tab, sine_tab = rotary_tables(group_rows)
    joined_qkv = jnp.einsum(
        "sd,jde->jse", all_normed, w_qkv, preferred_element_type=jnp.float32
    ) + b_qkv[:, None, :].astype(jnp.float32)
    queries = turn_heads(
        joined_qkv[0].reshape(group_rows, local_heads, HD), cos_tab, sine_tab
    ).astype(jnp.bfloat16)
    key_rows = turn_heads(
        joined_qkv[1].reshape(group_rows, local_heads, HD), cos_tab, sine_tab
    ).astype(jnp.bfloat16)
    values = joined_qkv[2].reshape(group_rows, local_heads, HD).astype(jnp.bfloat16)
    span_rows = min(512, SEQ)
    score_scale = HD ** (-0.5)
    key_pos = jnp.arange(SEQ, dtype=jnp.int32)
    block_count = group_rows // span_rows
    block_ids = jnp.arange(block_count, dtype=jnp.int32)

    def block_scores(block_id):
        row_start = block_id * span_rows
        seq_start = row_start // SEQ * SEQ
        q_block = lax.dynamic_slice_in_dim(queries, row_start, span_rows, 0)
        scores = (
            jnp.einsum("qhe,khe->hqk", q_block, key_rows, preferred_element_type=jnp.float32)
            * score_scale
        )
        query_pos = row_start - seq_start + jnp.arange(span_rows, dtype=jnp.int32)
        allowed = (key_pos[None, :] <= query_pos[:, None])[None]
        scores = jnp.where(allowed, scores, -1e30)
        return (row_start, seq_start, q_block, key_rows, values, scores, allowed)

    def attend(block_id):
        row_start, seq_start, q_block, k_seq, v_seq, scores, allowed = block_scores(block_id)
        row_max = jnp.max(scores, -1, keepdims=True)
        shifted = jnp.exp(scores - row_max)
        totals = jnp.sum(shifted, -1, keepdims=True)
        weights = (shifted / totals).astype(jnp.bfloat16)
        out_block = jnp.einsum("hqk,khe->qhe", weights, v_seq, preferred_element_type=jnp.float32)
        return (out_block, row_max + jnp.log(totals))

    attended, log_sums = lax.map(attend, block_ids)
    attn_rows = attended.reshape(group_rows, local_width).astype(jnp.bfloat16)
    gate_up = jnp.einsum("sd,jdf->jsf", all_normed, w_gu, preferred_element_type=jnp.float32)
    sigmoid_gate = jax.nn.sigmoid(gate_up[0])
    hidden = (gate_up[0] * sigmoid_gate * gate_up[1]).astype(jnp.bfloat16)
    branch_sum = lax.psum_scatter(
        jnp.dot(attn_rows, w_out, preferred_element_type=jnp.float32)
        + jnp.dot(hidden, w_down, preferred_element_type=jnp.float32),
        "tp",
        scatter_dimension=0,
        tiled=True,
    )
    result = inputs + valid_rows[:, None] * branch_sum
    mismatch = result - teacher.astype(jnp.float32)
    loss_part = jnp.sum(valid_rows[:, None] * mismatch * mismatch)
    count_part = jnp.sum(valid_rows)
    loss_total, valid_total = lax.psum((loss_part, count_part), ("fsdp", "tp"))
    loss_value = loss_total / (valid_total * D)
    seed_rows = valid_rows[:, None] * (out_grad.astype(jnp.float32) + mismatch)
    all_seed = lax.all_gather(seed_rows.astype(jnp.bfloat16), "tp", axis=0, tiled=True)
    w_qkv, w_out, w_gu, w_down = (
        lax.all_gather(qkv_weight, "fsdp", axis=1, tiled=True),
        lax.all_gather(out_weight, "fsdp", axis=1, tiled=True),
        lax.all_gather(gate_up_weight, "fsdp", axis=1, tiled=True),
        lax.all_gather(down_weight, "fsdp", axis=1, tiled=True),
    )
    grad_out_w = jnp.einsum("sa,sd->ad", attn_rows, all_seed, preferred_element_type=jnp.float32)
    grad_attn = (
        jnp.einsum("sd,ad->sa", all_seed, w_out, preferred_element_type=jnp.float32)
        .astype(jnp.bfloat16)
        .reshape(group_rows, local_heads, HD)
    )
    grad_down = jnp.einsum("sf,sd->fd", hidden, all_seed, preferred_element_type=jnp.float32)
    grad_hidden = jnp.einsum("sd,fd->sf", all_seed, w_down, preferred_element_type=jnp.float32)
    grad_gate = grad_hidden * gate_up[1] * sigmoid_gate * (1.0 + gate_up[0] * (1.0 - sigmoid_gate))
    grad_up = grad_hidden * gate_up[0] * sigmoid_gate
    grad_gu = jnp.stack([grad_gate, grad_up]).astype(jnp.bfloat16)
    grad_gu_w = jnp.einsum("sd,jsf->jdf", all_normed, grad_gu, preferred_element_type=jnp.float32)

    def attend_back(kv_grads, block_id):
        grad_keys, grad_values = kv_grads
        row_start, seq_start, q_block, k_seq, v_seq, scores, allowed = block_scores(block_id)
        probs = jnp.where(allowed, jnp.exp(scores - log_sums[block_id]), 0.0)
        d_block = lax.dynamic_slice_in_dim(grad_attn, row_start, span_rows, 0)
        grad_probs = jnp.einsum("qhe,khe->hqk", d_block, v_seq, preferred_element_type=jnp.float32)
        inner = jnp.sum(probs * grad_probs, -1, keepdims=True)
        grad_scores = (probs * (grad_probs - inner)).astype(jnp.bfloat16)
        grad_query = (
            jnp.einsum("hqk,khe->qhe", grad_scores, k_seq, preferred_element_type=jnp.float32)
            * score_scale
        )
        key_part = (
            jnp.einsum("hqk,qhe->khe", grad_scores, q_block, preferred_element_type=jnp.float32)
            * score_scale
        )
        value_part = jnp.einsum(
            "hqk,qhe->khe", probs.astype(jnp.bfloat16), d_block, preferred_element_type=jnp.float32
        )
        key_now = grad_keys
        grad_keys = key_now + key_part
        value_now = grad_values
        grad_values = value_now + value_part
        return ((grad_keys, grad_values), grad_query)

    zero_heads = jnp.zeros((group_rows, local_heads, HD), jnp.float32)
    (grad_keys, grad_values), grad_queries = lax.scan(
        attend_back, (zero_heads, zero_heads), block_ids
    )
    grad_queries = grad_queries.reshape(group_rows, local_heads, HD)
    grad_qkv = (
        jnp.stack(
            [
                unturn_heads(grad_queries, cos_tab, sine_tab),
                unturn_heads(grad_keys, cos_tab, sine_tab),
                grad_values,
            ]
        )
        .reshape(3, group_rows, local_width)
        .astype(jnp.bfloat16)
    )
    grad_bias = jnp.sum(grad_qkv, 1, dtype=jnp.float32)
    grad_qkv_w = jnp.einsum("sd,jse->jde", all_normed, grad_qkv, preferred_element_type=jnp.float32)
    grad_normed = lax.psum_scatter(
        jnp.einsum("jse,jde->sd", grad_qkv, w_qkv, preferred_element_type=jnp.float32)
        + jnp.einsum("jsf,jdf->sd", grad_gu, w_gu, preferred_element_type=jnp.float32),
        "tp",
        scatter_dimension=0,
        tiled=True,
    )
    gain_grad_part = jnp.sum(grad_normed * unit_rows, 0)
    bias_grad_part = jnp.sum(grad_normed, 0)
    grad_unit = grad_normed * gain_vec
    grad_inputs = inv_std * (
        grad_unit
        - jnp.mean(grad_unit, -1, keepdims=True)
        - unit_rows * jnp.mean(grad_unit * unit_rows, -1, keepdims=True)
    )
    input_grad = (seed_rows + grad_inputs).astype(jnp.bfloat16)
    gain_grad, bias_grad = (
        lax.psum_scatter(gain_grad_part, ("fsdp", "tp"), scatter_dimension=0, tiled=True),
        lax.psum_scatter(bias_grad_part, ("fsdp", "tp"), scatter_dimension=0, tiled=True),
    )
    qkv_w_grad, qkv_b_grad, out_w_grad, gu_w_grad, down_w_grad = (
        lax.psum_scatter(grad_qkv_w, "fsdp", scatter_dimension=1, tiled=True),
        lax.psum_scatter(grad_bias, "fsdp", scatter_dimension=1, tiled=True),
        lax.psum_scatter(grad_out_w, "fsdp", scatter_dimension=1, tiled=True),
        lax.psum_scatter(grad_gu_w, "fsdp", scatter_dimension=1, tiled=True),
        lax.psum_scatter(grad_down, "fsdp", scatter_dimension=1, tiled=True),
    )
    return (
        result.astype(jnp.bfloat16),
        loss_value,
        input_grad,
        gain_grad,
        bias_grad,
        qkv_w_grad,
        qkv_b_grad,
        out_w_grad,
        gu_w_grad,
        down_w_grad,
    )


def solution(mesh):
    placed = (
        P(("fsdp", "tp"), None),
        P(("fsdp", "tp"), None),
        P(("fsdp", "tp"), None),
        P("fsdp"),
        P(("fsdp", "tp")),
        P(("fsdp", "tp")),
        P(None, "fsdp", "tp"),
        P(None, ("tp", "fsdp")),
        P("tp", "fsdp"),
        P(None, "fsdp", "tp"),
        P("tp", "fsdp"),
    )
    return jax.shard_map(
        per_device,
        mesh=mesh,
        in_specs=placed,
        out_specs=(
            P(("fsdp", "tp"), None),
            P(),
            P(("fsdp", "tp"), None),
            P(("fsdp", "tp")),
            P(("fsdp", "tp")),
            P(None, "fsdp", "tp"),
            P(None, ("tp", "fsdp")),
            P("tp", "fsdp"),
            P(None, "fsdp", "tp"),
            P("tp", "fsdp"),
        ),
        check_vma=False,
    )
```

profile of v0, /device:TPU:0, one launch (start us, length us, event | category | flops | bytes accessed | tf_op | source)
XLA Modules:
  0.0 1318.2 jit_solution(7497582739152333700)
XLA Ops:
  12.2 42.0 %all-reduce.5 = (f32[2048]{0:T(1024)S(1)}, f32[2048]{0:T(1024)S(1)}) all-reduce(f32[2048]{0:T(1024)S(1)} %dynamic-update-slice.1, f32[2048]{0:T(1024)S(1)} %dynamic-update-slice), channel_id=1, replica_groups=mesh['fsdp'=8,'tp'=4] {'fsdp','tp'}, use_global_device_ids=true, to_apply=%add.1 | all-reduce | flops 4096 | bytes 32768
  54.2 2.7 fusion.44
  60.2 9.9 all-gather
  70.3 67.4 %all-gather.8.cloned.1.call-done = bf16[1024,2048]{1,0:T(8,128)(2,1)} async-done(((bf16[256,2048]{1,0:T(8,128)(2,1)}), bf16[1024,2048]{1,0:T(8,128)(2,1)}) %all-gather.8.cloned.1.call-update) | async-done | bytes 4194320 | tf_op jit(solution)/shard_map/all_gather | solution.py:75
  137.8 47.7 %all-gather.10.cloned.1.call-done = bf16[3,2048,512]{1,2,0:T(8,128)(2,1)} async-done(((bf16[3,256,512]{1,2,0:T(8,128)(2,1)}), bf16[3,2048,512]{1,2,0:T(8,128)(2,1)}) %all-gather.10.cloned.1.call-update) | async-done | bytes 6291472 | tf_op jit(solution)/shard_map/all_gather | solution.py:60
  185.4 10.1 add_bitcast_fusion
  199.0 32.3 %while.32 = (s32[]{:T(128)}, bf16[2,512,8,64]{1,3,2,0:T(8,128)(2,1)S(1)}, f32[2,8,512,1]{2,1,3,0:T(8,128)S(1)}, s32[2]{0:T(128)S(1)}, bf16[1024,8,64]{0,2,1:T(8,...) while((s32[]{:T(128)}, ...), condition=%wide.region_5.6_spmd.clone, body=%wide.region_2.5_spmd.clone.sunk | while | flops 1124594176 | bytes 56234364 | solution.py:117
  200.6 4.1 fusion.118
  204.8 4.2 fusion.119
  209.0 5.9 fusion.120
  216.6 4.1 fusion.118
  220.8 4.2 fusion.119
  225.0 5.9 fusion.120
  232.7 22.4 %all-gather.14.cloned.1.call-done = bf16[2,2048,1408]{2,1,0:T(8,128)(2,1)} async-done(((bf16[2,256,1408]{2,1,0:T(8,128)(2,1)}), bf16[2,2048,1408]{2,1,0:T(8,128)(2,1)}) %all-gather.14.cloned.1.call-update) | async-done | bytes 11534352 | tf_op jit(solution)/shard_map/all_gather | solution.py:63
  255.1 17.2 %convolution_bitcast_fusion.1 = f32[2,1024,1408]{2,1,0:T(8,128)S(1)} fusion(bf16[2,2048,1408]{2,1,0:T(8,128)(2,1)} %all-gather.14.cloned.1.call-done, bf16[1024,2048]{1,0:T(8,128)(2,1)} %all-gather.8.cloned.1.call-done), kind=kOutput, calls=%fused_computation.41 | convolution fusion | flops 11811160064 | bytes 27262976 | tf_op jit(solution)/shard_map/sd,jdf->jsf/dot_general | solution.py:119
  272.3 4.2 copy-done.8
  276.5 2.8 multiply_convert_fusion.3
  279.3 21.9 %all-gather.16.cloned.1.call-done = bf16[1408,2048]{1,0:T(8,128)(2,1)} async-done(((bf16[1408,256]{1,0:T(8,128)(2,1)}), bf16[1408,2048]{1,0:T(8,128)(2,1)}) %all-gather.16.cloned.1.call-update) | async-done | bytes 5767184 | tf_op jit(solution)/shard_map/all_gather | solution.py:64
  301.2 11.6 fusion.74
  312.8 18.3 %all-gather.12.cloned.1.call-done = bf16[512,2048]{1,0:T(8,128)(2,1)} async-done(((bf16[512,256]{1,0:T(8,128)(2,1)}), bf16[512,2048]{1,0:T(8,128)(2,1)}) %all-gather.12.cloned.1.call-update) | async-done | bytes 2097168 | tf_op jit(solution)/shard_map/all_gather | solution.py:62
  331.2 9.7 convolution_add_fusion
  341.7 143.8 %reduce-scatter.10.cloned.1.call-done = f32[256,2048]{1,0:T(8,128)} async-done(((f32[1024,2048]{1,0:T(8,128)}), f32[256,2048]{1,0:T(8,128)}) %reduce-scatter.10.cloned.1.call-update) | async-done | bytes 2097168 | tf_op jit(solution)/shard_map/reduce_scatter | solution.py:122
  485.5 3.7 fusion.59
  489.3 81.6 %all-gather.18.cloned.1.call-done = bf16[1024,2048]{1,0:T(8,128)(2,1)} async-done(((bf16[256,2048]{1,0:T(8,128)(2,1)}), bf16[1024,2048]{1,0:T(8,128)(2,1)}) %all-gather.18.cloned.1.call-update) | async-done | bytes 4194320 | tf_op jit(solution)/shard_map/all_gather | solution.py:136
  570.8 6.2 convolution_convert_fusion
  577.0 134.3 %while.33 = (s32[]{:T(128)}, f32[1024,8,64]{0,2,1:T(8,128)}, f32[1024,8,64]{0,2,1:T(8,128)}, f32[2,512,8,64]{1,0,3,2:T(2,128)}, s32[2]{0:T(128)S(1)}, /*index=5*...) while((s32[]{:T(128)}, f32[1024,8,64]{0,2,1:T(8,128)}, ...), condition=%wide.region_13.14_spmd.clone, body=%wide.region_11.13_spmd.clone.sunk | while | flops 2729701888 | bytes 200626816 | solution.py:182
  582.2 3.8 fusion.130
  586.0 12.2 multiply_reduce_fusion.3
  598.2 9.4 multiply_convert_fusion.5
  607.6 8.9 bitcast_add_fusion.6
  616.5 2.7 fusion.131
  619.2 2.9 bitcast_add_fusion.5
  622.1 2.0 copy.85
  624.1 19.7 %dynamic_update_slice.30 = f32[2,512,8,64]{1,0,3,2:T(2,128)} dynamic-update-slice(f32[2,512,8,64]{1,0,3,2:T(2,128)} %get-tuple-element.597, f32[1,512,8,64]{1,0,3,2:T(1,128)} %copy.85, s32[]{:T(128)S(6)} %copy.104, s32[]{:T(128)} %constant.200.clone.1..sunk.1, s32[]{:T(128)} %constant.200.clone.1..sunk.1, s32[]{:T(128)} %constant.200.clone.1..sunk.1) | dynamic-update-slice | bytes 2097156 | tf_op jit(solution)/shard_map/while/body/jit(dynamic_update_index_in_dim)/dynamic_update_slice | solution.py:117
  648.8 3.8 fusion.130
  652.5 12.3 multiply_reduce_fusion.3
  664.8 9.4 multiply_convert_fusion.5
  674.2 9.5 bitcast_add_fusion.6
  683.7 2.7 fusion.131
  686.4 2.9 bitcast_add_fusion.5
  689.3 2.0 copy.85
  691.3 19.7 %dynamic_update_slice.30 = f32[2,512,8,64]{1,0,3,2:T(2,128)} dynamic-update-slice(f32[2,512,8,64]{1,0,3,2:T(2,128)} %get-tuple-element.597, f32[1,512,8,64]{1,0,3,2:T(1,128)} %copy.85, s32[]{:T(128)S(6)} %copy.104, s32[]{:T(128)} %constant.200.clone.1..sunk.1, s32[]{:T(128)} %constant.200.clone.1..sunk.1, s32[]{:T(128)} %constant.200.clone.1..sunk.1) | dynamic-update-slice | bytes 2097156 | tf_op jit(solution)/shard_map/while/body/jit(dynamic_update_index_in_dim)/dynamic_update_slice | solution.py:117
  711.4 4.2 reshape.270
  721.2 2.7 convert.56
  726.8 15.7 %fusion.34 = (bf16[1,1024,1408]{2,1,0:T(8,128)(2,1)}, bf16[1,1024,1408]{2,1,0:T(8,128)(2,1)}) fusion(f32[2,1024,1408]{2,1,0:T(8,128)} %copy-done.8, bf16[1024,2048]{1,0:T(8,128)(2,1)} %all-gather.18.cloned.1.call-done, bf16[1408,2048]{1,0:T(8,128)(2,1)} %all-gather.16.cloned.1.call-done), kind=kOutput, calls=%fused_computation.64 | convolution fusion | flops 5924323328 | bytes 27262976 | tf_op jit(solution)/shard_map/sd,fd->sf/dot_general | solution.py:150
  742.5 10.8 fusion.69
  753.3 20.0 %bitcast_add_fusion.2 = f32[1024,2048]{1,0:T(8,128)} fusion(f32[1024,2048,1]{1,0,2:T(8,128)} %fusion.69, bf16[2,2048,1408]{2,1,0:T(8,128)(2,1)} %all-gather.14.cloned.1.call-done, bf16[1,1024,1408]{2,1,0:T(8,128)(2,1)} %get-tuple-element.399, bf16[1,1024,1408]{2,1,0:T(8,128)(2,1)} %get-tuple-element.398), kind=kOutput, calls=%fused_computation.40 | convolution fusion | flops 11816140800 | bytes 34078720 | tf_op jit(solution)/shard_map/jsf,jdf->sd/dot_general | solution.py:201
  773.3 12.2 convolution_bitcast_fusion.2
  785.6 1.8 copy-done.30
  787.4 19.1 %convolution_bitcast_fusion = f32[2,2048,1408]{1,2,0:T(8,128)} fusion(bf16[1024,2048]{1,0:T(8,128)(2,1)} %all-gather.8.cloned.1.call-done, bf16[1,1024,1408]{2,1,0:T(8,128)(2,1)} %get-tuple-element.399, bf16[1,1024,1408]{2,1,0:T(8,128)(2,1)S(1)} %copy-done.30), kind=kOutput, calls=%fused_computation.39 | convolution fusion | flops 11814043648 | bytes 33030144 | tf_op jit(solution)/shard_map/sd,jsf->jdf/dot_general | solution.py:154
  807.8 6.5 fusion.75
  814.3 1.7 copy-done.13
  816.1 10.7 fusion.76
  827.5 1.7 copy.70
  829.2 87.2 %reduce-scatter.12.cloned.1.call-done = f32[256,2048]{1,0:T(8,128)} async-done(((f32[1024,2048]{1,0:T(8,128)}), f32[256,2048]{1,0:T(8,128)}) %reduce-scatter.12.cloned.1.call-update) | async-done | bytes 2097168 | tf_op jit(solution)/shard_map/reduce_scatter | solution.py:199
  916.4 4.2 fusion.50
  920.6 41.6 %all-reduce.4 = (f32[]{:T(128)}, f32[]{:T(128)}, f32[2048]{0:T(1024)S(1)}, f32[2048]{0:T(1024)S(1)}) all-reduce(f32[]{:T(128)} %get-tuple-element.353, f32[]{:T(128)} %fusion.68, f32[2048]{0:T(1024)S(1)} %get-tuple-element.349, f32[2048]{0:T(1024)S(1)} %get-tuple-element.352), channel_id=1, replica_groups=mesh['fsdp'=8,'tp'=4] {'fsdp','tp'}, use_global_device_ids=true, to_apply=%region_8.9 | all-reduce | flops 4098 | bytes 32784 | tf_op jit(solution)/shard_map/psum | solution.py:133
  964.7 5.0 fusion.49
  969.7 44.2 %reduce-scatter.14.cloned.1.call-done = f32[3,256,512]{1,2,0:T(8,128)} async-done(((f32[3,2048,512]{1,2,0:T(8,128)}), f32[3,256,512]{1,2,0:T(8,128)}) %reduce-scatter.14.cloned.1.call-update) | async-done | bytes 1572880 | tf_op jit(solution)/shard_map/reduce_scatter | solution.py:220
  1013.9 3.0 copy.64
  1016.9 147.0 %reduce-scatter.18.cloned.1.call-done = f32[2,256,1408]{1,2,0:T(8,128)} async-done(((f32[2,2048,1408]{1,2,0:T(8,128)}), f32[2,256,1408]{1,2,0:T(8,128)}) %reduce-scatter.18.cloned.1.call-update) | async-done | bytes 2883600 | tf_op jit(solution)/shard_map/reduce_scatter | solution.py:223
  1163.9 3.4 copy.65
  1167.3 52.1 %reduce-scatter.16.cloned.1.call-done = f32[512,256]{1,0:T(8,128)} async-done(((f32[512,2048]{1,0:T(8,128)}), f32[512,256]{1,0:T(8,128)}) %reduce-scatter.16.cloned.1.call-update) | async-done | bytes 524304 | tf_op jit(solution)/shard_map/reduce_scatter | solution.py:222
  1219.5 90.9 %reduce-scatter.20.cloned.1.call-done = f32[1408,256]{1,0:T(8,128)} async-done(((f32[1408,2048]{1,0:T(8,128)}), f32[1408,256]{1,0:T(8,128)}) %reduce-scatter.20.cloned.1.call-update) | async-done | bytes 1441808 | tf_op jit(solution)/shard_map/reduce_scatter | solution.py:224
  (165 shorter events, 31.5 us)
Async XLA Ops:
  7.2 49.8 %copy-start.14 = (bf16[3,256,512]{2,1,0:T(8,128)(2,1)S(1)}, bf16[3,256,512]{2,1,0:T(8,128)(2,1)}, u32[]{:S(2)}) copy-start(bf16[3,256,512]{2,1,0:T(8,128)(2,1)} %param.21) | copy-start | bytes 2359300
  7.2 130.6 %all-gather.8.cloned.1.call-start = ((), (), s32[]{:S(2)}) async-start(), calls=%async_computation.7 | async-start | bytes 5242880 | tf_op jit(solution)/shard_map/all_gather | solution.py:75
  8.8 49.4 %copy-start.23 = (f32[256]{0:T(256)}, f32[256]{0:T(256)S(1)}, u32[]{:S(2)}) copy-start(f32[256]{0:T(256)S(1)} %broadcast_multiply_fusion.3) | copy-start | bytes 3076
  10.4 48.5 %copy-start.25 = (f32[256]{0:T(256)}, f32[256]{0:T(256)S(1)}, u32[]{:S(2)}) copy-start(f32[256]{0:T(256)S(1)} %add_rsqrt_fusion) | copy-start | bytes 3076
  54.2 4.7 copy-start.21
  56.9 3.3 copy-start.29
  56.9 128.6 %all-gather.10.cloned.1.call-start = ((), (), s32[]{:S(2)}) async-start(), calls=%async_computation.8 | async-start | bytes 7077888 | tf_op jit(solution)/shard_map/all_gather | solution.py:60
  58.1 196.9 %all-gather.14.cloned.1.call-start = ((), (), s32[]{:S(2)}) async-start(), calls=%async_computation.10 | async-start | bytes 12976128 | tf_op jit(solution)/shard_map/all_gather | solution.py:63
  58.9 242.3 %all-gather.16.cloned.1.call-start = ((), (), s32[]{:S(2)}) async-start(), calls=%async_computation.11 | async-start | bytes 6488064 | tf_op jit(solution)/shard_map/all_gather | solution.py:64
  59.5 271.7 %all-gather.12.cloned.1.call-start = ((), (), s32[]{:S(2)}) async-start(), calls=%async_computation.9 | async-start | bytes 2359296 | tf_op jit(solution)/shard_map/all_gather | solution.py:62
  60.1 425.4 %reduce-scatter.10.cloned.1.call-start = ((), (), s32[]{:S(2)}) async-start(), calls=%async_computation.12 | async-start | bytes 10485760 | tf_op jit(solution)/shard_map/reduce_scatter | solution.py:122
  70.3 127.3 %copy-start.15 = (f32[1024,16]{0,1:T(8,128)}, f32[1024,16]{0,1:T(8,128)S(1)}, u32[]{:S(2)}) copy-start(f32[1024,16]{0,1:T(8,128)S(1)} %get-tuple-element.419) | copy-start | bytes 196612
  70.3 127.3 %copy-start.17 = (f32[1024,16]{0,1:T(8,128)}, f32[1024,16]{0,1:T(8,128)S(1)}, u32[]{:S(2)}) copy-start(f32[1024,16]{0,1:T(8,128)S(1)} %get-tuple-element.418) | copy-start | bytes 196612
  232.7 98.5 %copy-start.11 = (bf16[64,8,2,512]{3,1,2,0:T(8,128)(2,1)}, bf16[64,8,2,512]{3,1,2,0:T(8,128)(2,1)S(1)}, u32[]{:S(2)}) copy-start(bf16[64,8,2,512]{3,1,2,0:T(8,128)(2,1)S(1)} %copy.82) | copy-start | bytes 3145732
  272.3 4.2 copy-start.8
  340.8 144.7 %copy-start.4 = (bf16[256,2048]{1,0:T(8,128)(2,1)S(1)}, bf16[256,2048]{1,0:T(8,128)(2,1)}, u32[]{:S(2)}) copy-start(bf16[256,2048]{1,0:T(8,128)(2,1)} %param.15) | copy-start | bytes 3145732
  340.9 144.7 %copy-start.9 = (bf16[256,2048]{1,0:T(8,128)(2,1)S(1)}, bf16[256,2048]{1,0:T(8,128)(2,1)}, u32[]{:S(2)}) copy-start(bf16[256,2048]{1,0:T(8,128)(2,1)} %param.16) | copy-start | bytes 3145732
  340.9 230.0 %all-gather.18.cloned.1.call-start = ((), (), s32[]{:S(2)}) async-start(), calls=%async_computation.13 | async-start | bytes 5242880 | tf_op jit(solution)/shard_map/all_gather | solution.py:136
  341.7 147.4 %copy-start.27 = (f32[256]{0:T(256)}, f32[256]{0:T(256)S(1)}, u32[]{:S(2)}) copy-start(f32[256]{0:T(256)S(1)} %compare_convert_fusion) | copy-start | bytes 3076
  489.2 338.3 %reduce-scatter.22.cloned.1.call-start = ((), (), s32[]{:S(2)}) async-start(), calls=%async_computation.19 | async-start | bytes 294912
  577.2 3.8 copy-start.19
  598.2 9.4 copy-start.6
  607.6 8.9 copy-start
  616.5 2.7 copy-start.1
  622.0 21.7 %copy-start.2 = (f32[1024,8,64]{0,2,1:T(8,128)}, f32[1024,8,64]{0,2,1:T(8,128)S(1)}, u32[]{:S(2)}) copy-start(f32[1024,8,64]{0,2,1:T(8,128)S(1)} %bitcast_add_fusion.5) | copy-start | bytes 6291460 | tf_op jit(solution)/shard_map/while
  622.0 21.7 %copy-start.20 = (f32[2,8,512,1]{2,1,3,0:T(8,128)S(1)}, f32[2,8,512,1]{2,1,3,0:T(8,128)}, u32[]{:S(2)}) copy-start(f32[2,8,512,1]{2,1,3,0:T(8,128)} %copy-done.19) | copy-start | bytes 98308 | tf_op jit(solution)/shard_map/while
  643.8 3.8 copy-start.19
  664.8 9.4 copy-start.6
  674.2 9.6 copy-start
  683.7 2.7 copy-start.1
  689.3 21.7 %copy-start.2 = (f32[1024,8,64]{0,2,1:T(8,128)}, f32[1024,8,64]{0,2,1:T(8,128)S(1)}, u32[]{:S(2)}) copy-start(f32[1024,8,64]{0,2,1:T(8,128)S(1)} %bitcast_add_fusion.5) | copy-start | bytes 6291460 | tf_op jit(solution)/shard_map/while
  689.3 21.7 %copy-start.20 = (f32[2,8,512,1]{2,1,3,0:T(8,128)S(1)}, f32[2,8,512,1]{2,1,3,0:T(8,128)}, u32[]{:S(2)}) copy-start(f32[2,8,512,1]{2,1,3,0:T(8,128)} %copy-done.19) | copy-start | bytes 98308 | tf_op jit(solution)/shard_map/while
  711.4 6.0 copy-start.3
  711.4 6.9 copy-start.16
  715.6 2.7 copy-start.10
  717.3 1.2 copy-start.18
  726.8 189.7 %reduce-scatter.12.cloned.1.call-start = ((), (), s32[]{:S(2)}) async-start(), calls=%async_computation.14 | async-start | bytes 10485760 | tf_op jit(solution)/shard_map/reduce_scatter | solution.py:199
  773.3 240.6 %reduce-scatter.14.cloned.1.call-start = ((), (), s32[]{:S(2)}) async-start(), calls=%async_computation.15 | async-start | bytes 14155776 | tf_op jit(solution)/shard_map/reduce_scatter | solution.py:220
  785.6 1.8 copy-start.30
  785.6 378.3 %reduce-scatter.18.cloned.1.call-start = ((), (), s32[]{:S(2)}) async-start(), calls=%async_computation.17 | async-start | bytes 25952256 | tf_op jit(solution)/shard_map/reduce_scatter | solution.py:223
  806.5 1.3 copy-start.12
  806.6 412.9 %reduce-scatter.16.cloned.1.call-start = ((), (), s32[]{:S(2)}) async-start(), calls=%async_computation.16 | async-start | bytes 4718592 | tf_op jit(solution)/shard_map/reduce_scatter | solution.py:222
  814.3 1.8 copy-start.13
  814.3 496.0 %reduce-scatter.20.cloned.1.call-start = ((), (), s32[]{:S(2)}) async-start(), calls=%async_computation.18 | async-start | bytes 12976128 | tf_op jit(solution)/shard_map/reduce_scatter | solution.py:224
  826.8 89.6 %copy-start.5 = (bf16[256,2048]{1,0:T(8,128)(2,1)S(1)}, bf16[256,2048]{1,0:T(8,128)(2,1)}, u32[]{:S(2)}) copy-start(bf16[256,2048]{1,0:T(8,128)(2,1)} %param.15) | copy-start | bytes 3145732
  826.8 89.6 %copy-start.7 = (f32[256,2048]{1,0:T(8,128)S(1)}, f32[256,2048]{1,0:T(8,128)}, u32[]{:S(2)}) copy-start(f32[256,2048]{1,0:T(8,128)} %reduce-scatter.10.cloned.1.call-done) | copy-start | bytes 6291460
  826.8 89.6 %copy-start.22 = (f32[2048]{0:T(1024)S(1)}, f32[2048]{0:T(1024)}, u32[]{:S(2)}) copy-start(f32[2048]{0:T(1024)} %copy-done.21) | copy-start | bytes 24580
  826.8 89.6 %copy-start.24 = (f32[256]{0:T(256)S(1)}, f32[256]{0:T(256)}, u32[]{:S(2)}) copy-start(f32[256]{0:T(256)} %copy-done.23) | copy-start | bytes 3076
  826.8 89.6 %copy-start.26 = (f32[256]{0:T(256)S(1)}, f32[256]{0:T(256)}, u32[]{:S(2)}) copy-start(f32[256]{0:T(256)} %copy-done.25) | copy-start | bytes 3076
  826.8 89.6 %copy-start.28 = (f32[256]{0:T(256)S(1)}, f32[256]{0:T(256)}, u32[]{:S(2)}) copy-start(f32[256]{0:T(256)} %copy-done.27) | copy-start | bytes 3076
Sparse Core Ops, SparseCore 0:
  57.0 80.7 all-gather.7
  140.2 45.1 all-gather.9
  187.4 67.6 all-gather.13
  256.8 44.3 all-gather.15
  302.9 28.1 all-gather.11
  341.0 144.4 reduce-scatter.9
  489.3 81.4 all-gather.17
  726.9 32.1 reduce-scatter.21
  773.4 142.9 reduce-scatter.11
  920.2 93.7 reduce-scatter.13
  1018.0 145.9 reduce-scatter.17
  1168.1 51.3 reduce-scatter.15
  1223.5 86.7 reduce-scatter.19
where the time goes:
time: 1320 us
  waiting for transfers between devices  826 us (63%)
  matrix products  231 us (18%)
  blocking collectives  93.6 us (7%)
  local copies, waits for them, and re-layouts  81.9 us (6%)
  other arithmetic  59 us (4%)
  between operations  17.9 us (1%)
    reduce_scatter x1, waiting for transfers between devices, per_device(): lax.psum_scatter(grad_gu_w, 'fsdp', scatter_dimension=1, tiled=True)  147 us
    reduce_scatter x1, waiting for transfers between devices, per_device(): lax.psum_scatter(jnp.dot(attn_rows, w_out, preferred_element_type=jnp.flo...  144 us
    reduce_scatter x1, waiting for transfers between devices, per_device(): lax.psum_scatter(grad_down, 'fsdp', scatter_dimension=1, tiled=True)  90.9 us
    reduce_scatter x1, waiting for transfers between devices, per_device(): lax.psum_scatter(jnp.einsum('jse,jde->sd', grad_qkv, w_qkv, preferred_ele...  87.2 us
    all_gather x1, waiting for transfers between devices, per_device(): lax.all_gather(seed_rows.astype(jnp.bfloat16), 'tp', axis=0, tiled=True)  81.6 us
    all_gather x1, waiting for transfers between devices, per_device(): all_normed = lax.all_gather(normed, 'tp', axis=0, tiled=True)  67.4 us
    reduce_scatter x1, waiting for transfers between devices, per_device(): lax.psum_scatter(grad_out_w, 'fsdp', scatter_dimension=1, tiled=True)  52.1 us
    all_gather x1, waiting for transfers between devices, per_device(): lax.all_gather(qkv_weight, 'fsdp', axis=1, tiled=True)  47.7 us
  transfers between devices with their start and end apart: 13, of which 12 were waited for; matrix products, arithmetic and copies ran while one was open for 15% of the time, Pallas kernels for 0%

commit v1 on v0

v1 whole, which is shorter than its diff:
```python
import functools

import jax
import jax.numpy as jnp
from jax import lax
from jax.experimental import pallas as pl
from jax.experimental.pallas import tpu as pltpu
from jax.sharding import Mesh
from jax.sharding import PartitionSpec as P

D = 2048
HD = 64
ROT = 16
SEQ = 1024
PAIR = 2 * HD
SPAN = 256
epsilon = 1e-05
f32 = jnp.float32
bf16 = jnp.bfloat16


def swap_core(a):
    return lax.ppermute(a, "core", [(0, 1), (1, 0)])


def gather_axis(a, axis, n):
    me = lax.axis_index(axis)
    buf = a[None]
    k = 1
    while k < n:
        other = lax.ppermute(buf, axis, [(j, j ^ k) for j in range(n)])
        upper = (me // k) % 2 == 1
        buf = jnp.concatenate(
            [jnp.where(upper, other, buf), jnp.where(upper, buf, other)], 0
        )
        k *= 2
    return buf


def scatter_axis(a, axis, n):
    me = lax.axis_index(axis)
    buf = a
    k = n // 2
    while k >= 1:
        upper = (me // k) % 2 == 1
        lo, hi = buf[:k], buf[k:]
        sent = lax.ppermute(
            jnp.where(upper, lo, hi), axis, [(j, j ^ k) for j in range(n)]
        )
        buf = jnp.where(upper, hi, lo) + sent
        k //= 2
    return buf[0]


def line_gather(piece, n):
    me = lax.axis_index("tp")
    rows = piece.shape[0]
    ups, downs = [], []
    cur = piece
    for s in range(n - 1):
        cur = lax.ppermute(cur, "tp", [(k, k + 1) for k in range(s, n - 1)])
        ups.append(cur)
    cur = piece
    for s in range(n - 1):
        cur = lax.ppermute(cur, "tp", [(k, k - 1) for k in range(1, n - s)])
        downs.append(cur)
    out = jnp.zeros((n * rows,) + piece.shape[1:], piece.dtype)
    for s in reversed(range(n - 1)):
        out = lax.dynamic_update_slice_in_dim(out, ups[s], jnp.maximum(me - 1 - s, 0) * rows, 0)
        out = lax.dynamic_update_slice_in_dim(
            out, downs[s], jnp.minimum(me + 1 + s, n - 1) * rows, 0
        )
    return lax.dynamic_update_slice_in_dim(out, piece, me * rows, 0)


def line_scatter(part, n):
    me = lax.axis_index("tp")
    rows = part.shape[0] // n

    def chunk(j):
        return lax.dynamic_slice_in_dim(part, jnp.clip(j, 0, n - 1) * rows, rows, 0)

    up = down = None
    for s in range(n - 1):
        val = chunk(n - 1 - s + me)
        if up is not None:
            val = val + up.astype(f32)
        up = lax.ppermute(val.astype(bf16), "tp", [(k, k + 1) for k in range(s + 1)])
        val = chunk(s - (n - 1) + me)
        if down is not None:
            val = val + down.astype(f32)
        down = lax.ppermute(
            val.astype(bf16), "tp", [(k, k - 1) for k in range(n - 1 - s, n)]
        )
    return chunk(me) + up.astype(f32) + down.astype(f32)


def rotary_tables():
    half_rot = ROT // 2
    positions = jnp.arange(SEQ, dtype=jnp.int32).astype(f32)
    frequency = 10000.0 ** (-2.0 * jnp.arange(half_rot, dtype=f32) / ROT)
    angles = positions[:, None] * frequency[None, :]
    cos, sin = jnp.cos(angles), jnp.sin(angles)
    rest = HD - ROT
    zero = jnp.zeros((SEQ, rest), f32)
    keep = jnp.concatenate([cos, cos, jnp.ones((SEQ, rest), f32)], -1)
    ahead = jnp.concatenate([-sin, jnp.zeros_like(sin), zero], -1)
    behind = jnp.concatenate([jnp.zeros_like(sin), sin, zero], -1)
    one = jnp.stack([keep, ahead, behind])
    return jnp.concatenate([one, one], -1)


def turned(v, tab_ref, sign):
    half_rot = ROT // 2
    return (
        v * tab_ref[0]
        + sign
        * (
            pltpu.roll(v, PAIR - half_rot, 1) * tab_ref[1]
            + pltpu.roll(v, half_rot, 1) * tab_ref[2]
        )
    )


def dot_nt(a, b):
    return lax.dot_general(a, b, (((1,), (1,)), ((), ())), preferred_element_type=f32)


def dot_nn(a, b):
    return lax.dot_general(a, b, (((1,), (0,)), ((), ())), preferred_element_type=f32)


def dot_tn(a, b):
    return lax.dot_general(a, b, (((0,), (0,)), ((), ())), preferred_element_type=f32)


def own_lanes(a, head):
    lane = lax.broadcasted_iota(jnp.int32, a.shape, 1)
    mine = (lane < HD) if head == 0 else (lane >= HD)
    return jnp.where(mine, a, jnp.zeros_like(a))


def diagonal(span):
    row = lax.broadcasted_iota(jnp.int32, (span, span), 0)
    col = lax.broadcasted_iota(jnp.int32, (span, span), 1)
    return col <= row


def attend_kernel(joined_ref, tab_ref, qkv_ref, attn_ref, lse_ref):
    scale = HD ** (-0.5)
    qkv_ref[0] = (turned(joined_ref[0], tab_ref, 1.0) * scale).astype(bf16)
    qkv_ref[1] = turned(joined_ref[1], tab_ref, 1.0).astype(bf16)
    qkv_ref[2] = joined_ref[2].astype(bf16)
    allowed = diagonal(SPAN)
    lane = lax.broadcasted_iota(jnp.int32, (SPAN, PAIR), 1)
    for i in range(SEQ // SPAN):
        lo, hi = i * SPAN, (i + 1) * SPAN
        q_block = qkv_ref[0, lo:hi, :]
        outs, sums = [], []
        for head in range(2):
            qh = own_lanes(q_block, head)
            near = jnp.where(allowed, dot_nt(qh, qkv_ref[1, lo:hi, :]), -1e30)
            top = jnp.max(near, -1, keepdims=True)
            if i:
                far = dot_nt(qh, qkv_ref[1, 0:lo, :])
                top = jnp.maximum(top, jnp.max(far, -1, keepdims=True))
            near = jnp.exp(near - top)
            total = jnp.sum(near, -1, keepdims=True)
            if i:
                far = jnp.exp(far - top)
                total = total + jnp.sum(far, -1, keepdims=True)
            inverse = 1.0 / total
            out = dot_nn((near * inverse).astype(bf16), qkv_ref[2, lo:hi, :])
            if i:
                out = out + dot_nn((far * inverse).astype(bf16), qkv_ref[2, 0:lo, :])
            outs.append(out)
            sums.append(jnp.broadcast_to(top + jnp.log(total), (SPAN, PAIR)))
        attn_ref[lo:hi, :] = jnp.where(lane < HD, outs[0], outs[1]).astype(bf16)
        lse_ref[lo:hi, :] = jnp.where(lane < HD, sums[0], sums[1])


def attend(joined, tables):
    width = joined.shape[2]
    pairs = width // PAIR
    flops = pairs * 2 * SEQ * SEQ * PAIR * 4
    return pl.pallas_call(
        attend_kernel,
        grid=(pairs,),
        in_specs=[
            pl.BlockSpec((3, SEQ, PAIR), lambda p: (0, 0, p)),
            pl.BlockSpec((3, SEQ, PAIR), lambda p: (0, 0, 0)),
        ],
        out_specs=[
            pl.BlockSpec((3, SEQ, PAIR), lambda p: (0, 0, p)),
            pl.BlockSpec((SEQ, PAIR), lambda p: (0, p)),
            pl.BlockSpec((SEQ, PAIR), lambda p: (0, p)),
        ],
        out_shape=[
            jax.ShapeDtypeStruct((3, SEQ, width), bf16),
            jax.ShapeDtypeStruct((SEQ, width), bf16),
            jax.ShapeDtypeStruct((SEQ, width), f32),
        ],
        compiler_params=pltpu.CompilerParams(vmem_limit_bytes=40 << 20),
        cost_estimate=pl.CostEstimate(
            flops=flops, transcendentals=pairs * SEQ * SEQ, bytes_accessed=24 * SEQ * width
        ),
        name="attend",
    )(joined, tables)


def attend_back_kernel(qkv_ref, grad_ref, lse_ref, tab_ref, out_ref, bias_ref, gk_ref, gv_ref):
    scale = HD ** (-0.5)
    allowed = diagonal(SPAN)
    gk_ref[...] = jnp.zeros_like(gk_ref)
    gv_ref[...] = jnp.zeros_like(gv_ref)
    queries = []
    for i in range(SEQ // SPAN):
        lo, hi = i * SPAN, (i + 1) * SPAN
        gq = jnp.zeros((SPAN, PAIR), f32)
        for head in range(2):
            qh = own_lanes(qkv_ref[0, lo:hi, :], head)
            gh = own_lanes(grad_ref[lo:hi, :], head)
            lse = lse_ref[lo:hi, head * HD : head * HD + 1]
            spans = [(lo, hi, True)] + ([(0, lo, False)] if i else [])
            probs, gprobs = [], []
            inner = jnp.zeros((SPAN, 1), f32)
            for a, b, masked in spans:
                p = jnp.exp(dot_nt(qh, qkv_ref[1, a:b, :]) - lse)
                if masked:
                    p = jnp.where(allowed, p, 0.0)
                g = dot_nt(gh, qkv_ref[2, a:b, :])
                inner = inner + jnp.sum(p * g, -1, keepdims=True)
                probs.append(p)
                gprobs.append(g)
            for (a, b, masked), p, g in zip(spans, probs, gprobs):
                gs = (p * (g - inner)).astype(bf16)
                gk_ref[a:b, :] += dot_tn(gs, qh)
                gv_ref[a:b, :] += dot_tn(p.astype(bf16), gh)
                gq = gq + dot_nn(gs, own_lanes(qkv_ref[1, a:b, :], head))
        queries.append(gq)
    gq = jnp.concatenate(queries, 0) * scale
    for j, g in enumerate((gq, gk_ref[...], gv_ref[...])):
        if j < 2:
            g = turned(g, tab_ref, -1.0)
        g = g.astype(bf16)
        out_ref[j] = g
        bias_ref[j] = jnp.sum(g.astype(f32).reshape(SEQ // 8, 8, PAIR), 0)


def attend_back(qkv, grad, lse, tables):
    width = grad.shape[1]
    pairs = width // PAIR
    flops = pairs * 2 * SEQ * SEQ * PAIR * 10
    return pl.pallas_call(
        attend_back_kernel,
        grid=(pairs,),
        in_specs=[
            pl.BlockSpec((3, SEQ, PAIR), lambda p: (0, 0, p)),
            pl.BlockSpec((SEQ, PAIR), lambda p: (0, p)),
            pl.BlockSpec((SEQ, PAIR), lambda p: (0, p)),
            pl.BlockSpec((3, SEQ, PAIR), lambda p: (0, 0, 0)),
        ],
        out_specs=[
            pl.BlockSpec((3, SEQ, PAIR), lambda p: (0, 0, p)),
            pl.BlockSpec((3, 8, PAIR), lambda p: (0, 0, p)),
        ],
        out_shape=[
            jax.ShapeDtypeStruct((3, SEQ, width), bf16),
            jax.ShapeDtypeStruct((3, 8, width), f32),
        ],
        scratch_shapes=[pltpu.VMEM((SEQ, PAIR), f32), pltpu.VMEM((SEQ, PAIR), f32)],
        compiler_params=pltpu.CompilerParams(vmem_limit_bytes=40 << 20),
        cost_estimate=pl.CostEstimate(
            flops=flops, transcendentals=pairs * SEQ * SEQ, bytes_accessed=20 * SEQ * width
        ),
        name="attend_back",
    )(qkv, grad, lse, tables)


def per_device(
    chips,
    line,
    layer_input,
    teacher,
    out_grad,
    lengths,
    norm_gain,
    norm_bias,
    qkv_weight,
    qkv_bias,
    out_weight,
    gate_up_weight,
    down_weight,
):
    core = lax.axis_index("core")
    place = lax.axis_index("tp")
    rows = layer_input.shape[0]
    feats = D // (2 * chips)
    width = qkv_weight.shape[2]
    dot = functools.partial(jnp.einsum, preferred_element_type=f32)

    def halves(a):
        b = a.reshape(a.shape[:-1] + (chips, 2, feats))
        first, second = b[..., 0, :], b[..., 1, :]
        flat = a.shape[:-1] + (chips * feats,)
        own = jnp.where(core == 0, first, second).reshape(flat)
        other = jnp.where(core == 0, second, first).reshape(flat)
        return own, other

    def whole(own, other):
        flat = own.shape[:-1] + (chips, feats)
        own, other = own.reshape(flat), other.reshape(flat)
        first = jnp.where(core == 0, own, other)
        second = jnp.where(core == 0, other, own)
        return jnp.stack([first, second], -2).reshape(own.shape[:-2] + (D,))

    def weight_halves(w, axis):
        own = lax.all_gather(w, "chip", axis=axis, tiled=True)
        return own, swap_core(own)

    wq = weight_halves(qkv_weight, 1)
    wgu = weight_halves(gate_up_weight, 1)
    wo = weight_halves(out_weight, 1)
    wd = weight_halves(down_weight, 1)

    small = jnp.stack([norm_gain, norm_bias])
    small = gather_axis(small, "tp", line)
    small = small.transpose(1, 0, 2).reshape(2 * feats)
    small = jnp.concatenate([small, qkv_bias.astype(f32).reshape(-1)])
    small = gather_axis(gather_axis(small, "core", 2), "chip", chips)
    small = small.reshape(2 * chips, -1)
    gain = small[:, :feats].reshape(D)
    shift = small[:, feats : 2 * feats].reshape(D)
    bias = small[:, 2 * feats :].reshape(2 * chips, 3, -1)
    bias = bias.transpose(1, 0, 2).reshape(3, width)
    gain_h, shift_h = halves(gain), halves(shift)

    x_own = halves(layer_input)
    x_all = tuple(line_gather(h, line) for h in x_own)

    def moments(xs):
        xs = [h.astype(f32) for h in xs]
        mean = (jnp.sum(xs[0], -1, keepdims=True) + jnp.sum(xs[1], -1, keepdims=True)) / D
        centered = [h - mean for h in xs]
        var = sum(jnp.sum(h * h, -1, keepdims=True) for h in centered) / D
        inv = lax.rsqrt(var + epsilon)
        return mean, inv

    mean, inv_std = moments(x_all)
    unit = [(h.astype(f32) - mean) * inv_std for h in x_all]
    normed = [(u * g + s).astype(bf16) for u, g, s in zip(unit, gain_h, shift_h)]

    joined = dot("sd,jde->jse", normed[0], wq[0]) + dot("sd,jde->jse", normed[1], wq[1])
    joined = joined + bias[:, None, :]
    tables = rotary_tables()
    qkv, attn, lse = attend(joined, tables)
    gate_up = dot("sd,jdf->jsf", normed[0], wgu[0]) + dot("sd,jdf->jsf", normed[1], wgu[1])
    sigmoid = jax.nn.sigmoid(gate_up[0])
    hidden = (gate_up[0] * sigmoid * gate_up[1]).astype(bf16)

    ids = place * rows + jnp.arange(rows, dtype=jnp.int32)
    valid = (ids < lengths[0]).astype(f32)[:, None]
    teach, cot = halves(teacher), halves(out_grad)
    results, seeds, seed_all = [], [], []
    loss_part = jnp.zeros((), f32)
    for h in range(2):
        branch = dot("sa,ad->sd", attn, wo[h]) + dot("sf,fd->sd", hidden, wd[h])
        result = x_own[h].astype(f32) + valid * line_scatter(branch, line)
        mismatch = result - teach[h].astype(f32)
        loss_part = loss_part + jnp.sum(valid * mismatch * mismatch)
        seed = valid * (cot[h].astype(f32) + mismatch)
        results.append(result.astype(bf16))
        seeds.append(seed)
        seed_all.append(line_gather(seed.astype(bf16), line))
    count_part = jnp.sum(valid)

    def weight_grad(make, axis):
        own, other = make(0), make(1)
        both = (own + swap_core(other.astype(bf16)).astype(f32)).astype(bf16)
        return lax.psum_scatter(both, "chip", scatter_dimension=axis, tiled=True).astype(f32)

    down_grad = weight_grad(lambda h: dot("sf,sd->fd", hidden, seed_all[h]), 1)
    out_w_grad = weight_grad(lambda h: dot("sa,sd->ad", attn, seed_all[h]), 1)
    grad_attn = (
        dot("sd,ad->sa", seed_all[0], wo[0]) + dot("sd,ad->sa", seed_all[1], wo[1])
    ).astype(bf16)
    grad_qkv, grad_bias = attend_back(qkv, grad_attn, lse, tables)
    grad_hidden = dot("sd,fd->sf", seed_all[0], wd[0]) + dot("sd,fd->sf", seed_all[1], wd[1])
    grad_gate = grad_hidden * gate_up[1] * sigmoid * (1.0 + gate_up[0] * (1.0 - sigmoid))
    grad_up = grad_hidden * gate_up[0] * sigmoid
    grad_gu = jnp.stack([grad_gate, grad_up]).astype(bf16)
    gu_grad = weight_grad(lambda h: dot("sd,jsf->jdf", normed[h], grad_gu), 1)
    qkv_grad = weight_grad(lambda h: dot("sd,jse->jde", normed[h], grad_qkv), 1)

    grad_normed, gain_parts, shift_parts = [], [], []
    for h in range(2):
        part = dot("jse,jde->sd", grad_qkv, wq[h]) + dot("jsf,jdf->sd", grad_gu, wgu[h])
        gain_parts.append(jnp.sum(part * unit[h], 0))
        shift_parts.append(jnp.sum(part, 0))
        grad_normed.append(line_scatter(part, line))

    mean, inv_std = moments(x_own)
    unit = [(h.astype(f32) - mean) * inv_std for h in x_own]
    grad_unit = [g * w for g, w in zip(grad_normed, gain_h)]
    m1 = sum(jnp.sum(g, -1, keepdims=True) for g in grad_unit) / D
    m2 = sum(jnp.sum(g * u, -1, keepdims=True) for g, u in zip(grad_unit, unit)) / D
    input_grad = [
        (s + inv_std * (g - m1 - u * m2)).astype(bf16)
        for s, g, u in zip(seeds, grad_unit, unit)
    ]

    scalars = jnp.stack([loss_part, count_part])
    vectors = jnp.stack([whole(*gain_parts), whole(*shift_parts)])
    vectors = vectors.reshape(2, chips, 2, line, -1).transpose(1, 2, 3, 0, 4)
    vectors = vectors.reshape(chips, 2, line, -1)
    vectors = jnp.concatenate(
        [vectors, jnp.broadcast_to(scalars, (chips, 2, line, 2))], -1
    ).reshape(chips, 2, -1)
    heads = jnp.sum(grad_bias, 1).reshape(3, chips, 2, -1).transpose(1, 2, 0, 3)
    heads = heads.reshape(chips, 2, -1)
    sums = jnp.concatenate([vectors, heads], -1)
    sums = scatter_axis(scatter_axis(sums, "chip", chips), "core", 2)
    qkv_b_grad = sums[vectors.shape[-1] :].reshape(3, -1)
    sums = scatter_axis(sums[: vectors.shape[-1]].reshape(line, -1), "tp", line)
    n = norm_gain.shape[0]
    gain_grad, bias_grad = sums[:n], sums[n : 2 * n]
    loss_value = sums[2 * n] / (sums[2 * n + 1] * D)
    return (
        whole(*results),
        loss_value,
        whole(*input_grad),
        gain_grad,
        bias_grad,
        qkv_grad,
        qkv_b_grad,
        out_w_grad,
        gu_grad,
        down_grad,
    )


def solution(mesh):
    chips, line = mesh.shape["fsdp"] // 2, mesh.shape["tp"]
    fine = Mesh(mesh.devices.reshape(chips, 2, line), ("chip", "core", "tp"))
    fsdp = ("chip", "core")
    tokens = P(fsdp + ("tp",), None)
    vector = P(fsdp + ("tp",))
    return jax.shard_map(
        functools.partial(per_device, chips, line),
        mesh=fine,
        in_specs=(
            tokens,
            tokens,
            tokens,
            P(fsdp),
            vector,
            vector,
            P(None, fsdp, "tp"),
            P(None, ("tp",) + fsdp),
            P("tp", fsdp),
            P(None, fsdp, "tp"),
            P("tp", fsdp),
        ),
        out_specs=(
            tokens,
            P(),
            tokens,
            vector,
            vector,
            P(None, fsdp, "tp"),
            P(None, ("tp",) + fsdp),
            P("tp", fsdp),
            P(None, fsdp, "tp"),
            P("tp", fsdp),
        ),
        check_vma=False,
    )
```

time: 1320 us -> 714 us (0.54)
  waiting for transfers between devices: 826 us -> 213 us
  starting transfers between devices: 0.53 us -> 116 us
  blocking collectives: 93.6 us -> 0 us
  matrix products: 231 us -> 166 us
  Pallas kernels: 0 us -> 45.4 us
    reduce_scatter x6 -> x4, waiting for transfers between devices: 565 us -> 0.01 us  [weight_grad(): lax.psum_scatter(both, 'chip', scatter_dimension=axis, tiled=True)]
    all_gather x6 -> x4, waiting for transfers between devices: 259 us -> 58.8 us  [weight_halves(): own = lax.all_gather(w, 'chip', axis=axis, tiled=True)]
    ppermute x0 -> x66, waiting for transfers between devices: none -> 152 us  [the longest x12 71.1 us: line_gather(): cur = lax.ppermute(cur, 'tp', [(k, k - 1) for k in range(1, n - s)])]
    ppermute x0 -> x66, starting transfers between devices: none -> 116 us  [the longest x12 44.5 us: line_scatter(): lax.ppermute(val.astype(bf16), 'tp', [(k, k + 1) for k in range(s + 1)])]
    dot_general x26 -> x24, matrix products: 231 us -> 166 us  [the longest x2 26.8 us: per_device(): gu_grad = weight_grad(lambda h: dot('sd,jsf->jdf', normed[h], grad_gu), 1)]
    pallas_call x0 -> x2, Pallas kernels: none -> 45.4 us  [the longest x1 26.3 us: attend_back(): pl.pallas_call(attend_back_kernel, grid=(pairs,), in_specs=[pl.BlockSpec(...]
    unnamed x1 -> x0, blocking collectives: 42 us -> none
    psum x1 -> x0, blocking collectives: 41.6 us -> none  [per_device(): loss_total, valid_total = lax.psum((loss_part, count_part), ('fsdp', 'tp'))]
  transfers between devices with their start and end apart: 13 -> 74, of which waited for: 12 -> 28; matrix products, arithmetic and copies ran while one was open for 15% -> 41% of each run, Pallas kernels for 0% -> 6%
where the time goes in v1:
time: 714 us; the launch traced here: 706 us
  waiting for transfers between devices  213 us (30%)
  matrix products  166 us (23%)
  starting transfers between devices  116 us (16%)
  local copies, waits for them, and re-layouts  87.2 us (12%)
  other arithmetic  57.7 us (8%)
  Pallas kernels  45.4 us (6%)
  between operations  20.5 us (3%)
    ppermute x12, waiting for transfers between devices, line_gather(): cur = lax.ppermute(cur, 'tp', [(k, k - 1) for k in range(1, n - s)])  71.1 us
    all_gather x4, waiting for transfers between devices, weight_halves(): own = lax.all_gather(w, 'chip', axis=axis, tiled=True)  58.8 us
    ppermute x12, starting transfers between devices, line_scatter(): lax.ppermute(val.astype(bf16), 'tp', [(k, k + 1) for k in range(s + 1)])  44.5 us
    ppermute x12, waiting for transfers between devices, line_scatter(): lax.ppermute(val.astype(bf16), 'tp', [(k, k + 1) for k in range(s + 1)])  41.4 us
    unnamed x124, local copies, waits for them, and re-layouts  28.1 us
    ppermute x12, starting transfers between devices, line_gather(): cur = lax.ppermute(cur, 'tp', [(k, k + 1) for k in range(s, n - 1)])  27.7 us
    dot_general x2, matrix products, per_device(): gu_grad = weight_grad(lambda h: dot('sd,jsf->jdf', normed[h], grad_gu), 1)  26.8 us
    pallas_call x1, Pallas kernels, attend_back(): pl.pallas_call(attend_back_kernel, grid=(pairs,), in_specs=[pl.BlockSpec(...  26.3 us
  transfers between devices with their start and end apart: 74, of which 28 were waited for; matrix products, arithmetic and copies ran while one was open for 41% of the time, Pallas kernels for 6%

profile of v1, /device:TPU:0, one launch (start us, length us, event | category | flops | bytes accessed | tf_op | source)
XLA Modules:
  0.0 706.0 jit_solution(9816168905542488777)
XLA Ops:
  14.5 5.7 collective-permute-start.6
  21.5 5.4 collective-permute-start
  33.0 13.9 %collective-permute-done.12 = f32[1,2,64]{2,1,0:T(2,128)S(1)} collective-permute-done((f32[1,2,64]{2,1,0:T(2,128)S(1)}, f32[1,2,64]{2,1,0:T(2,128)S(1)}, u32[]{:S(2)}, u32[]{:S(2)}) %collective-permute-start.12) | collective-permute-done | bytes 544 | tf_op jit(solution)/shard_map/ppermute | solution.py:31
  68.6 9.3 %collective-permute-done.10 = bf16[256,1024]{0,1:T(8,128)(2,1)} collective-permute-done((bf16[256,1024]{0,1:T(8,128)(2,1)}, bf16[256,1024]{0,1:T(8,128)(2,1)}, u32[]{:S(2)}, u32[]{:S(2)}) %collective-permute-start.10) | collective-permute-done | bytes 524320 | tf_op jit(solution)/shard_map/ppermute | solution.py:65
  79.2 9.9 %collective-permute-done.4 = bf16[256,1024]{0,1:T(8,128)(2,1)} collective-permute-done((bf16[256,1024]{0,1:T(8,128)(2,1)}, bf16[256,1024]{0,1:T(8,128)(2,1)}, u32[]{:S(2)}, u32[]{:S(2)}) %collective-permute-start.4) | collective-permute-done | bytes 524320 | tf_op jit(solution)/shard_map/ppermute | solution.py:65
  100.2 10.6 %collective-permute-done.5 = bf16[256,1024]{0,1:T(8,128)(2,1)} collective-permute-done((bf16[256,1024]{0,1:T(8,128)(2,1)}, bf16[256,1024]{0,1:T(8,128)(2,1)}, u32[]{:S(2)}, u32[]{:S(2)}) %collective-permute-start.5) | collective-permute-done | bytes 524320 | tf_op jit(solution)/shard_map/ppermute | solution.py:65
  120.7 3.7 all-gather.9.cloned.1.call-done
  137.8 3.3 fusion.16
  141.1 11.7 %all-gather.7.cloned.1.call-done = bf16[512,1024]{1,0:T(8,128)(2,1)} async-done(((bf16[512,256]{1,0:T(8,128)(2,1)}), bf16[512,1024]{1,0:T(8,128)(2,1)}) %all-gather.7.cloned.1.call-update) | async-done | bytes 1048592 | tf_op jit(solution)/shard_map/all_gather | solution.py:318
  152.8 43.4 %all-gather.11.cloned.1.call-done = bf16[1408,1024]{1,0:T(8,128)(2,1)} async-done(((bf16[1408,256]{1,0:T(8,128)(2,1)}), bf16[1408,1024]{1,0:T(8,128)(2,1)}) %all-gather.11.cloned.1.call-update) | async-done | bytes 2883600 | tf_op jit(solution)/shard_map/all_gather | solution.py:318
  196.2 6.5 fusion.68
  202.7 5.6 add_bitcast_fusion.1.joined_ref
  208.3 19.1 %attend.1 = (bf16[3,1024,512]{2,1,0:T(8,128)(2,1)S(1)}, bf16[1024,512]{1,0:T(8,128)(2,1)S(1)}, f32[1024,512]{1,0:T(8,128)S(1)}) custom-call(f32[3,1024,512]{2,1,0:T(8,128)S(1)} %add_bitcast_fusion.1.joined_ref, f32[3,1024,128]{2,1,0:T(8,128)S(1)} %maximum_maximum_fusion.tab_ref), custom_call_target="tpu_custom_call" | custom-call | flops 4294967296 | bytes 12582912 | tf_op jit(solution)/shard_map/attend/pallas_call | solution.py:186
  227.5 11.3 %fusion.59 = f32[1024,2,1408]{2,0,1:T(8,128)} fusion(bf16[2,1024,1408]{2,1,0:T(8,128)(2,1)S(1)} %bitcast.235, bf16[1024,1024]{0,1:T(8,128)(2,1)} %constant_dynamic-update-slice_fusion.21, f32[1024]{0:T(1024)S(1)} %bitcast.223, f32[1024]{0:T(1024)S(1)} %bitcast.213, f32[1024]{0:T(1024)S(1)} %add_rsqrt_fusion, f32[1024]{0:T(1024)S(1)} %add_multiply_fusion.2), kind=kOutput, calls=%fused_computation.223 | convolution fusion | flops 5911871488 | bytes 19415040 | tf_op jit(solution)/shard_map/sd,jdf->jsf/dot_general | solution.py:357
  238.8 12.0 %add_bitcast_fusion = f32[2,1024,1408]{2,1,0:T(8,128)S(1)} fusion(f32[1024,2,1408]{2,0,1:T(8,128)} %fusion.59, bf16[2,1024,1408]{2,1,0:T(8,128)(2,1)} %collective-permute-done.18, bf16[1024,1024]{0,1:T(8,128)(2,1)} %constant_dynamic-update-slice_fusion.14, f32[1024]{0:T(1024)S(1)} %bitcast.227, f32[1024]{0:T(1024)S(1)} %bitcast.218, ...), kind=kOutput, calls=%fused_computation.2 | convolution fusion | flops 5914755072 | bytes 30949376 | tf_op jit(solution)/shard_map/sd,jdf->jsf/dot_general | solution.py:357
  252.8 7.6 %fusion.80 = f32[1024,1024]{0,1:T(8,128)S(1)} fusion(bf16[1024,1408]{1,0:T(8,128)(2,1)S(1)} %multiply_convert_fusion.2, bf16[1408,1024]{1,0:T(8,128)(2,1)} %collective-permute-done.26), kind=kOutput, calls=%fused_computation.234 | convolution fusion | flops 2952790016 | bytes 9961472 | tf_op jit(solution)/shard_map/sf,fd->sd/dot_general | solution.py:367
  260.4 4.7 convolution_add_fusion.1
  267.7 4.3 collective-permute-start.27
  272.1 3.6 fusion.79
  275.6 3.3 convolution_add_fusion.2
  287.4 3.4 collective-permute-start.28
  292.4 3.1 collective-permute-done.19
  297.7 5.2 collective-permute-start.20
  311.9 5.7 collective-permute-done.20
  324.1 5.9 collective-permute-start.29
  330.0 4.6 collective-permute-start.21
  343.9 3.5 copy.140
  347.4 3.5 copy.141
  350.8 3.5 copy.142
  354.3 3.5 copy.143
  362.8 3.6 fusion.43
  367.0 3.3 collective-permute-start.39
  371.7 4.6 collective-permute-start.33
  377.5 5.1 collective-permute-done.39
  383.4 3.7 collective-permute-done.42
  388.4 3.1 collective-permute-done.33
  392.2 6.2 collective-permute-done.36
  400.3 9.2 %collective-permute-done.43 = bf16[256,1024]{0,1:T(8,128)(2,1)S(1)} collective-permute-done((bf16[256,1024]{0,1:T(8,128)(2,1)S(1)}, bf16[256,1024]{0,1:T(8,128)(2,1)S(1)}, u32[]{:S(2)}, u32[]{:S(2)}) %collective-permute-start.43) | collective-permute-done | bytes 524320 | tf_op jit(solution)/shard_map/ppermute | solution.py:65
  411.6 9.2 %collective-permute-done.37 = bf16[256,1024]{0,1:T(8,128)(2,1)S(1)} collective-permute-done((bf16[256,1024]{0,1:T(8,128)(2,1)S(1)}, bf16[256,1024]{0,1:T(8,128)(2,1)S(1)}, u32[]{:S(2)}, u32[]{:S(2)}) %collective-permute-start.37) | collective-permute-done | bytes 524320 | tf_op jit(solution)/shard_map/ppermute | solution.py:65
  422.5 9.6 %collective-permute-done.44 = bf16[256,1024]{0,1:T(8,128)(2,1)S(1)} collective-permute-done((bf16[256,1024]{0,1:T(8,128)(2,1)S(1)}, bf16[256,1024]{0,1:T(8,128)(2,1)S(1)}, u32[]{:S(2)}, u32[]{:S(2)}) %collective-permute-start.44) | collective-permute-done | bytes 524320 | tf_op jit(solution)/shard_map/ppermute | solution.py:65
  432.5 4.6 convolution_convert_fusion
  446.4 3.3 fusion.81
  452.1 6.0 add_convert_fusion
  462.9 26.3 %attend_back.1 = (bf16[3,1024,512]{2,1,0:T(8,128)(2,1)S(1)}, f32[3,8,512]{2,1,0:T(8,128)S(1)}) custom-call(bf16[3,1024,512]{2,1,0:T(8,128)(2,1)S(1)} %copy-done.2, bf16[1024,512]{1,0:T(8,128)(2,1)S(1)} %copy-done, f32[1024,512]{1,0:T(8,128)S(1)} %copy-done.4, f32[3,1024,128]{2,1,0:T(8,128)S(1)} %maximum_maximum_fusion.tab_ref), custom_call_target="tpu_custom_call" | custom-call | flops 10737418240 | bytes 10485760 | tf_op jit(solution)/shard_map/attend_back/pallas_call | solution.py:254
  489.2 7.4 %convert_bitcast_fusion.1 = bf16[3,1024,512]{1,2,0:T(8,128)(2,1)S(1)} fusion(bf16[3,1024,512]{2,1,0:T(8,128)(2,1)S(1)} %get-tuple-element.18, bf16[1024,1024]{0,1:T(8,128)(2,1)} %constant_dynamic-update-slice_fusion.14, f32[1024]{0:T(1024)S(1)} %bitcast.228, f32[1024]{0:T(1024)S(1)} %bitcast.219, f32[1024]{0:T(1024)S(1)} %add_rsqrt_fusion, ...), kind=kOutput, calls=%fused_computation.39 | convolution fusion | flops 3229089792 | bytes 8404992 | tf_op jit(solution)/shard_map/sd,jse->jde/dot_general | solution.py:393
  496.7 7.4 %fusion.83 = f32[1024,1408]{1,0:T(8,128)} fusion(bf16[1024,1024]{0,1:T(8,128)(2,1)S(1)} %copy-done.37, bf16[1408,1024]{1,0:T(8,128)(2,1)} %collective-permute-done.26), kind=kOutput, calls=%fused_computation.237 | convolution fusion | flops 2952790016 | bytes 10747904 | tf_op jit(solution)/shard_map/sd,fd->sf/dot_general | solution.py:388
  504.2 11.3 %fusion.19 = (bf16[1,1024,1408]{2,1,0:T(8,128)(2,1)}, bf16[1,1024,1408]{2,1,0:T(8,128)(2,1)}) fusion(f32[2,1024,1408]{2,1,0:T(8,128)} %copy-done.13, f32[1024,1408]{1,0:T(8,128)} %fusion.83, bf16[1024,1024]{0,1:T(8,128)(2,1)S(1)} %copy-done.35, bf16[1408,1024]{1,0:T(8,128)(2,1)S(1)} %copy-done.51), kind=kOutput, calls=%fused_computation.41 | convolution fusion | flops 2972975104 | bytes 28049408 | tf_op jit(solution)/shard_map/sd,fd->sf/dot_general | solution.py:388
  515.5 12.0 %convert_bitcast_fusion = bf16[2,1024,1408]{1,2,0:T(8,128)(2,1)} fusion(bf16[1,1024,1408]{2,1,0:T(8,128)(2,1)} %get-tuple-element.90, bf16[1,1024,1408]{2,1,0:T(8,128)(2,1)} %get-tuple-element.89, bf16[1024,1024]{0,1:T(8,128)(2,1)} %constant_dynamic-update-slice_fusion.14, f32[1024]{0:T(1024)S(1)} %bitcast.229, f32[1024]{0:T(1024)S(1)} %bitcast.220, ...), kind=kOutput, calls=%fused_computation.10 | convolution fusion | flops 5917638656 | bytes 13647872 | tf_op jit(solution)/shard_map/sd,jsf->jdf/dot_general | solution.py:392
  527.9 7.3 %fusion.1 = bf16[3,1024,512]{1,2,0:T(8,128)(2,1)} fusion(bf16[3,1024,512]{1,2,0:T(8,128)(2,1)S(1)} %collective-permute-done.62, bf16[3,1024,512]{2,1,0:T(8,128)(2,1)S(1)} %get-tuple-element.18, bf16[1024,1024]{0,1:T(8,128)(2,1)} %constant_dynamic-update-slice_fusion.21, f32[1024]{0:T(1024)S(1)} %bitcast.224, f32[1024]{0:T(1024)S(1)} %bitcast.214, ...), kind=kOutput, calls=%fused_computation.4 | convolution fusion | flops 3232235520 | bytes 11550720 | tf_op jit(solution)/shard_map/sd,jse->jde/dot_general | solution.py:393
  538.7 14.8 %fusion = bf16[2,1024,1408]{1,2,0:T(8,128)(2,1)} fusion(bf16[2,1024,1408]{1,2,0:T(8,128)(2,1)} %collective-permute-done.64, bf16[1,1024,1408]{2,1,0:T(8,128)(2,1)} %get-tuple-element.90, bf16[1,1024,1408]{2,1,0:T(8,128)(2,1)} %get-tuple-element.89, bf16[1024,1024]{0,1:T(8,128)(2,1)} %constant_dynamic-update-slice_fusion.21, f32[1024]{0:T(1024)S(1)} %bitcast.225, ...), kind=kOutput, calls=%fused_computation.1 | convolution fusion | flops 5923405824 | bytes 19415040 | tf_op jit(solution)/shard_map/sd,jsf->jdf/dot_general | solution.py:392
  555.4 5.5 fusion.84
  560.9 3.4 fusion.82
  564.4 9.8 %bitcast_add_fusion.2 = f32[1024,1024]{0,1:T(8,128)S(1)} fusion(f32[1024,1024,1]{0,1,2:T(8,128)S(1)} %fusion.84, bf16[2,1024,1408]{2,1,0:T(8,128)(2,1)} %collective-permute-done.18, bf16[1,1024,1408]{2,1,0:T(8,128)(2,1)} %get-tuple-element.90, bf16[1,1024,1408]{2,1,0:T(8,128)(2,1)S(1)} %copy-done.52), kind=kOutput, calls=%fused_computation.36 | convolution fusion | flops 5909512192 | bytes 19922944 | tf_op jit(solution)/shard_map/jsf,jdf->sd/dot_general | solution.py:397
  574.2 12.4 %fusion.12 = (f32[1024]{0:T(1024)S(1)}, f32[1024]{0:T(1024)S(1)}, f32[1024]{0:T(1024)S(1)}, f32[1024]{0:T(1024)S(1)}, f32[1024,1024]{0,1:T(8,128)}) fusion(bf16[1024,1024]{0,1:T(8,128)(2,1)} %constant_dynamic-update-slice_fusion.21, f32[1024]{0:T(1024)S(1)} %add_rsqrt_fusion, f32[1024]{0:T(1024)S(1)} %add_multiply_fusion.2, ...), kind=kOutput, calls=%fused_computation.30 | convolution fusion | flops 5922091008 | bytes 28336128 | tf_op jit(solution)/shard_map/jsf,jdf->sd/dot_general | solution.py:397
  599.7 6.1 collective-permute-done.50
  607.3 4.3 collective-permute-start.51
  611.5 5.4 collective-permute-done.56
  618.4 5.1 collective-permute-start.57
  623.8 4.5 collective-permute-done.51
  630.7 7.7 %collective-permute-done.57 = bf16[256,1024]{0,1:T(8,128)(2,1)} collective-permute-done((bf16[256,1024]{0,1:T(8,128)(2,1)S(1)}, bf16[256,1024]{0,1:T(8,128)(2,1)}, u32[]{:S(2)}, u32[]{:S(2)}) %collective-permute-start.57) | collective-permute-done | bytes 524320 | tf_op jit(solution)/shard_map/ppermute | solution.py:88
  647.5 4.6 collective-permute-start.58
  660.1 8.9 %collective-permute-done.58 = bf16[256,1024]{0,1:T(8,128)(2,1)S(1)} collective-permute-done((bf16[256,1024]{0,1:T(8,128)(2,1)S(1)}, bf16[256,1024]{0,1:T(8,128)(2,1)S(1)}, u32[]{:S(2)}, u32[]{:S(2)}) %collective-permute-start.58) | collective-permute-done | bytes 524320 | tf_op jit(solution)/shard_map/ppermute | solution.py:88
  670.2 8.4 %collective-permute-done.61 = bf16[256,1024]{0,1:T(8,128)(2,1)S(1)} collective-permute-done((bf16[256,1024]{0,1:T(8,128)(2,1)S(1)}, bf16[256,1024]{0,1:T(8,128)(2,1)S(1)}, u32[]{:S(2)}, u32[]{:S(2)}) %collective-permute-start.61) | collective-permute-done | bytes 524320 | tf_op jit(solution)/shard_map/ppermute | solution.py:92
  694.8 3.0 copy.117
  (392 shorter events, 201.7 us)
Async XLA Ops:
  7.2 83.9 %all-gather.5.cloned.1.call-start = ((), (), s32[]{:S(2)}) async-start(), calls=%async_computation.4 | async-start | bytes 3932160 | tf_op jit(solution)/shard_map/all_gather | solution.py:318
  7.9 116.5 %all-gather.9.cloned.1.call-start = ((), (), s32[]{:S(2)}) async-start(), calls=%async_computation.6 | async-start | bytes 7208960 | tf_op jit(solution)/shard_map/all_gather | solution.py:318
  8.7 144.1 %all-gather.7.cloned.1.call-start = ((), (), s32[]{:S(2)}) async-start(), calls=%async_computation.5 | async-start | bytes 1310720 | tf_op jit(solution)/shard_map/all_gather | solution.py:318
  9.4 186.8 %all-gather.11.cloned.1.call-start = ((), (), s32[]{:S(2)}) async-start(), calls=%async_computation.7 | async-start | bytes 3604480 | tf_op jit(solution)/shard_map/all_gather | solution.py:318
  14.5 41.1 %collective-permute-start.6 = (bf16[256,1024]{0,1:T(8,128)(2,1)S(1)}, bf16[256,1024]{0,1:T(8,128)(2,1)}, u32[]{:S(2)}, u32[]{:S(2)}) collective-permute-start(bf16[256,1024]{0,1:T(8,128)(2,1)S(1)} %bitcast.200), channel_id=1, source_target_pairs={{0,1},{1,2},{2,3},{4,5},{5,6},{6,7},{8,9},{9,10},{10,11},{12,13},{... | collective-permute-start | bytes 1572872 | tf_op jit(solution)/shard_map/ppermute | solution.py:61
  20.3 38.4 %collective-permute-start.9 = (bf16[256,1024]{0,1:T(8,128)(2,1)S(1)}, bf16[256,1024]{0,1:T(8,128)(2,1)}, u32[]{:S(2)}, u32[]{:S(2)}) collective-permute-start(bf16[256,1024]{0,1:T(8,128)(2,1)S(1)} %bitcast.201), channel_id=1, source_target_pairs={{1,0},{2,1},{3,2},{5,4},{6,5},{7,6},{9,8},{10,9},{11,10},{13,12},{... | collective-permute-start | bytes 1572872 | tf_op jit(solution)/shard_map/ppermute | solution.py:65
  21.5 35.6 %collective-permute-start = (bf16[256,1024]{0,1:T(8,128)(2,1)S(1)}, bf16[256,1024]{0,1:T(8,128)(2,1)}, u32[]{:S(2)}, u32[]{:S(2)}) collective-permute-start(bf16[256,1024]{0,1:T(8,128)(2,1)S(1)} %bitcast.203), channel_id=1, source_target_pairs={{0,1},{1,2},{2,3},{4,5},{5,6},{6,7},{8,9},{9,10},{10,11},{12,13},{... | collective-permute-start | bytes 1572872 | tf_op jit(solution)/shard_map/ppermute | solution.py:61
  26.9 33.1 %collective-permute-start.3 = (bf16[256,1024]{0,1:T(8,128)(2,1)S(1)}, bf16[256,1024]{0,1:T(8,128)(2,1)}, u32[]{:S(2)}, u32[]{:S(2)}) collective-permute-start(bf16[256,1024]{0,1:T(8,128)(2,1)S(1)} %bitcast.204), channel_id=1, source_target_pairs={{1,0},{2,1},{3,2},{5,4},{6,5},{7,6},{9,8},{10,9},{11,10},{13,12},{... | collective-permute-start | bytes 1572872 | tf_op jit(solution)/shard_map/ppermute | solution.py:65
  28.2 18.6 %collective-permute-start.12 = (f32[1,2,64]{2,1,0:T(2,128)S(1)}, f32[1,2,64]{2,1,0:T(2,128)S(1)}, u32[]{:S(2)}, u32[]{:S(2)}) collective-permute-start(f32[1,2,64]{2,1,0:T(2,128)S(1)} %maximum_bitcast_fusion.6), channel_id=1, source_target_pairs={{0,1},{1,0},{2,3},{3,2},{4,5},{5,4},{6,7},{7,6},{8,9},{9,8},{10,11... | collective-permute-start | bytes 1544 | tf_op jit(solution)/shard_map/ppermute | solution.py:31
  31.0 657.2 %reduce-scatter.7.cloned.1.call-start = ((), (), s32[]{:S(2)}) async-start(), calls=%async_computation.9 | async-start | bytes 1310720 | tf_op jit(solution)/shard_map/reduce_scatter | solution.py:380
  58.7 19.2 %collective-permute-start.10 = (bf16[256,1024]{0,1:T(8,128)(2,1)}, bf16[256,1024]{0,1:T(8,128)(2,1)}, u32[]{:S(2)}, u32[]{:S(2)}) collective-permute-start(bf16[256,1024]{0,1:T(8,128)(2,1)} %collective-permute-done.9), channel_id=1, source_target_pairs={{1,0},{2,1},{5,4},{6,5},{9,8},{10,9},{13,12},{14,13},{17,16},{18,1... | collective-permute-start | bytes 1572872 | tf_op jit(solution)/shard_map/ppermute | solution.py:65
  60.0 29.1 %collective-permute-start.4 = (bf16[256,1024]{0,1:T(8,128)(2,1)}, bf16[256,1024]{0,1:T(8,128)(2,1)}, u32[]{:S(2)}, u32[]{:S(2)}) collective-permute-start(bf16[256,1024]{0,1:T(8,128)(2,1)} %collective-permute-done.3), channel_id=1, source_target_pairs={{1,0},{2,1},{5,4},{6,5},{9,8},{10,9},{13,12},{14,13},{17,16},{18,1... | collective-permute-start | bytes 1572872 | tf_op jit(solution)/shard_map/ppermute | solution.py:65
  65.6 25.6 %collective-permute-start.8 = (bf16[256,1024]{0,1:T(8,128)(2,1)}, bf16[256,1024]{0,1:T(8,128)(2,1)}, u32[]{:S(2)}, u32[]{:S(2)}) collective-permute-start(bf16[256,1024]{0,1:T(8,128)(2,1)} %collective-permute-done.7), channel_id=1, source_target_pairs={{2,3},{6,7},{10,11},{14,15},{18,19},{22,23},{26,27},{30,31}} | collective-permute-start | bytes 1572872 | tf_op jit(solution)/shard_map/ppermute | solution.py:61
  67.1 27.6 %collective-permute-start.2 = (bf16[256,1024]{0,1:T(8,128)(2,1)}, bf16[256,1024]{0,1:T(8,128)(2,1)}, u32[]{:S(2)}, u32[]{:S(2)}) collective-permute-start(bf16[256,1024]{0,1:T(8,128)(2,1)} %collective-permute-done.1), channel_id=1, source_target_pairs={{2,3},{6,7},{10,11},{14,15},{18,19},{22,23},{26,27},{30,31}} | collective-permute-start | bytes 1572872 | tf_op jit(solution)/shard_map/ppermute | solution.py:61
  77.9 22.4 %collective-permute-start.11 = (bf16[256,1024]{0,1:T(8,128)(2,1)}, bf16[256,1024]{0,1:T(8,128)(2,1)S(1)}, u32[]{:S(2)}, u32[]{:S(2)}) collective-permute-start(bf16[256,1024]{0,1:T(8,128)(2,1)} %collective-permute-done.10), channel_id=1, source_target_pairs={{1,0},{5,4},{9,8},{13,12},{17,16},{21,20},{25,24},{29,28}} | collective-permute-start | bytes 1572872 | tf_op jit(solution)/shard_map/ppermute | solution.py:65
  89.1 21.8 %collective-permute-start.5 = (bf16[256,1024]{0,1:T(8,128)(2,1)}, bf16[256,1024]{0,1:T(8,128)(2,1)}, u32[]{:S(2)}, u32[]{:S(2)}) collective-permute-start(bf16[256,1024]{0,1:T(8,128)(2,1)} %collective-permute-done.4), channel_id=1, source_target_pairs={{1,0},{5,4},{9,8},{13,12},{17,16},{21,20},{25,24},{29,28}} | collective-permute-start | bytes 1572872 | tf_op jit(solution)/shard_map/ppermute | solution.py:65
  91.1 105.1 %collective-permute-start.17 = (bf16[3,1024,512]{2,1,0:T(8,128)(2,1)}, bf16[3,1024,512]{2,1,0:T(8,128)(2,1)}, u32[]{:S(2)}, u32[]{:S(2)}) collective-permute-start(bf16[3,1024,512]{2,1,0:T(8,128)(2,1)} %all-gather.5.cloned.1.call-done), channel_id=1, source_target_pairs={{0,4},{4,0},{1,5},{5,1},{2,6},{6,2},{3,7},{7,3},{8,12},{12,8},{9,1... | collective-permute-start | bytes 9437192 | tf_op jit(solution)/shard_map/ppermute | solution.py:23
  124.4 114.3 %collective-permute-start.18 = (bf16[2,1024,1408]{2,1,0:T(8,128)(2,1)}, bf16[2,1024,1408]{2,1,0:T(8,128)(2,1)}, u32[]{:S(2)}, u32[]{:S(2)}) collective-permute-start(bf16[2,1024,1408]{2,1,0:T(8,128)(2,1)} %all-gather.9.cloned.1.call-done), channel_id=1, source_target_pairs={{0,4},{4,0},{1,5},{5,1},{2,6},{6,2},{3,7},{7,3},{8,12},{12,8},{9,1... | collective-permute-start | bytes 17301512 | tf_op jit(solution)/shard_map/ppermute | solution.py:23
  152.8 107.6 %collective-permute-start.25 = (bf16[512,1024]{1,0:T(8,128)(2,1)}, bf16[512,1024]{1,0:T(8,128)(2,1)}, u32[]{:S(2)}, u32[]{:S(2)}) collective-permute-start(bf16[512,1024]{1,0:T(8,128)(2,1)} %all-gather.7.cloned.1.call-done), channel_id=1, source_target_pairs={{0,4},{4,0},{1,5},{5,1},{2,6},{6,2},{3,7},{7,3},{8,12},{12,8},{9,1... | collective-permute-start | bytes 3145736 | tf_op jit(solution)/shard_map/ppermute | solution.py:23
  196.2 56.6 %collective-permute-start.26 = (bf16[1408,1024]{1,0:T(8,128)(2,1)}, bf16[1408,1024]{1,0:T(8,128)(2,1)}, u32[]{:S(2)}, u32[]{:S(2)}) collective-permute-start(bf16[1408,1024]{1,0:T(8,128)(2,1)} %all-gather.11.cloned.1.call-done), channel_id=1, source_target_pairs={{0,4},{4,0},{1,5},{5,1},{2,6},{6,2},{3,7},{7,3},{8,12},{12,8},{9,1... | collective-permute-start | bytes 8650760 | tf_op jit(solution)/shard_map/ppermute | solution.py:23
  267.7 17.4 %collective-permute-start.27 = (bf16[256,1024]{0,1:T(8,128)(2,1)}, bf16[256,1024]{0,1:T(8,128)(2,1)}, u32[]{:S(2)}, u32[]{:S(2)}) collective-permute-start(bf16[256,1024]{0,1:T(8,128)(2,1)} %get-tuple-element.101), channel_id=1, source_target_pairs={{0,1},{4,5},{8,9},{12,13},{16,17},{20,21},{24,25},{28,29}} | collective-permute-start | bytes 1572872 | tf_op jit(solution)/shard_map/ppermute | solution.py:88
  281.6 13.8 %collective-permute-start.19 = (bf16[256,1024]{0,1:T(8,128)(2,1)}, bf16[256,1024]{0,1:T(8,128)(2,1)}, u32[]{:S(2)}, u32[]{:S(2)}) collective-permute-start(bf16[256,1024]{0,1:T(8,128)(2,1)} %get-tuple-element.105), channel_id=1, source_target_pairs={{0,1},{4,5},{8,9},{12,13},{16,17},{20,21},{24,25},{28,29}} | collective-permute-start | bytes 1572872 | tf_op jit(solution)/shard_map/ppermute | solution.py:88
  283.7 24.4 %collective-permute-start.30 = (bf16[256,1024]{0,1:T(8,128)(2,1)}, bf16[256,1024]{0,1:T(8,128)(2,1)}, u32[]{:S(2)}, u32[]{:S(2)}) collective-permute-start(bf16[256,1024]{0,1:T(8,128)(2,1)} %get-tuple-element.102), channel_id=1, source_target_pairs={{3,2},{7,6},{11,10},{15,14},{19,18},{23,22},{27,26},{31,30}} | collective-permute-start | bytes 1572872 | tf_op jit(solution)/shard_map/ppermute | solution.py:92
  287.4 20.7 %collective-permute-start.28 = (bf16[256,1024]{0,1:T(8,128)(2,1)}, bf16[256,1024]{0,1:T(8,128)(2,1)}, u32[]{:S(2)}, u32[]{:S(2)}) collective-permute-start(bf16[256,1024]{0,1:T(8,128)(2,1)} %add_convert_fusion.14), channel_id=1, source_target_pairs={{0,1},{1,2},{4,5},{5,6},{8,9},{9,10},{12,13},{13,14},{16,17},{17,1... | collective-permute-start | bytes 1572872 | tf_op jit(solution)/shard_map/ppermute | solution.py:88
  290.9 21.0 %collective-permute-start.22 = (bf16[256,1024]{0,1:T(8,128)(2,1)}, bf16[256,1024]{0,1:T(8,128)(2,1)}, u32[]{:S(2)}, u32[]{:S(2)}) collective-permute-start(bf16[256,1024]{0,1:T(8,128)(2,1)} %get-tuple-element.106), channel_id=1, source_target_pairs={{3,2},{7,6},{11,10},{15,14},{19,18},{23,22},{27,26},{31,30}} | collective-permute-start | bytes 1572872 | tf_op jit(solution)/shard_map/ppermute | solution.py:92
  297.7 19.8 %collective-permute-start.20 = (bf16[256,1024]{0,1:T(8,128)(2,1)}, bf16[256,1024]{0,1:T(8,128)(2,1)}, u32[]{:S(2)}, u32[]{:S(2)}) collective-permute-start(bf16[256,1024]{0,1:T(8,128)(2,1)} %add_convert_fusion.18), channel_id=1, source_target_pairs={{0,1},{1,2},{4,5},{5,6},{8,9},{9,10},{12,13},{13,14},{16,17},{17,1... | collective-permute-start | bytes 1572872 | tf_op jit(solution)/shard_map/ppermute | solution.py:88
  311.0 23.5 %collective-permute-start.31 = (bf16[256,1024]{0,1:T(8,128)(2,1)S(1)}, bf16[256,1024]{0,1:T(8,128)(2,1)S(1)}, u32[]{:S(2)}, u32[]{:S(2)}) collective-permute-start(bf16[256,1024]{0,1:T(8,128)(2,1)S(1)} %get-tuple-element.100), channel_id=1, source_target_pairs={{2,1},{3,2},{6,5},{7,6},{10,9},{11,10},{14,13},{15,14},{18,17},{19... | collective-permute-start | bytes 1572872 | tf_op jit(solution)/shard_map/ppermute | solution.py:92
  320.4 17.5 %collective-permute-start.23 = (bf16[256,1024]{0,1:T(8,128)(2,1)S(1)}, bf16[256,1024]{0,1:T(8,128)(2,1)S(1)}, u32[]{:S(2)}, u32[]{:S(2)}) collective-permute-start(bf16[256,1024]{0,1:T(8,128)(2,1)S(1)} %get-tuple-element.104), channel_id=1, source_target_pairs={{2,1},{3,2},{6,5},{7,6},{10,9},{11,10},{14,13},{15,14},{18,17},{19... | collective-permute-start | bytes 1572872 | tf_op jit(solution)/shard_map/ppermute | solution.py:92
  324.1 36.2 %collective-permute-start.29 = (bf16[256,1024]{0,1:T(8,128)(2,1)}, bf16[256,1024]{0,1:T(8,128)(2,1)}, u32[]{:S(2)}, u32[]{:S(2)}) collective-permute-start(bf16[256,1024]{0,1:T(8,128)(2,1)} %get-tuple-element.99), channel_id=1, source_target_pairs={{0,1},{1,2},{2,3},{4,5},{5,6},{6,7},{8,9},{9,10},{10,11},{12,13},{... | collective-permute-start | bytes 1572872 | tf_op jit(solution)/shard_map/ppermute | solution.py:88
  330.0 30.3 %collective-permute-start.21 = (bf16[256,1024]{0,1:T(8,128)(2,1)}, bf16[256,1024]{0,1:T(8,128)(2,1)}, u32[]{:S(2)}, u32[]{:S(2)}) collective-permute-start(bf16[256,1024]{0,1:T(8,128)(2,1)} %get-tuple-element.103), channel_id=1, source_target_pairs={{0,1},{1,2},{2,3},{4,5},{5,6},{6,7},{8,9},{9,10},{10,11},{12,13},{... | collective-permute-start | bytes 1572872 | tf_op jit(solution)/shard_map/ppermute | solution.py:88
  336.7 23.6 %collective-permute-start.32 = (bf16[256,1024]{0,1:T(8,128)(2,1)}, bf16[256,1024]{0,1:T(8,128)(2,1)}, u32[]{:S(2)}, u32[]{:S(2)}) collective-permute-start(bf16[256,1024]{0,1:T(8,128)(2,1)} %add_convert_fusion.11), channel_id=1, source_target_pairs={{1,0},{2,1},{3,2},{5,4},{6,5},{7,6},{9,8},{10,9},{11,10},{13,12},{... | collective-permute-start | bytes 1572872 | tf_op jit(solution)/shard_map/ppermute | solution.py:92
  340.2 22.7 %collective-permute-start.24 = (bf16[256,1024]{0,1:T(8,128)(2,1)}, bf16[256,1024]{0,1:T(8,128)(2,1)}, u32[]{:S(2)}, u32[]{:S(2)}) collective-permute-start(bf16[256,1024]{0,1:T(8,128)(2,1)} %add_convert_fusion.15), channel_id=1, source_target_pairs={{1,0},{2,1},{3,2},{5,4},{6,5},{7,6},{9,8},{10,9},{11,10},{13,12},{... | collective-permute-start | bytes 1572872 | tf_op jit(solution)/shard_map/ppermute | solution.py:92
  367.0 15.7 %collective-permute-start.39 = (bf16[256,1024]{0,1:T(8,128)(2,1)S(1)}, bf16[256,1024]{0,1:T(8,128)(2,1)S(1)}, u32[]{:S(2)}, u32[]{:S(2)}) collective-permute-start(bf16[256,1024]{0,1:T(8,128)(2,1)S(1)} %get-tuple-element.154), channel_id=1, source_target_pairs={{0,1},{1,2},{2,3},{4,5},{5,6},{6,7},{8,9},{9,10},{10,11},{12,13},{... | collective-permute-start | bytes 1572872 | tf_op jit(solution)/shard_map/ppermute | solution.py:61
  370.4 16.8 %collective-permute-start.42 = (bf16[256,1024]{0,1:T(8,128)(2,1)S(1)}, bf16[256,1024]{0,1:T(8,128)(2,1)S(1)}, u32[]{:S(2)}, u32[]{:S(2)}) collective-permute-start(bf16[256,1024]{0,1:T(8,128)(2,1)S(1)} %get-tuple-element.154), channel_id=1, source_target_pairs={{1,0},{2,1},{3,2},{5,4},{6,5},{7,6},{9,8},{10,9},{11,10},{13,12},{... | collective-permute-start | bytes 1572872 | tf_op jit(solution)/shard_map/ppermute | solution.py:65
  371.7 19.8 %collective-permute-start.33 = (bf16[256,1024]{0,1:T(8,128)(2,1)S(1)}, bf16[256,1024]{0,1:T(8,128)(2,1)S(1)}, u32[]{:S(2)}, u32[]{:S(2)}) collective-permute-start(bf16[256,1024]{0,1:T(8,128)(2,1)S(1)} %get-tuple-element.153), channel_id=1, source_target_pairs={{0,1},{1,2},{2,3},{4,5},{5,6},{6,7},{8,9},{9,10},{10,11},{12,13},{... | collective-permute-start | bytes 1572872 | tf_op jit(solution)/shard_map/ppermute | solution.py:61
  376.2 22.1 %collective-permute-start.36 = (bf16[256,1024]{0,1:T(8,128)(2,1)S(1)}, bf16[256,1024]{0,1:T(8,128)(2,1)S(1)}, u32[]{:S(2)}, u32[]{:S(2)}) collective-permute-start(bf16[256,1024]{0,1:T(8,128)(2,1)S(1)} %get-tuple-element.153), channel_id=1, source_target_pairs={{1,0},{2,1},{3,2},{5,4},{6,5},{7,6},{9,8},{10,9},{11,10},{13,12},{... | collective-permute-start | bytes 1572872 | tf_op jit(solution)/shard_map/ppermute | solution.py:65
  382.7 17.0 %collective-permute-start.40 = (bf16[256,1024]{0,1:T(8,128)(2,1)S(1)}, bf16[256,1024]{0,1:T(8,128)(2,1)S(1)}, u32[]{:S(2)}, u32[]{:S(2)}) collective-permute-start(bf16[256,1024]{0,1:T(8,128)(2,1)S(1)} %collective-permute-done.39), channel_id=1, source_target_pairs={{1,2},{2,3},{5,6},{6,7},{9,10},{10,11},{13,14},{14,15},{17,18},{18... | collective-permute-start | bytes 1572872 | tf_op jit(solution)/shard_map/ppermute | solution.py:61
  387.1 22.5 %collective-permute-start.43 = (bf16[256,1024]{0,1:T(8,128)(2,1)S(1)}, bf16[256,1024]{0,1:T(8,128)(2,1)S(1)}, u32[]{:S(2)}, u32[]{:S(2)}) collective-permute-start(bf16[256,1024]{0,1:T(8,128)(2,1)S(1)} %collective-permute-done.42), channel_id=1, source_target_pairs={{1,0},{2,1},{5,4},{6,5},{9,8},{10,9},{13,12},{14,13},{17,16},{18,1... | collective-permute-start | bytes 1572872 | tf_op jit(solution)/shard_map/ppermute | solution.py:65
  391.5 19.4 %collective-permute-start.34 = (bf16[256,1024]{0,1:T(8,128)(2,1)S(1)}, bf16[256,1024]{0,1:T(8,128)(2,1)S(1)}, u32[]{:S(2)}, u32[]{:S(2)}) collective-permute-start(bf16[256,1024]{0,1:T(8,128)(2,1)S(1)} %collective-permute-done.33), channel_id=1, source_target_pairs={{1,2},{2,3},{5,6},{6,7},{9,10},{10,11},{13,14},{14,15},{17,18},{18... | collective-permute-start | bytes 1572872 | tf_op jit(solution)/shard_map/ppermute | solution.py:61
  398.3 22.5 %collective-permute-start.37 = (bf16[256,1024]{0,1:T(8,128)(2,1)S(1)}, bf16[256,1024]{0,1:T(8,128)(2,1)S(1)}, u32[]{:S(2)}, u32[]{:S(2)}) collective-permute-start(bf16[256,1024]{0,1:T(8,128)(2,1)S(1)} %collective-permute-done.36), channel_id=1, source_target_pairs={{1,0},{2,1},{5,4},{6,5},{9,8},{10,9},{13,12},{14,13},{17,16},{18,1... | collective-permute-start | bytes 1572872 | tf_op jit(solution)/shard_map/ppermute | solution.py:65
  399.6 22.5 %collective-permute-start.41 = (bf16[256,1024]{0,1:T(8,128)(2,1)S(1)}, bf16[256,1024]{0,1:T(8,128)(2,1)S(1)}, u32[]{:S(2)}, u32[]{:S(2)}) collective-permute-start(bf16[256,1024]{0,1:T(8,128)(2,1)S(1)} %collective-permute-done.40), channel_id=1, source_target_pairs={{2,3},{6,7},{10,11},{14,15},{18,19},{22,23},{26,27},{30,31}} | collective-permute-start | bytes 1572872 | tf_op jit(solution)/shard_map/ppermute | solution.py:61
  409.6 22.5 %collective-permute-start.44 = (bf16[256,1024]{0,1:T(8,128)(2,1)S(1)}, bf16[256,1024]{0,1:T(8,128)(2,1)S(1)}, u32[]{:S(2)}, u32[]{:S(2)}) collective-permute-start(bf16[256,1024]{0,1:T(8,128)(2,1)S(1)} %collective-permute-done.43), channel_id=1, source_target_pairs={{1,0},{5,4},{9,8},{13,12},{17,16},{21,20},{25,24},{29,28}} | collective-permute-start | bytes 1572872 | tf_op jit(solution)/shard_map/ppermute | solution.py:65
  410.9 28.1 %collective-permute-start.35 = (bf16[256,1024]{0,1:T(8,128)(2,1)S(1)}, bf16[256,1024]{0,1:T(8,128)(2,1)S(1)}, u32[]{:S(2)}, u32[]{:S(2)}) collective-permute-start(bf16[256,1024]{0,1:T(8,128)(2,1)S(1)} %collective-permute-done.34), channel_id=1, source_target_pairs={{2,3},{6,7},{10,11},{14,15},{18,19},{22,23},{26,27},{30,31}} | collective-permute-start | bytes 1572872 | tf_op jit(solution)/shard_map/ppermute | solution.py:61
  420.8 19.8 %collective-permute-start.38 = (bf16[256,1024]{0,1:T(8,128)(2,1)S(1)}, bf16[256,1024]{0,1:T(8,128)(2,1)S(1)}, u32[]{:S(2)}, u32[]{:S(2)}) collective-permute-start(bf16[256,1024]{0,1:T(8,128)(2,1)S(1)} %collective-permute-done.37), channel_id=1, source_target_pairs={{1,0},{5,4},{9,8},{13,12},{17,16},{21,20},{25,24},{29,28}} | collective-permute-start | bytes 1572872 | tf_op jit(solution)/shard_map/ppermute | solution.py:65
  437.1 15.0 %collective-permute-start.65 = (bf16[1408,1024]{1,0:T(8,128)(2,1)}, bf16[1408,1024]{1,0:T(8,128)(2,1)}, u32[]{:S(2)}, u32[]{:S(2)}) collective-permute-start(bf16[1408,1024]{1,0:T(8,128)(2,1)} %convolution_convert_fusion), channel_id=1, source_target_pairs={{0,4},{4,0},{1,5},{5,1},{2,6},{6,2},{3,7},{7,3},{8,12},{12,8},{9,1... | collective-permute-start | bytes 8650760 | tf_op jit(solution)/shard_map/ppermute | solution.py:23
  446.2 243.8 %reduce-scatter.11.cloned.1.call-start = ((), (), s32[]{:S(2)}) async-start(), calls=%async_computation.11 | async-start | bytes 3604480 | tf_op jit(solution)/shard_map/reduce_scatter | solution.py:380
  458.1 234.2 %reduce-scatter.5.cloned.1.call-start = ((), (), s32[]{:S(2)}) async-start(), calls=%async_computation.8 | async-start | bytes 3932160 | tf_op jit(solution)/shard_map/reduce_scatter | solution.py:380
  496.6 31.3 %collective-permute-start.62 = (bf16[3,1024,512]{1,2,0:T(8,128)(2,1)S(1)}, bf16[3,1024,512]{1,2,0:T(8,128)(2,1)S(1)}, u32[]{:S(2)}, u32[]{:S(2)}) collective-permute-start(bf16[3,1024,512]{1,2,0:T(8,128)(2,1)S(1)} %convert_bitcast_fusion.1), channel_id=1, source_target_pairs={{0,4},{4,0},{1,5},{5,1},{2,6},{6,2},{3,7},{7,3},{8,12},{12,8},{9,1... | collective-permute-start | bytes 9437192 | tf_op jit(solution)/shard_map/ppermute | solution.py:23
  535.3 159.6 %reduce-scatter.9.cloned.1.call-start = ((), (), s32[]{:S(2)}) async-start(), calls=%async_computation.10 | async-start | bytes 7208960 | tf_op jit(solution)/shard_map/reduce_scatter | solution.py:380
  591.7 14.1 %collective-permute-start.50 = (bf16[256,1024]{0,1:T(8,128)(2,1)S(1)}, bf16[256,1024]{0,1:T(8,128)(2,1)S(1)}, u32[]{:S(2)}, u32[]{:S(2)}) collective-permute-start(bf16[256,1024]{0,1:T(8,128)(2,1)S(1)} %get-tuple-element.97), channel_id=1, source_target_pairs={{0,1},{4,5},{8,9},{12,13},{16,17},{20,21},{24,25},{28,29}} | collective-permute-start | bytes 1572872 | tf_op jit(solution)/shard_map/ppermute | solution.py:88
  596.8 26.9 %collective-permute-start.53 = (bf16[256,1024]{0,1:T(8,128)(2,1)}, bf16[256,1024]{0,1:T(8,128)(2,1)S(1)}, u32[]{:S(2)}, u32[]{:S(2)}) collective-permute-start(bf16[256,1024]{0,1:T(8,128)(2,1)} %get-tuple-element.98), channel_id=1, source_target_pairs={{3,2},{7,6},{11,10},{15,14},{19,18},{23,22},{27,26},{31,30}} | collective-permute-start | bytes 1572872 | tf_op jit(solution)/shard_map/ppermute | solution.py:92
  597.5 19.5 %collective-permute-start.56 = (bf16[256,1024]{0,1:T(8,128)(2,1)S(1)}, bf16[256,1024]{0,1:T(8,128)(2,1)S(1)}, u32[]{:S(2)}, u32[]{:S(2)}) collective-permute-start(bf16[256,1024]{0,1:T(8,128)(2,1)S(1)} %get-tuple-element.93), channel_id=1, source_target_pairs={{0,1},{4,5},{8,9},{12,13},{16,17},{20,21},{24,25},{28,29}} | collective-permute-start | bytes 1572872 | tf_op jit(solution)/shard_map/ppermute | solution.py:88
  598.8 31.9 %collective-permute-start.59 = (bf16[256,1024]{0,1:T(8,128)(2,1)}, bf16[256,1024]{0,1:T(8,128)(2,1)S(1)}, u32[]{:S(2)}, u32[]{:S(2)}) collective-permute-start(bf16[256,1024]{0,1:T(8,128)(2,1)} %get-tuple-element.94), channel_id=1, source_target_pairs={{3,2},{7,6},{11,10},{15,14},{19,18},{23,22},{27,26},{31,30}} | collective-permute-start | bytes 1572872 | tf_op jit(solution)/shard_map/ppermute | solution.py:92
  599.6 24.0 %collective-permute-start.47 = (f32[1,712]{1,0:T(1,128)S(1)}, f32[1,712]{1,0:T(1,128)S(1)}, u32[]{:S(2)}, u32[]{:S(2)}) collective-permute-start(f32[1,712]{1,0:T(1,128)S(1)} %fusion.52), channel_id=1, source_target_pairs={{0,4},{4,0},{1,5},{5,1},{2,6},{6,2},{3,7},{7,3},{8,12},{12,8},{9,1... | collective-permute-start | bytes 8552 | tf_op jit(solution)/shard_map/ppermute | solution.py:47
  607.3 21.0 %collective-permute-start.51 = (bf16[256,1024]{0,1:T(8,128)(2,1)S(1)}, bf16[256,1024]{0,1:T(8,128)(2,1)S(1)}, u32[]{:S(2)}, u32[]{:S(2)}) collective-permute-start(bf16[256,1024]{0,1:T(8,128)(2,1)S(1)} %add_convert_fusion.10), channel_id=1, source_target_pairs={{0,1},{1,2},{4,5},{5,6},{8,9},{9,10},{12,13},{13,14},{16,17},{17,1... | collective-permute-start | bytes 1572872 | tf_op jit(solution)/shard_map/ppermute | solution.py:88
  618.4 20.0 %collective-permute-start.57 = (bf16[256,1024]{0,1:T(8,128)(2,1)S(1)}, bf16[256,1024]{0,1:T(8,128)(2,1)}, u32[]{:S(2)}, u32[]{:S(2)}) collective-permute-start(bf16[256,1024]{0,1:T(8,128)(2,1)S(1)} %add_convert_fusion.6), channel_id=1, source_target_pairs={{0,1},{1,2},{4,5},{5,6},{8,9},{9,10},{12,13},{13,14},{16,17},{17,1... | collective-permute-start | bytes 1572872 | tf_op jit(solution)/shard_map/ppermute | solution.py:88
  623.7 19.4 %collective-permute-start.48 = (f32[2,130]{1,0:T(2,128)S(1)}, f32[2,130]{1,0:T(2,128)S(1)}, u32[]{:S(2)}, u32[]{:S(2)}) collective-permute-start(f32[2,130]{1,0:T(2,128)S(1)} %select_n.580), channel_id=1, source_target_pairs={{0,2},{1,3},{2,0},{3,1},{4,6},{5,7},{6,4},{7,5},{8,10},{9,11},{10,... | collective-permute-start | bytes 3128 | tf_op jit(solution)/shard_map/ppermute | solution.py:47
  630.0 22.1 %collective-permute-start.54 = (bf16[256,1024]{0,1:T(8,128)(2,1)S(1)}, bf16[256,1024]{0,1:T(8,128)(2,1)S(1)}, u32[]{:S(2)}, u32[]{:S(2)}) collective-permute-start(bf16[256,1024]{0,1:T(8,128)(2,1)S(1)} %get-tuple-element.96), channel_id=1, source_target_pairs={{2,1},{3,2},{6,5},{7,6},{10,9},{11,10},{14,13},{15,14},{18,17},{19... | collective-permute-start | bytes 1572872 | tf_op jit(solution)/shard_map/ppermute | solution.py:92
  640.7 14.1 %collective-permute-start.60 = (bf16[256,1024]{0,1:T(8,128)(2,1)}, bf16[256,1024]{0,1:T(8,128)(2,1)}, u32[]{:S(2)}, u32[]{:S(2)}) collective-permute-start(bf16[256,1024]{0,1:T(8,128)(2,1)} %get-tuple-element.92), channel_id=1, source_target_pairs={{2,1},{3,2},{6,5},{7,6},{10,9},{11,10},{14,13},{15,14},{18,17},{19... | collective-permute-start | bytes 1572872 | tf_op jit(solution)/shard_map/ppermute | solution.py:92
  643.1 14.5 %collective-permute-start.49 = (f32[1,130]{1,0:T(1,128)S(1)}, f32[1,130]{1,0:T(1,128)S(1)}, u32[]{:S(2)}, u32[]{:S(2)}) collective-permute-start(f32[1,130]{1,0:T(1,128)S(1)} %broadcast_select_fusion.30), channel_id=1, source_target_pairs={{0,1},{1,0},{2,3},{3,2},{4,5},{5,4},{6,7},{7,6},{8,9},{9,8},{10,11... | collective-permute-start | bytes 1568 | tf_op jit(solution)/shard_map/ppermute | solution.py:47
  645.6 14.6 %collective-permute-start.52 = (bf16[256,1024]{0,1:T(8,128)(2,1)S(1)}, bf16[256,1024]{0,1:T(8,128)(2,1)S(1)}, u32[]{:S(2)}, u32[]{:S(2)}) collective-permute-start(bf16[256,1024]{0,1:T(8,128)(2,1)S(1)} %get-tuple-element.95), channel_id=1, source_target_pairs={{0,1},{1,2},{2,3},{4,5},{5,6},{6,7},{8,9},{9,10},{10,11},{12,13},{... | collective-permute-start | bytes 1572872 | tf_op jit(solution)/shard_map/ppermute | solution.py:88
  647.5 21.5 %collective-permute-start.58 = (bf16[256,1024]{0,1:T(8,128)(2,1)S(1)}, bf16[256,1024]{0,1:T(8,128)(2,1)S(1)}, u32[]{:S(2)}, u32[]{:S(2)}) collective-permute-start(bf16[256,1024]{0,1:T(8,128)(2,1)S(1)} %get-tuple-element.91), channel_id=1, source_target_pairs={{0,1},{1,2},{2,3},{4,5},{5,6},{6,7},{8,9},{9,10},{10,11},{12,13},{... | collective-permute-start | bytes 1572872 | tf_op jit(solution)/shard_map/ppermute | solution.py:88
  653.5 16.8 %collective-permute-start.55 = (bf16[256,1024]{0,1:T(8,128)(2,1)S(1)}, bf16[256,1024]{0,1:T(8,128)(2,1)S(1)}, u32[]{:S(2)}, u32[]{:S(2)}) collective-permute-start(bf16[256,1024]{0,1:T(8,128)(2,1)S(1)} %add_convert_fusion.7), channel_id=1, source_target_pairs={{1,0},{2,1},{3,2},{5,4},{6,5},{7,6},{9,8},{10,9},{11,10},{13,12},{... | collective-permute-start | bytes 1572872 | tf_op jit(solution)/shard_map/ppermute | solution.py:92
  656.3 22.3 %collective-permute-start.61 = (bf16[256,1024]{0,1:T(8,128)(2,1)S(1)}, bf16[256,1024]{0,1:T(8,128)(2,1)S(1)}, u32[]{:S(2)}, u32[]{:S(2)}) collective-permute-start(bf16[256,1024]{0,1:T(8,128)(2,1)S(1)} %add_convert_fusion.3), channel_id=1, source_target_pairs={{1,0},{2,1},{3,2},{5,4},{6,5},{7,6},{9,8},{10,9},{11,10},{13,12},{... | collective-permute-start | bytes 1572872 | tf_op jit(solution)/shard_map/ppermute | solution.py:92
  (68 other events, 1465.9 us)
Sparse Core Ops, SparseCore 0:
  9.9 46.6 all-gather.4
  58.4 65.9 all-gather.8
  126.2 26.4 all-gather.6
  154.4 41.6 all-gather.10
  446.3 25.0 reduce-scatter.6
  474.6 41.7 reduce-scatter.10
  535.4 41.3 reduce-scatter.4
  580.1 65.8 reduce-scatter.8

commit v2 on v1

v2 whole, which is shorter than its diff:
```python
import functools

import jax
import jax.numpy as jnp
from jax import lax
from jax.experimental import pallas as pl
from jax.experimental.pallas import tpu as pltpu
from jax.sharding import Mesh
from jax.sharding import PartitionSpec as P

D = 2048
HD = 64
ROT = 16
SEQ = 1024
PAIR = 2 * HD
SPAN = 256
epsilon = 1e-05
f32 = jnp.float32
bf16 = jnp.bfloat16


def after(value, *others):
    return lax.optimization_barrier((value,) + others)[0]


def swap_core(a):
    return lax.ppermute(a, "core", [(0, 1), (1, 0)])


def gather_axis(a, axis, n):
    me = lax.axis_index(axis)
    buf = a[None]
    k = 1
    while k < n:
        other = lax.ppermute(buf, axis, [(j, j ^ k) for j in range(n)])
        upper = (me // k) % 2 == 1
        buf = jnp.concatenate(
            [jnp.where(upper, other, buf), jnp.where(upper, buf, other)], 0
        )
        k *= 2
    return buf


def scatter_axis(a, axis, n):
    me = lax.axis_index(axis)
    buf = a
    k = n // 2
    while k >= 1:
        upper = (me // k) % 2 == 1
        lo, hi = buf[:k], buf[k:]
        sent = lax.ppermute(
            jnp.where(upper, lo, hi), axis, [(j, j ^ k) for j in range(n)]
        )
        buf = jnp.where(upper, hi, lo) + sent
        k //= 2
    return buf[0]


def line_scatter(part, n, holds=()):
    me = lax.axis_index("tp")
    rows = part.shape[0] // n

    def chunk(j):
        return lax.dynamic_slice_in_dim(part, jnp.clip(j, 0, n - 1) * rows, rows, 0)

    def plus(a, b):
        return a if b is None else (a.astype(f32) + b.astype(f32)).astype(bf16)

    up = down = None
    for s in range(n - 1):
        up = plus(chunk(n - 1 - s + me), up)
        down = plus(chunk(s - (n - 1) + me), down)
        up = lax.ppermute(up, "tp", [(k, k + 1) for k in range(s + 1)])
        down = lax.ppermute(down, "tp", [(k, k - 1) for k in range(n - 1 - s, n)])
        if s < len(holds):
            up, down = after(up, holds[s]), after(down, holds[s])
    return chunk(me).astype(f32) + up.astype(f32) + down.astype(f32)


def rotary_tables(line):
    half_rot = ROT // 2
    positions = jnp.arange(SEQ, dtype=jnp.int32).astype(f32)
    frequency = 10000.0 ** (-2.0 * jnp.arange(half_rot, dtype=f32) / ROT)
    angles = positions[:, None] * frequency[None, :]
    cos, sin = jnp.cos(angles), jnp.sin(angles)
    rest = HD - ROT
    zero = jnp.zeros((SEQ, rest), f32)
    keep = jnp.concatenate([cos, cos, jnp.ones((SEQ, rest), f32)], -1)
    ahead = jnp.concatenate([-sin, jnp.zeros_like(sin), zero], -1)
    behind = jnp.concatenate([jnp.zeros_like(sin), sin, zero], -1)
    one = jnp.stack([keep, ahead, behind])
    one = jnp.concatenate([one, one], -1).reshape(3, line, 2, -1, PAIR)
    return [one[:, :, t].reshape(3, SEQ // 2, PAIR) for t in range(2)]


def turned(v, tab_ref, sign):
    half_rot = ROT // 2
    return (
        v * tab_ref[0]
        + sign
        * (
            pltpu.roll(v, PAIR - half_rot, 1) * tab_ref[1]
            + pltpu.roll(v, half_rot, 1) * tab_ref[2]
        )
    )


def dot_nt(a, b):
    return lax.dot_general(a, b, (((1,), (1,)), ((), ())), preferred_element_type=f32)


def dot_nn(a, b):
    return lax.dot_general(a, b, (((1,), (0,)), ((), ())), preferred_element_type=f32)


def dot_tn(a, b):
    return lax.dot_general(a, b, (((0,), (0,)), ((), ())), preferred_element_type=f32)


def two_heads(a):
    lane = lax.broadcasted_iota(jnp.int32, a.shape, 1)
    zero = jnp.zeros_like(a)
    return jnp.concatenate([jnp.where(lane < HD, a, zero), jnp.where(lane < HD, zero, a)], 0)


def one_row_each(a):
    rows = a.shape[1] // 2
    dim = lax.broadcasted_iota(jnp.int32, (PAIR, rows), 0)
    return jnp.where(dim < HD, a[:, :rows], a[:, rows:]).T


def spans(part, z, span):
    return ((z + 1) * span, (z + part) * span)


def masked(a, span, fill):
    lo = a.shape[0] - span
    key = lax.broadcasted_iota(jnp.int32, (span, 2 * span), 0)
    query = lax.broadcasted_iota(jnp.int32, (span, 2 * span), 1)
    query = jnp.where(query >= span, query - span, query)
    tail = jnp.where(key <= query, a[lo:], fill)
    return jnp.concatenate([a[:lo], tail], 0) if lo else tail


def attend_kernel(part, span, q_ref, k0_ref, v0_ref, k1_ref, v1_ref, attn_ref, lse_ref):
    keys, values = (k0_ref, k1_ref), (v0_ref[0].T, v1_ref[0].T)
    for z in range(SEQ // 2 // span):
        rows = slice(z * span, (z + 1) * span)
        q = two_heads(q_ref[0, rows, :])
        scores = {}
        for t, count in enumerate(spans(part, z, span)):
            if count:
                scores[t] = dot_nt(keys[t][0, :count, :], q)
        scores[part] = masked(scores[part], span, -1e30)
        top = functools.reduce(
            jnp.maximum, [jnp.max(a, 0, keepdims=True) for a in scores.values()]
        )
        scores = {t: jnp.exp(a - top) for t, a in scores.items()}
        total = sum(jnp.sum(a, 0, keepdims=True) for a in scores.values())
        inverse = 1.0 / total
        out = sum(
            dot_nn(values[t][:, : a.shape[0]], (a * inverse).astype(bf16))
            for t, a in scores.items()
        )
        attn_ref[rows, :] = one_row_each(out).astype(bf16)
        lse_ref[0, z : z + 1, :] = top + jnp.log(total)


def head_spec(j):
    return pl.BlockSpec((1, SEQ // 2, PAIR), lambda p: (j, 0, p))


def attend(part, span, qkv):
    width = qkv[0].shape[2]
    pairs = width // PAIR
    blocks = SEQ // 2 // span
    half = SEQ // 2
    mine = pl.BlockSpec((half, PAIR), lambda p: (0, p))
    return pl.pallas_call(
        functools.partial(attend_kernel, part, span),
        grid=(pairs,),
        in_specs=[head_spec(0), head_spec(1), head_spec(2), head_spec(1), head_spec(2)],
        out_specs=[mine, pl.BlockSpec((1, blocks, 2 * span), lambda p: (p, 0, 0))],
        out_shape=[
            jax.ShapeDtypeStruct((half, width), bf16),
            jax.ShapeDtypeStruct((pairs, blocks, 2 * span), f32),
        ],
        compiler_params=pltpu.CompilerParams(vmem_limit_bytes=30 << 20),
        cost_estimate=pl.CostEstimate(
            flops=pairs * SEQ * SEQ * PAIR * 4,
            transcendentals=pairs * SEQ * SEQ,
            bytes_accessed=10 * SEQ * width,
        ),
        name="attend",
    )(qkv[part], qkv[0], qkv[0], qkv[1], qkv[1])


def attend_back_kernel(
    part, span, q_ref, k0_ref, v0_ref, k1_ref, v1_ref, grad_ref, lse_ref, tab0_ref, tab1_ref, *refs
):
    scale = HD ** (-0.5)
    half = SEQ // 2
    if part == 0:
        gq_ref, *gkv_refs = refs
        sums = gkv_refs
        for ref in sums:
            ref[...] = jnp.zeros_like(ref)
    else:
        gq0_ref, *kept = refs[:5]
        out_ref, bias_ref, gq_ref, *sums = refs[5:]
        for ref, old in zip(sums, kept):
            ref[...] = old[...]
    keys, values = (k0_ref, k1_ref), (v0_ref, v1_ref)
    turned_keys = (k0_ref[0].T, k1_ref[0].T)
    for z in range(half // span):
        rows = slice(z * span, (z + 1) * span)
        q, g = two_heads(q_ref[0, rows, :]), two_heads(grad_ref[rows, :])
        lse = lse_ref[0, z : z + 1, :]
        probs, gprobs = {}, {}
        inner = 0.0
        for t, count in enumerate(spans(part, z, span)):
            if count:
                p = jnp.exp(dot_nt(keys[t][0, :count, :], q) - lse)
                probs[t] = masked(p, span, 0.0) if t == part else p
                gprobs[t] = dot_nt(values[t][0, :count, :], g)
                inner = inner + jnp.sum(probs[t] * gprobs[t], 0, keepdims=True)
        gq = 0.0
        for t, p in probs.items():
            count = p.shape[0]
            gs = (p * (gprobs[t] - inner)).astype(bf16)
            sums[2 * t][:count, :] += dot_nn(gs, q)
            sums[2 * t + 1][:count, :] += dot_nn(p.astype(bf16), g)
            gq = gq + dot_nn(turned_keys[t][:, :count], gs)
        gq_ref[rows, :] = one_row_each(gq) * scale
    if part == 1:
        pairs = pl.num_programs(0)
        pair = pl.program_id(0)
        for j in range(3):
            lanes = pl.ds(pl.multiple_of((j * pairs + pair) * PAIR, PAIR), PAIR)
            bias = 0.0
            for t, tab_ref in enumerate((tab0_ref, tab1_ref)):
                g = sums[2 * t + j - 1][...] if j else (gq_ref if t else gq0_ref)[...]
                if j < 2:
                    g = turned(g, tab_ref, -1.0)
                g = g.astype(bf16)
                out_ref[t * half : (t + 1) * half, lanes] = g
                bias = bias + jnp.sum(g.astype(f32).reshape(half // 8, 8, PAIR), 0)
            bias_ref[:, lanes] = bias


def attend_back(part, span, qkv, grad, lse, tables, kept=()):
    width = grad.shape[1]
    pairs = width // PAIR
    blocks = SEQ // 2 // span
    half = SEQ // 2
    mine = pl.BlockSpec((half, PAIR), lambda p: (0, p))
    table = pl.BlockSpec((3, half, PAIR), lambda p: (0, 0, 0))
    partial_shapes = [jax.ShapeDtypeStruct((half, width), f32)] * 5
    if part == 0:
        out_specs, out_shape, scratch = [mine] * 5, partial_shapes, []
    else:
        out_specs = [
            pl.BlockSpec((SEQ, 3 * width), lambda p: (0, 0)),
            pl.BlockSpec((8, 3 * width), lambda p: (0, 0)),
        ]
        out_shape = [
            jax.ShapeDtypeStruct((SEQ, 3 * width), bf16),
            jax.ShapeDtypeStruct((8, 3 * width), f32),
        ]
        scratch = [pltpu.VMEM((half, PAIR), f32)] * 5
    return pl.pallas_call(
        functools.partial(attend_back_kernel, part, span),
        grid=(pairs,),
        in_specs=[head_spec(0), head_spec(1), head_spec(2), head_spec(1), head_spec(2)]
        + [mine, pl.BlockSpec((1, blocks, 2 * span), lambda p: (p, 0, 0)), table, table]
        + [mine] * len(kept),
        out_specs=out_specs,
        out_shape=out_shape,
        scratch_shapes=scratch,
        compiler_params=pltpu.CompilerParams(vmem_limit_bytes=30 << 20),
        cost_estimate=pl.CostEstimate(
            flops=pairs * SEQ * SEQ * PAIR * 10,
            transcendentals=pairs * SEQ * SEQ,
            bytes_accessed=20 * SEQ * width,
        ),
        name="attend_back",
    )(qkv[part], qkv[0], qkv[0], qkv[1], qkv[1], grad, lse, *tables, *kept)


def call(kernel, name, grid, in_specs, out_specs, out_shape, scalars, args, flops=0, scratch=()):
    moved = sum(a.size * a.dtype.itemsize for a in args)
    moved += sum(o.size * jnp.dtype(o.dtype).itemsize for o in out_shape)
    return pl.pallas_call(
        kernel,
        grid_spec=pltpu.PrefetchScalarGridSpec(
            num_scalar_prefetch=1,
            grid=grid,
            in_specs=in_specs,
            out_specs=out_specs,
            scratch_shapes=scratch,
        ),
        out_shape=out_shape,
        compiler_params=pltpu.CompilerParams(vmem_limit_bytes=30 << 20),
        cost_estimate=pl.CostEstimate(flops=flops, transcendentals=0, bytes_accessed=moved),
        name=name,
    )(scalars, *args)


def whole_spec(shape):
    zeros = (0,) * len(shape)
    return pl.BlockSpec(shape, lambda i, s: zeros, pipeline_mode=pl.Buffered(1))


def shard_spec(w):
    rest = (0,) * (w.ndim - 1)
    return pl.BlockSpec((1,) + w.shape[1:], lambda k, s: (k,) + rest)


def all_spec(rows, cols):
    return pl.BlockSpec((rows, cols), lambda k, s: (0, 0), pipeline_mode=pl.Buffered(1))


def over_rows(rows, step, body):
    @pl.loop(0, rows // step)
    def _(i):
        body(pl.ds(pl.multiple_of(i * step, step), step))


def row_spec(rows, cols):
    return pl.BlockSpec((rows, cols), lambda i, s: (i, 0))


def shape_of(shape, dtype):
    return jax.ShapeDtypeStruct(shape, dtype)


def lanes_of(scalar_ref, h, p, feats):
    block = 2 * p + jnp.bitwise_xor(scalar_ref[0], h)
    return pl.ds(pl.multiple_of(block * feats, feats), feats)


def shard_lanes(scalar_ref, k, feats, first=0):
    block = jnp.bitwise_xor(scalar_ref[1], k)
    return pl.ds(pl.multiple_of(first + block * feats, feats), feats)


def moments(x):
    mean = jnp.sum(x, -1, keepdims=True) / D
    x = x - mean
    return mean, lax.rsqrt(jnp.sum(x * x, -1, keepdims=True) / D + epsilon)


def norm_kernel(feats, s_ref, x_ref, vec_ref, own_ref, other_ref, stat_ref, copy_ref):
    mean, inv = moments(x_ref[...].astype(f32))
    copy_ref[...] = x_ref[...]
    for h, out_ref in enumerate((own_ref, other_ref)):
        for p in range(D // (2 * feats)):
            at = lanes_of(s_ref, h, p, feats)
            u = (x_ref[:, at].astype(f32) - mean) * inv
            out_ref[:, p * feats : (p + 1) * feats] = (
                u * vec_ref[0:1, at] + vec_ref[1:2, at]
            ).astype(bf16)
    lane = lax.broadcasted_iota(jnp.int32, stat_ref.shape, 1)
    stat_ref[...] = jnp.where(lane < PAIR // 2, mean, inv)


def norm(scalars, part, span, x, vectors, feats):
    half = D // 2
    rows = SEQ // 2
    return call(
        functools.partial(norm_kernel, feats),
        "norm",
        (rows // span,),
        [pl.BlockSpec((span, D), lambda z, s: (2 * z + part, 0)), whole_spec((2, D))],
        [row_spec(span, half), row_spec(span, half), row_spec(span, PAIR), row_spec(span, D)],
        [shape_of((rows, half), bf16)] * 2
        + [shape_of((rows, PAIR), f32), shape_of((rows, D), bf16)],
        scalars,
        (x, vectors),
    )


def joined_kernel(
    s_ref, own_ref, other_ref, bias_ref, tab_ref, w0_ref, w1_ref, out_ref, sum_ref
):
    _, many, feats, width = w0_ref.shape
    k, last_k = pl.program_id(0), pl.num_programs(0) - 1
    at = shard_lanes(s_ref, k, feats)
    rows = own_ref.shape[0]

    @pl.when(k == 0)
    def _():
        for j in range(many):
            sum_ref[j] = jnp.broadcast_to(bias_ref[j], (rows, width))

    def step(here):
        x0, x1 = own_ref[here, at], other_ref[here, at]
        for j in range(many):
            sum_ref[j, here, :] += dot_nn(x0, w0_ref[0, j]) + dot_nn(x1, w1_ref[0, j])

    over_rows(rows, SPAN, step)

    @pl.when(k == last_k)
    def _():
        def rotate(here):
            tab = tab_ref[:, here, :]
            for j in range(2):
                scale = 1.0 if j else HD ** (-0.5)
                for p in range(width // PAIR):
                    lanes = slice(p * PAIR, (p + 1) * PAIR)
                    out_ref[j, here, lanes] = (
                        turned(sum_ref[j, here, lanes], tab, 1.0) * scale
                    ).astype(bf16)
            out_ref[2, here, :] = sum_ref[2, here, :].astype(bf16)

        over_rows(rows, 64, rotate)


def joined_heads(scalars, normed, weights, bias, table):
    chips, many, _, width = weights[0].shape
    rows = normed[0].shape[0]
    return call(
        joined_kernel,
        "joined",
        (chips,),
        [all_spec(rows, D // 2)] * 2
        + [whole_spec((3, 1, width)), whole_spec((3, rows, PAIR))]
        + [shard_spec(w) for w in weights],
        [pl.BlockSpec((3, rows, width), lambda k, s: (0, 0, 0))],
        [shape_of((3, rows, width), bf16)],
        scalars,
        (*normed, bias, table, *weights),
        flops=2 * rows * D * 3 * width,
        scratch=[pltpu.VMEM((many, rows, width), f32)],
    )[0]


def gate_up_kernel(
    s_ref, own_ref, other_ref, attn_ref, w0_ref, w1_ref, gate_ref, up_ref, acts_ref
):
    width = attn_ref.shape[1]
    feats = w0_ref.shape[2]
    k, last_k = pl.program_id(0), pl.num_programs(0) - 1
    at = shard_lanes(s_ref, k, feats)
    rows = own_ref.shape[0]

    @pl.when(k == 0)
    def _():
        gate_ref[...] = jnp.zeros_like(gate_ref)
        up_ref[...] = jnp.zeros_like(up_ref)
        acts_ref[:, :width] = attn_ref[...]

    def step(here):
        x0, x1 = own_ref[here, at], other_ref[here, at]
        for j, out_ref in enumerate((gate_ref, up_ref)):
            out_ref[here, :] += dot_nn(x0, w0_ref[0, j]) + dot_nn(x1, w1_ref[0, j])

    over_rows(rows, SPAN, step)

    @pl.when(k == last_k)
    def _():
        def join(here):
            gate = gate_ref[here, :]
            acts_ref[here, width:] = (gate * jax.nn.sigmoid(gate) * up_ref[here, :]).astype(bf16)

        over_rows(rows, 64, join)


def gate_up(scalars, normed, attn, weights):
    chips, _, _, hid = weights[0].shape
    rows, width = attn.shape
    return call(
        gate_up_kernel,
        "gate_up",
        (chips,),
        [all_spec(rows, D // 2)] * 2
        + [all_spec(rows, width)]
        + [shard_spec(w) for w in weights],
        [all_spec(rows, hid), all_spec(rows, hid), all_spec(rows, width + hid)],
        [shape_of((rows, hid), f32)] * 2 + [shape_of((rows, width + hid), bf16)],
        scalars,
        (*normed, attn, *weights),
        flops=4 * rows * D * hid,
    )


def branch_kernel(s_ref, acts_ref, w0_ref, w1_ref, out_ref):
    feats = w0_ref.shape[2]
    p = pl.program_id(0)
    rows = acts_ref.shape[0]

    def step(here):
        acts = acts_ref[here, :]
        for h, w_ref in enumerate((w0_ref, w1_ref)):
            at = pl.ds(pl.multiple_of(h * D // 2 + p * feats, feats), feats)
            out_ref[here, at] = dot_nn(acts, w_ref[0]).astype(bf16)

    over_rows(rows, SPAN, step)


def branch_sums(scalars, acts, weights):
    chips = weights[0].shape[0]
    rows, deep = acts.shape
    return call(
        branch_kernel,
        "branch",
        (chips,),
        [all_spec(rows, deep)] + [shard_spec(w) for w in weights],
        [all_spec(rows, D)],
        [shape_of((rows, D), bf16)],
        scalars,
        (acts, *weights),
        flops=2 * rows * deep * D,
    )[0]


def finish_kernel(
    feats, part, s_ref, branch_ref, x_ref, teach_ref, cot_ref, old_ref,
    result_ref, seed_ref, low_ref, loss_ref,
):
    rows = x_ref.shape[0]
    first = (2 * s_ref[2] + part) * rows
    valid = (first + lax.broadcasted_iota(jnp.int32, (rows, 1), 0) < s_ref[3]).astype(f32)
    loss = jnp.zeros((8, PAIR), f32)
    chips = D // (2 * feats)
    for h in range(2):
        for k in range(chips):
            at = lanes_of(s_ref, h, k, feats)
            here = slice((h * chips + k) * feats, (h * chips + k + 1) * feats)
            y = x_ref[:, at].astype(f32) + valid * branch_ref[:, here].astype(f32)
            mismatch = y - teach_ref[:, at].astype(f32)
            square = jnp.sum((valid * mismatch * mismatch).reshape(rows // 8, 8, feats), 0)
            for q in range(feats // PAIR):
                loss = loss + square[:, q * PAIR : (q + 1) * PAIR]
            seed = valid * (cot_ref[:, at].astype(f32) + mismatch)
            result_ref[:, at] = y.astype(bf16)
            seed_ref[:, at] = seed
            low_ref[:, here] = seed.astype(bf16)
    loss_ref[...] = loss


def part_spec(rows, cols, part):
    return pl.BlockSpec((rows, cols), lambda i, s: (part, 0))


def aliased(kernel, name, in_specs, out_specs, out_shape, scalars, args, aliases):
    moved = sum(o.size * jnp.dtype(o.dtype).itemsize for o in out_shape)
    return pl.pallas_call(
        kernel,
        grid_spec=pltpu.PrefetchScalarGridSpec(
            num_scalar_prefetch=1, grid=(1,), in_specs=in_specs, out_specs=out_specs
        ),
        out_shape=out_shape,
        input_output_aliases=aliases,
        compiler_params=pltpu.CompilerParams(vmem_limit_bytes=24 << 20),
        cost_estimate=pl.CostEstimate(flops=0, transcendentals=0, bytes_accessed=3 * moved),
        name=name,
    )(scalars, *args)


def finish(scalars, part, branch, x, teacher, out_grad, old, feats):
    rows = branch.shape[0]
    mine = part_spec(rows, D, part)
    one = part_spec(rows, D, 0)
    aliases = {}
    if old is None:
        old = jnp.zeros((8, PAIR), bf16)
        old_spec = part_spec(8, PAIR, 0)
    else:
        old_spec = pl.BlockSpec(memory_space=pl.ANY)
        aliases = {5: 0}
    return aliased(
        functools.partial(finish_kernel, feats, part),
        "finish",
        [one, mine, mine, mine, old_spec],
        [mine, one, one, part_spec(8, PAIR, 0)],
        [
            shape_of((2 * rows, D), bf16),
            shape_of((rows, D), f32),
            shape_of((rows, D), bf16),
            shape_of((8, PAIR), f32),
        ],
        scalars,
        (branch, x, teacher, out_grad, old),
        aliases,
    )


def grad_acts_kernel(
    s_ref, seed_ref, gate_ref, up_ref, w0_ref, w1_ref, attn_ref, gu_ref, sum_ref
):
    hid = gate_ref.shape[1]
    width = attn_ref.shape[1]
    feats = w0_ref.shape[2]
    p, last_p = pl.program_id(0), pl.num_programs(0) - 1
    rows = seed_ref.shape[0]

    @pl.when(p == 0)
    def _():
        sum_ref[...] = jnp.zeros_like(sum_ref)

    def step(here):
        total = sum_ref[here, :]
        for h, w_ref in enumerate((w0_ref, w1_ref)):
            at = pl.ds(pl.multiple_of(h * D // 2 + p * feats, feats), feats)
            total = total + dot_nt(seed_ref[here, at], w_ref[0])
        sum_ref[here, :] = total

    over_rows(rows, SPAN, step)

    @pl.when(p == last_p)
    def _():
        def split(here):
            attn_ref[here, :] = sum_ref[here, :width].astype(bf16)
            grad = sum_ref[here, width:]
            gate, up = gate_ref[here, :], up_ref[here, :]
            sigmoid = jax.nn.sigmoid(gate)
            gu_ref[here, :hid] = (
                grad * up * sigmoid * (1.0 + gate * (1.0 - sigmoid))
            ).astype(bf16)
            gu_ref[here, hid:] = (grad * gate * sigmoid).astype(bf16)

        over_rows(rows, 64, split)


def grad_acts(scalars, seed, weights, gate, up):
    chips, deep, _ = weights[0].shape
    rows, hid = gate.shape
    width = deep - hid
    return call(
        grad_acts_kernel,
        "grad_acts",
        (chips,),
        [all_spec(rows, D), all_spec(rows, hid), all_spec(rows, hid)]
        + [shard_spec(w) for w in weights],
        [all_spec(rows, width), all_spec(rows, 2 * hid)],
        [shape_of((rows, width), bf16), shape_of((rows, 2 * hid), bf16)],
        scalars,
        (seed, gate, up, *weights),
        flops=2 * rows * D * deep,
        scratch=[pltpu.VMEM((rows, deep), f32)],
    )


def grad_normed_kernel(s_ref, qkv_ref, gu_ref, x_ref, stat_ref, *refs):
    w_refs, (out_ref, gain_ref, shift_ref) = refs[:4], refs[4:]
    feats = w_refs[0].shape[2]
    k = pl.program_id(0)
    rows = x_ref.shape[0]
    at = [shard_lanes(s_ref, k, feats, h * D // 2) for h in range(2)]
    for h in range(2):
        gain_ref[:, at[h]] = jnp.zeros((8, feats), f32)
        shift_ref[:, at[h]] = jnp.zeros((8, feats), f32)

    def step(here):
        mean, inv = stat_ref[here, 0:1], stat_ref[here, PAIR // 2 : PAIR // 2 + 1]
        for h in range(2):
            g = 0.0
            for a_ref, w_ref in ((qkv_ref, w_refs[h]), (gu_ref, w_refs[2 + h])):
                _, many, _, wide = w_ref.shape
                for j in range(many):
                    g = g + dot_nt(a_ref[here, j * wide : (j + 1) * wide], w_ref[0, j])
            out_ref[here, at[h]] = g.astype(bf16)
            lanes = lanes_of(s_ref, h, jnp.bitwise_xor(s_ref[1], k), feats)
            u = (x_ref[here, lanes].astype(f32) - mean) * inv
            gain_ref[:, at[h]] += jnp.sum((g * u).reshape(-1, 8, feats), 0)
            shift_ref[:, at[h]] += jnp.sum(g.reshape(-1, 8, feats), 0)

    over_rows(rows, SPAN, step)


def grad_normed(scalars, part, grad_qkv, grad_gu, w_qkv, w_gu, x, stats):
    chips, _, _, width = w_qkv[0].shape
    hid = w_gu[0].shape[3]
    rows = x.shape[0]
    weights = (*w_qkv, *w_gu)
    return call(
        grad_normed_kernel,
        "grad_normed",
        (chips,),
        [
            pl.BlockSpec((rows, 3 * width), lambda k, s: (part, 0)),
            all_spec(rows, 2 * hid),
            all_spec(rows, D),
            all_spec(rows, PAIR),
        ]
        + [shard_spec(w) for w in weights],
        [all_spec(rows, D), all_spec(8, D), all_spec(8, D)],
        [shape_of((rows, D), bf16), shape_of((8, D), f32), shape_of((8, D), f32)],
        scalars,
        (grad_qkv, grad_gu, x, stats, *weights),
        flops=2 * rows * D * (3 * width + 2 * hid),
    )


def last_kernel(feats, s_ref, sum_ref, x_ref, vec_ref, seed_ref, old_ref, out_ref):
    mean, inv = moments(x_ref[...].astype(f32))
    chips = D // (2 * feats)

    def units(h, k):
        here = slice((h * chips + k) * feats, (h * chips + k + 1) * feats)
        at = lanes_of(s_ref, h, k, feats)
        g = sum_ref[:, here].astype(f32) * vec_ref[0:1, at]
        return g, (x_ref[:, at].astype(f32) - mean) * inv, at

    m1 = m2 = 0.0
    for h in range(2):
        for k in range(chips):
            g, u, _ = units(h, k)
            m1 = m1 + jnp.sum(g, -1, keepdims=True)
            m2 = m2 + jnp.sum(g * u, -1, keepdims=True)
    m1, m2 = m1 / D, m2 / D
    for h in range(2):
        for k in range(chips):
            g, u, at = units(h, k)
            out_ref[:, at] = (seed_ref[:, at] + inv * (g - m1 - u * m2)).astype(bf16)


def last(scalars, part, total, x, vectors, seed, old, feats):
    rows = total.shape[0]
    mine = part_spec(rows, D, part)
    one = part_spec(rows, D, 0)
    aliases = {}
    if old is None:
        old = jnp.zeros((8, PAIR), bf16)
        old_spec = part_spec(8, PAIR, 0)
    else:
        old_spec = pl.BlockSpec(memory_space=pl.ANY)
        aliases = {5: 0}
    return aliased(
        functools.partial(last_kernel, feats),
        "last",
        [one, mine, part_spec(2, D, 0), one, old_spec],
        [mine],
        [shape_of((2 * rows, D), bf16)],
        scalars,
        (total, x, vectors, seed, old),
        aliases,
    )[0]


def per_device(
    chips,
    line,
    layer_input,
    teacher,
    out_grad,
    lengths,
    norm_gain,
    norm_bias,
    qkv_weight,
    qkv_bias,
    out_weight,
    gate_up_weight,
    down_weight,
):
    core = lax.axis_index("core")
    chip = lax.axis_index("chip")
    place = lax.axis_index("tp")
    scalars = jnp.stack([core, chip, place, lengths[0]]).astype(jnp.int32)
    feats = D // (2 * chips)
    width = qkv_weight.shape[2]
    hid = down_weight.shape[0]
    n = norm_gain.shape[0]
    cat = jnp.concatenate

    def to_chip(a, k):
        return lax.ppermute(a, "chip", [(c, c ^ k) for c in range(chips)])

    def near_shards(w):
        if chips != 4:
            every = lax.all_gather(w, "chip", axis=0, tiled=False)
            return [
                lax.dynamic_index_in_dim(every, chip ^ k, 0, keepdims=False)
                for k in range(1, chips)
            ]
        return [to_chip(w, 1), to_chip(w, 2)]

    def far_shard(near):
        if chips != 4:
            return []
        return [cat([to_chip(near[0][:1], 2), to_chip(near[1][1:], 1)], 0)]

    def both_cores(own):
        return [own, swap_core(own)]

    small = cat([norm_gain, norm_bias, qkv_bias.astype(f32).reshape(-1)])
    small = gather_axis(gather_axis(small, "core", 2), "chip", chips)
    small = small.reshape(2 * chips, -1)
    bias = small[:, 2 * n :].reshape(2 * chips, 3, -1)
    bias = bias.transpose(1, 0, 2).reshape(3, 1, width)
    vectors = gather_axis(small[:, : 2 * n], "tp", line)
    vectors = vectors.reshape(line, 2 * chips, 2, n).transpose(2, 1, 0, 3).reshape(2, D)

    rows = layer_input.shape[0]
    span = rows // 2
    tables = rotary_tables(line)

    def along_line(a):
        return lax.all_gather(a, "tp", axis=0, tiled=True)

    def summed_line(a):
        return lax.psum_scatter(a, "tp", scatter_dimension=0, tiled=True)

    slot = along_line(layer_input)
    w_od = lax.all_gather(cat([out_weight, down_weight], 0), "chip", axis=0, tiled=False)
    shard = after(gate_up_weight, small)
    near = near_shards(shard)
    slot = after(slot, *near)
    qkv_shard = after(qkv_weight, vectors, *near)
    w_gu = both_cores(jnp.stack([shard, *near, *far_shard(near)]))
    near = near_shards(qkv_shard) + ([to_chip(qkv_shard, 3)] if chips == 4 else [])
    w_qkv = both_cores(jnp.stack([qkv_shard, *near]))
    normed, stats, x, qkv = [None] * 2, [None] * 2, [None] * 2, [None] * 2
    for t in range(2):
        *normed[t], stats[t], x[t] = norm(scalars, t, span, slot, vectors, feats)
    for t in range(2):
        qkv[t] = joined_heads(scalars, normed[t], w_qkv, bias, tables[t])
    gate, up, acts = [None] * 2, [None] * 2, [None] * 2
    attn, lse, branch = [None] * 2, [None] * 2, [None] * 2
    attn[0], lse[0] = attend(0, span, qkv)
    w_od = both_cores(after(w_od, attn[0]))
    gate[0], up[0], acts[0] = gate_up(scalars, normed[0], attn[0], w_gu)
    branch[0] = branch_sums(scalars, acts[0], w_od)
    qkv[1] = after(qkv[1], branch[0])
    attn[1], lse[1] = attend(1, span, qkv)
    gate[1], up[1], acts[1] = gate_up(scalars, normed[1], attn[1], w_gu)
    branch[1] = branch_sums(scalars, acts[1], w_od)
    seeds, seed_all, losses = [None] * 2, [None] * 2, [None] * 2
    result = None
    for t in range(2):
        total = summed_line(branch[t])
        result, seeds[t], low, loss = finish(
            scalars, t, total, layer_input, teacher, out_grad, result, feats
        )
        losses[t] = jnp.sum(loss)
        seed_all[t] = along_line(low)

    half = D // 2

    def seed_half(t, h):
        return seed_all[t][:, h * half : (h + 1) * half]

    def od_part(t, h, *hold):
        return dot_tn(after(acts[t], *hold), seed_half(t, h))

    def with_other(mine, theirs):
        return (mine + theirs.astype(f32)).astype(bf16)

    def scattered(a, axis):
        return lax.psum_scatter(a, "chip", scatter_dimension=axis, tiled=True).astype(f32)

    def rows_of(a, k):
        return lax.dynamic_slice_in_dim(a, (chip ^ k) * feats, feats, 0)

    def sent_rows(a, some):
        return [to_chip(rows_of(a, k), k) for k in some]

    def gu_part(t, h, hold):
        return dot_tn(normed[t][h], after(grad_gu[t], hold))

    grad_attn, grad_gu = [None] * 2, [None] * 2
    grad_attn[0], grad_gu[0] = grad_acts(scalars, seed_all[0], w_od, gate[0], up[0])
    kept = attend_back(0, span, qkv, grad_attn[0], lse[0], tables)
    od_early = [od_part(0, h, kept[0]) for h in range(2)]
    gu_early = [gu_part(0, h, kept[0]) for h in range(2)]

    seed_all[1] = after(seed_all[1], *od_early, *gu_early)
    od_sent = (od_early[1] + od_part(1, 1)).astype(bf16)
    od_theirs = swap_core(od_sent)
    seed_all[1] = after(seed_all[1], od_sent)
    grad_attn[1], grad_gu[1] = grad_acts(scalars, seed_all[1], w_od, gate[1], up[1])
    od_sum = with_other(od_early[0] + od_part(1, 0, grad_gu[1]), od_theirs)
    od_grad = scattered(od_sum, 1)
    gu_sent = (gu_early[1] + gu_part(1, 1, od_sum)).astype(bf16)
    gu_theirs = swap_core(gu_sent)
    grad_qkv, grad_bias = attend_back(
        1, span, qkv, after(grad_attn[1], gu_sent), lse[1], tables, kept
    )
    gu_sum = with_other(gu_early[0] + gu_part(1, 0, grad_qkv), gu_theirs)
    normed_all = [cat([normed[0][h], normed[1][h]], 0) for h in range(2)]
    grads, gains, shifts, sums = [None] * 2, [None] * 2, [None] * 2, [None] * 2

    def back(t, hold):
        grads[t], gain, shift = grad_normed(
            scalars, t, after(grad_qkv, hold), grad_gu[t], w_qkv, w_gu, x[t], stats[t]
        )
        gains[t], shifts[t] = jnp.sum(gain, 0), jnp.sum(shift, 0)
        sums[t] = summed_line(grads[t])

    back(0, gu_sum)
    gu_got = sent_rows(gu_sum, (1, 2))
    qkv_held = after(grad_qkv, grads[0], *gu_got)
    qkv_sent = dot_tn(normed_all[1], qkv_held).astype(bf16)
    qkv_theirs = swap_core(qkv_sent)
    gu_got += sent_rows(after(gu_sum, *gu_got), range(3, chips))
    back(1, qkv_sent)
    qkv_held = after(qkv_held, grads[1], *gu_got)
    qkv_sum = with_other(dot_tn(normed_all[0], qkv_held), qkv_theirs)
    qkv_got = sent_rows(qkv_sum, range(1, chips))
    gu_grad = rows_of(gu_sum, 0).astype(f32) + sum(g.astype(f32) for g in gu_got)
    qkv_grad = rows_of(qkv_sum, 0).astype(f32) + sum(g.astype(f32) for g in qkv_got)
    input_grad = None
    for t in range(2):
        input_grad = last(
            scalars, t, sums[t], layer_input, vectors, seeds[t], input_grad, feats
        )
    gains = [(gains[0] + gains[1])[h * half : (h + 1) * half] for h in range(2)]
    shifts = [(shifts[0] + shifts[1])[h * half : (h + 1) * half] for h in range(2)]

    count = jnp.clip(lengths[0] - place * rows, 0, rows)
    scalar_sums = jnp.stack([losses[0] + losses[1], count.astype(f32)])
    scalar_sums = jnp.broadcast_to(scalar_sums, (chips, line, 2))
    heads = jnp.sum(grad_bias, 0).reshape(3, chips, 2, -1).transpose(2, 1, 0, 3)
    heads = [jnp.where(core == h, heads[0], heads[1]) for h in range(2)]
    small_sums = []
    for h in range(2):
        vector = jnp.stack([gains[h], shifts[h]]).reshape(2, chips, line, n)
        vector = cat([vector.transpose(1, 2, 0, 3).reshape(chips, line, 2 * n), scalar_sums], -1)
        small_sums.append(cat([vector.reshape(chips, -1), heads[h].reshape(chips, -1)], -1))
    small_sums = [after(v, qkv_grad) for v in small_sums]
    total = scatter_axis(small_sums[0] + swap_core(small_sums[1]), "chip", chips)
    cut = line * (2 * n + 2)
    qkv_b_grad = total[cut:].reshape(3, -1)
    total = scatter_axis(total[:cut].reshape(line, -1), "tp", line)
    gain_grad, bias_grad = total[:n], total[n : 2 * n]
    loss_value = total[2 * n] / (total[2 * n + 1] * D)
    return (
        result,
        loss_value,
        input_grad,
        gain_grad,
        bias_grad,
        jnp.stack([qkv_grad[:, j * width : (j + 1) * width] for j in range(3)]),
        qkv_b_grad,
        od_grad[:width],
        jnp.stack([gu_grad[:, j * hid : (j + 1) * hid] for j in range(2)]),
        od_grad[width:],
    )


def solution(mesh):
    chips, line = mesh.shape["fsdp"] // 2, mesh.shape["tp"]
    fine = Mesh(mesh.devices.reshape(chips, 2, line), ("chip", "core", "tp"))
    fsdp = ("chip", "core")
    tokens = P(fsdp + ("tp",), None)
    vector = P(fsdp + ("tp",))
    return jax.shard_map(
        functools.partial(per_device, chips, line),
        mesh=fine,
        in_specs=(
            tokens,
            tokens,
            tokens,
            P(fsdp),
            vector,
            vector,
            P(None, fsdp, "tp"),
            P(None, ("tp",) + fsdp),
            P("tp", fsdp),
            P(None, fsdp, "tp"),
            P("tp", fsdp),
        ),
        out_specs=(
            tokens,
            P(),
            tokens,
            vector,
            vector,
            P(None, fsdp, "tp"),
            P(None, ("tp",) + fsdp),
            P("tp", fsdp),
            P(None, fsdp, "tp"),
            P("tp", fsdp),
        ),
        check_vma=False,
    )
```

time: 714 us -> 619 us (0.87)
  Pallas kernels: 45.4 us -> 157 us
  matrix products: 166 us -> 70.9 us
  starting transfers between devices: 116 us -> 32.1 us
  other arithmetic: 57.7 us -> 20.3 us
  waiting for transfers between devices: 213 us -> 228 us
    pallas_call x2 -> x20, Pallas kernels: 45.4 us -> 157 us  [the longest x12 108 us: call(): pl.pallas_call(kernel, grid_spec=pltpu.PrefetchScalarGridSpec(num_scalar_...]
    dot_general x24 -> x10, matrix products: 166 us -> 70.9 us  [dot_tn(): lax.dot_general(a, b, (((0,), (0,)), ((), ())), preferred_element_type=f32)]
    ppermute x48 -> x13, starting transfers between devices: 102 us -> 17.1 us  [to_chip(): return lax.ppermute(a, 'chip', [(c, c ^ k) for c in range(chips)])]
    reduce_scatter x4 -> x5, waiting for transfers between devices: 0.01 us -> 48.5 us  [the longest x4 48.5 us: summed_line(): return lax.psum_scatter(a, 'tp', scatter_dimension=0, tiled=True)]
    unnamed x124 -> x202, local copies, waits for them, and re-layouts: 28.1 us -> 60.8 us
    convert_element_type x17 -> x0, other arithmetic: 31.2 us -> none  [the longest x12 24.6 us: line_scatter(): val.astype(bf16)]
    dynamic_update_slice x27 -> x0, local copies, waits for them, and re-layouts: 23.9 us -> none  [the longest x12 11.8 us: line_gather(): lax.dynamic_update_slice_in_dim(out, ups[s], jnp.maximum(me - 1 - s, 0) *...]
    all_gather x4, waiting for transfers between devices: 58.8 us -> 42.4 us  [the longest x3 42.4 us: along_line(): return lax.all_gather(a, 'tp', axis=0, tiled=True)]
  transfers between devices with their start and end apart: 74 -> 38, of which waited for: 28 -> 23; matrix products, arithmetic and copies ran while one was open for 41% -> 14% of each run, Pallas kernels for 6% -> 24%
where the time goes in v2:
time: 619 us; the launch traced here: 610 us
  waiting for transfers between devices  228 us (37%)
  Pallas kernels  157 us (25%)
  local copies, waits for them, and re-layouts  81.6 us (13%)
  matrix products  70.9 us (11%)
  starting transfers between devices  32.1 us (5%)
  other arithmetic  20.3 us (3%)
  between operations  19.7 us (3%)
    ppermute x13, waiting for transfers between devices, to_chip(): return lax.ppermute(a, 'chip', [(c, c ^ k) for c in range(chips)])  120 us
    pallas_call x12, Pallas kernels, call(): pl.pallas_call(kernel, grid_spec=pltpu.PrefetchScalarGridSpec(num_scalar_...  108 us
    dot_general x10, matrix products, dot_tn(): lax.dot_general(a, b, (((0,), (0,)), ((), ())), preferred_element_type=f32)  70.9 us
    unnamed x202, local copies, waits for them, and re-layouts  60.8 us
    reduce_scatter x4, waiting for transfers between devices, summed_line(): return lax.psum_scatter(a, 'tp', scatter_dimension=0, tiled=True)  48.5 us
    all_gather x3, waiting for transfers between devices, along_line(): return lax.all_gather(a, 'tp', axis=0, tiled=True)  42.4 us
    pallas_call x2, Pallas kernels, attend_back(): pl.pallas_call(functools.partial(attend_back_kernel, part, span), grid=(p...  23.1 us
    ppermute x13, starting transfers between devices, to_chip(): return lax.ppermute(a, 'chip', [(c, c ^ k) for c in range(chips)])  17.1 us
  transfers between devices with their start and end apart: 38, of which 23 were waited for; matrix products, arithmetic and copies ran while one was open for 14% of the time, Pallas kernels for 24%

profile of v2, /device:TPU:0, one launch (start us, length us, event | category | flops | bytes accessed | tf_op | source)
XLA Modules:
  0.0 609.6 jit_solution(16764051514750786230)
XLA Ops:
  10.8 2.9 collective-permute-start.1
  15.2 2.1 collective-permute-start.2
  19.0 2.1 collective-permute-start.4
  22.6 2.2 pad_maximum_fusion.4
  26.5 4.4 collective-permute-done.5
  31.2 4.5 collective-permute-done.6
  36.0 15.0 %collective-permute-done.4 = bf16[2,256,1408]{2,1,0:T(8,128)(2,1)S(1)} collective-permute-done((bf16[2,256,1408]{2,1,0:T(8,128)(2,1)}, bf16[2,256,1408]{2,1,0:T(8,128)(2,1)S(1)}, u32[]{:S(2)}, u32[]{:S(2)}) %collective-permute-start.4) | collective-permute-done | bytes 1441824 | tf_op jit(solution)/shard_map/ppermute | solution.py:768
  58.1 16.1 %collective-permute-done.9 = bf16[3,256,512]{2,1,0:T(8,128)(2,1)S(1)} collective-permute-done((bf16[3,256,512]{2,1,0:T(8,128)(2,1)}, bf16[3,256,512]{2,1,0:T(8,128)(2,1)S(1)}, u32[]{:S(2)}, u32[]{:S(2)}) %collective-permute-start.9) | collective-permute-done | bytes 786464 | tf_op jit(solution)/shard_map/ppermute | solution.py:768
  74.3 12.4 %collective-permute-done.8 = bf16[3,256,512]{2,1,0:T(8,128)(2,1)S(1)} collective-permute-done((bf16[3,256,512]{2,1,0:T(8,128)(2,1)}, bf16[3,256,512]{2,1,0:T(8,128)(2,1)S(1)}, u32[]{:S(2)}, u32[]{:S(2)}) %collective-permute-start.8) | collective-permute-done | bytes 786464 | tf_op jit(solution)/shard_map/ppermute | solution.py:768
  86.7 3.1 collective-permute-done.7
  90.3 11.3 %collective-permute-done.12 = bf16[1,256,1408]{2,1,0:T(8,128)(2,1)S(1)} collective-permute-done((bf16[1,256,1408]{2,1,0:T(8,128)(2,1)S(1)}, bf16[1,256,1408]{2,1,0:T(8,128)(2,1)S(1)}, u32[]{:S(2)}, u32[]{:S(2)}) %collective-permute-start.12) | collective-permute-done | bytes 720928 | tf_op jit(solution)/shard_map/ppermute | solution.py:768
  102.2 3.2 pad_maximum_fusion.w0_ref.refs_2_
  109.6 2.0 maximum_bitcast_fusion.2
  113.6 2.2 copy-done.1
  115.8 2.7 norm.3
  120.6 2.7 norm.2
  124.7 8.9 %joined.3.q_ref.k0_ref.v0_ref = bf16[3,512,512]{2,1,0:T(8,128)(2,1)S(1)} custom-call(s32[4]{0:T(128)S(1)} %pad_add_fusion.s_ref, bf16[512,1024]{1,0:T(8,128)(2,1)S(1)} %get-tuple-element.78.own_ref, bf16[512,1024]{1,0:T(8,128)(2,1)S(1)} %get-tuple-element.79.other_ref, f32[3,1,512]{2,1,0:T(1,128)S(1)} %reshape.135.bias_ref, f32[3,512,128]{2,1,0:T(8,128)S(1)} %bitcast.79, ...), custom_call_target="tpu_custom_call" | custom-call | flops 3221225472 | bytes 10754048 | tf_op jit(solution)/shard_map/joined/pallas_call | solution.py:293
  133.7 8.4 %joined.2.k1_ref.v1_ref.q_ref = bf16[3,512,512]{2,1,0:T(8,128)(2,1)S(1)} custom-call(s32[4]{0:T(128)S(1)} %pad_add_fusion.s_ref, bf16[512,1024]{1,0:T(8,128)(2,1)S(1)} %get-tuple-element.75.own_ref, bf16[512,1024]{1,0:T(8,128)(2,1)S(1)} %get-tuple-element.76.other_ref, f32[3,1,512]{2,1,0:T(1,128)S(1)} %reshape.135.bias_ref, f32[3,512,128]{2,1,0:T(8,128)S(1)} %bitcast.82, ...), custom_call_target="tpu_custom_call" | custom-call | flops 3221225472 | bytes 10754048 | tf_op jit(solution)/shard_map/joined/pallas_call | solution.py:293
  142.1 8.1 %attend.2 = (bf16[512,512]{1,0:T(8,128)(2,1)S(1)}, f32[4,4,256]{2,1,0:T(4,128)S(1)}) custom-call(bf16[3,512,512]{2,1,0:T(8,128)(2,1)S(1)} %joined.3.q_ref.k0_ref.v0_ref, bf16[3,512,512]{2,1,0:T(8,128)(2,1)S(1)} %joined.3.q_ref.k0_ref.v0_ref, bf16[3,512,512]{2,1,0:T(8,128)(2,1)S(1)} %joined.3.q_ref.k0_ref.v0_ref, ...), custom_call_target="tpu_custom_call" | custom-call | flops 2147483648 | bytes 5242880 | tf_op jit(solution)/shard_map/attend/pallas_call | solution.py:179
  151.9 11.5 %gate_up.2 = (f32[512,1408]{1,0:T(8,128)S(1)}, f32[512,1408]{1,0:T(8,128)S(1)}, bf16[512,1920]{1,0:T(8,128)(2,1)S(1)}) custom-call(s32[4]{0:T(128)S(1)} %pad_add_fusion.s_ref, bf16[512,1024]{1,0:T(8,128)(2,1)S(1)} %copy-done.54, bf16[512,1024]{1,0:T(8,128)(2,1)S(1)} %copy-done.62, bf16[512,512]{1,0:T(8,128)(2,1)S(1)} %get-tuple-element.80.attn_ref, ...), custom_call_target="tpu_custom_call" | custom-call | flops 5905580032 | bytes 21889024 | tf_op jit(solution)/shard_map/gate_up/pallas_call | solution.py:293
  166.7 7.7 %branch.2 = bf16[512,2048]{1,0:T(8,128)(2,1)} custom-call(s32[4]{0:T(128)S(1)} %pad_add_fusion.s_ref, bf16[512,1920]{1,0:T(8,128)(2,1)S(1)} %get-tuple-element.95.acts_ref, bf16[4,1920,256]{2,1,0:T(8,128)(2,1)S(1)} %bitcast.75, bf16[4,1920,256]{2,1,0:T(8,128)(2,1)S(1)} %collective-permute-done.14.w1_ref), custom_call_target="tpu_custom_call" | custom-call | flops 4026531840 | bytes 11927552 | tf_op jit(solution)/shard_map/branch/pallas_call | solution.py:293
  174.4 1.9 copy-done.6
  181.0 8.9 %attend.3 = (bf16[512,512]{1,0:T(8,128)(2,1)S(1)}, f32[4,4,256]{2,1,0:T(4,128)S(1)}) custom-call(bf16[3,512,512]{2,1,0:T(8,128)(2,1)S(1)} %copy-done.76, bf16[3,512,512]{2,1,0:T(8,128)(2,1)S(1)} %copy-done.72, bf16[3,512,512]{2,1,0:T(8,128)(2,1)S(1)} %copy-done.72, bf16[3,512,512]{2,1,0:T(8,128)(2,1)S(1)} %copy-done.76, bf16[3,512,512]{2,1,0:T(8,128)(2,1)S(1)} %copy-done.76), custom_call_target="tpu_custom_call" | custom-call | flops 2147483648 | bytes 5242880 | tf_op jit(solution)/shard_map/attend/pallas_call | solution.py:179
  190.0 11.7 %gate_up.3 = (f32[512,1408]{1,0:T(8,128)S(1)}, f32[512,1408]{1,0:T(8,128)S(1)}, bf16[512,1920]{1,0:T(8,128)(2,1)S(1)}) custom-call(s32[4]{0:T(128)S(1)} %pad_add_fusion.s_ref, bf16[512,1024]{1,0:T(8,128)(2,1)S(1)} %copy-done.58, bf16[512,1024]{1,0:T(8,128)(2,1)S(1)} %copy-done.66, bf16[512,512]{1,0:T(8,128)(2,1)S(1)} %get-tuple-element.84.attn_ref, ...), custom_call_target="tpu_custom_call" | custom-call | flops 5905580032 | bytes 21889024 | tf_op jit(solution)/shard_map/gate_up/pallas_call | solution.py:293
  204.9 6.4 %branch.3 = bf16[512,2048]{1,0:T(8,128)(2,1)S(1)} custom-call(s32[4]{0:T(128)S(1)} %pad_add_fusion.s_ref, bf16[512,1920]{1,0:T(8,128)(2,1)S(1)} %get-tuple-element.104.acts_ref, bf16[4,1920,256]{2,1,0:T(8,128)(2,1)S(1)} %bitcast.76, bf16[4,1920,256]{2,1,0:T(8,128)(2,1)S(1)} %copy-done.7), custom_call_target="tpu_custom_call" | custom-call | flops 4026531840 | bytes 11927552 | tf_op jit(solution)/shard_map/branch/pallas_call | solution.py:293
  214.2 7.9 %reduce-scatter.8.cloned.1.call-done.branch_ref = bf16[128,2048]{1,0:T(8,128)(2,1)} async-done(((bf16[512,2048]{1,0:T(8,128)(2,1)}), bf16[128,2048]{1,0:T(8,128)(2,1)}) %reduce-scatter.8.cloned.1.call-update) | async-done | bytes 524304 | tf_op jit(solution)/shard_map/reduce_scatter | solution.py:803
  223.2 1.9 finish.2
  227.0 40.5 %reduce-scatter.6.cloned.1.call-done.branch_ref = bf16[128,2048]{1,0:T(8,128)(2,1)} async-done(((bf16[512,2048]{1,0:T(8,128)(2,1)}), bf16[128,2048]{1,0:T(8,128)(2,1)}) %reduce-scatter.6.cloned.1.call-update) | async-done | bytes 524304 | tf_op jit(solution)/shard_map/reduce_scatter | solution.py:803
  268.6 1.9 finish.3
  272.4 42.4 %all-gather.10.cloned.1.call-done.seed_ref = bf16[512,2048]{1,0:T(8,128)(2,1)} async-done(((bf16[128,2048]{1,0:T(8,128)(2,1)}), bf16[512,2048]{1,0:T(8,128)(2,1)}) %all-gather.10.cloned.1.call-update) | async-done | bytes 2097168 | tf_op jit(solution)/shard_map/all_gather | solution.py:800
  314.9 2.1 copy-done.4
  317.0 2.1 copy-done.8
  320.9 2.0 copy-done.23
  324.5 8.1 %grad_acts.2 = (bf16[512,512]{1,0:T(8,128)(2,1)S(1)}, bf16[512,2816]{1,0:T(8,128)(2,1)S(1)}) custom-call(s32[4]{0:T(128)S(1)} %pad_add_fusion.s_ref, bf16[512,2048]{1,0:T(8,128)(2,1)S(1)} %copy-done.24, f32[512,1408]{1,0:T(8,128)S(1)} %copy-done.21, f32[512,1408]{1,0:T(8,128)S(1)} %copy-done.23, bf16[4,1920,256]{2,1,0:T(8,128)(2,1)S(1)} %bitcast.77, ...), custom_call_target="tpu_custom_call" | custom-call | flops 4026531840 | bytes 19136512 | tf_op jit(solution)/shard_map/grad_acts/pallas_call | solution.py:293
  332.7 10.1 %attend_back.2 = (f32[512,512]{1,0:T(8,128)S(1)}, f32[512,512]{1,0:T(8,128)S(1)}, f32[512,512]{1,0:T(8,128)S(1)}, f32[512,512]{1,0:T(8,128)S(1)}, f32[512,512]{1,0:T(8,128)S(1)}) custom-call(bf16[3,512,512]{2,1,0:T(8,128)(2,1)S(1)} %copy-done.73, bf16[3,512,512]{2,1,0:T(8,128)(2,1)S(1)} %copy-done.73, bf16[3,512,512]{2,1,0:T(8,128)(2,1)S(1)} %copy-done.73, ...), custom_call_target="tpu_custom_call" | custom-call | flops 5368709120 | bytes 10485760 | tf_op jit(solution)/shard_map/attend_back/pallas_call | solution.py:271
  342.9 5.3 fusion.6
  348.2 5.3 fusion.8
  353.5 5.9 fusion.24
  359.4 6.1 %fusion.23 = f32[1024,2816]{1,0:T(8,128)} fusion(bf16[512,1024]{1,0:T(8,128)(2,1)S(1)} %copy-done.55, bf16[512,2816]{1,0:T(8,128)(2,1)S(1)} %get-tuple-element.97.gu_ref), kind=kOutput, calls=%fused_computation.94 | convolution fusion | flops 2952790016 | bytes 15466496 | tf_op jit(solution)/shard_map/dot_general | solution.py:117
  365.7 5.9 add_convert_fusion.3
  373.7 8.4 %grad_acts.3 = (bf16[512,512]{1,0:T(8,128)(2,1)S(1)}, bf16[512,2816]{1,0:T(8,128)(2,1)S(1)}) custom-call(s32[4]{0:T(128)S(1)} %pad_add_fusion.s_ref, bf16[512,2048]{1,0:T(8,128)(2,1)S(1)} %copy-done.10, f32[512,1408]{1,0:T(8,128)S(1)} %copy-done.17, f32[512,1408]{1,0:T(8,128)S(1)} %copy-done.19, bf16[4,1920,256]{2,1,0:T(8,128)(2,1)S(1)} %bitcast.78, ...), custom_call_target="tpu_custom_call" | custom-call | flops 4026531840 | bytes 19136512 | tf_op jit(solution)/shard_map/grad_acts/pallas_call | solution.py:293
  384.6 7.8 %add_convert_fusion.2 = bf16[1920,1024]{1,0:T(8,128)(2,1)} fusion(bf16[1920,1024]{1,0:T(8,128)(2,1)S(1)} %collective-permute-done.15, f32[1920,1024]{1,0:T(8,128)} %fusion.8, bf16[512,1920]{1,0:T(8,128)(2,1)S(1)} %copy-done.27, bf16[512,2048]{1,0:T(8,128)(2,1)S(1)} %copy-done.10), kind=kOutput, calls=%fused_computation.2 | convolution fusion | flops 2021130240 | bytes 18743296 | tf_op jit(solution)/shard_map/dot_general | solution.py:117
  392.3 11.2 %add_convert_fusion.1 = bf16[1024,2816]{1,0:T(8,128)(2,1)} fusion(f32[1024,2816]{1,0:T(8,128)} %fusion.24, bf16[512,1024]{1,0:T(8,128)(2,1)} %copy-done.65, bf16[512,2816]{1,0:T(8,128)(2,1)} %copy-done.44), kind=kOutput, calls=%fused_computation.1 | convolution fusion | flops 2958557184 | bytes 21233664 | tf_op jit(solution)/shard_map/dot_general | solution.py:117
  415.0 13.0 %attend_back.3 = (bf16[1024,1536]{1,0:T(8,128)(2,1)S(1)}, f32[8,1536]{1,0:T(8,128)S(1)}) custom-call(bf16[3,512,512]{2,1,0:T(8,128)(2,1)S(1)} %copy-done.78, bf16[3,512,512]{2,1,0:T(8,128)(2,1)S(1)} %copy-done.74, bf16[3,512,512]{2,1,0:T(8,128)(2,1)S(1)} %copy-done.74, bf16[3,512,512]{2,1,0:T(8,128)(2,1)S(1)} %copy-done.78, ...), custom_call_target="tpu_custom_call" | custom-call | flops 5368709120 | bytes 10485760 | tf_op jit(solution)/shard_map/attend_back/pallas_call | solution.py:271
  428.1 10.7 %add_convert_fusion = bf16[1024,2816]{1,0:T(8,128)(2,1)} fusion(bf16[1024,2816]{1,0:T(8,128)(2,1)} %collective-permute-done.16, f32[1024,2816]{1,0:T(8,128)} %fusion.23, bf16[512,1024]{1,0:T(8,128)(2,1)S(1)} %copy-done.59, bf16[512,2816]{1,0:T(8,128)(2,1)S(1)} %copy-done.45), kind=kOutput, calls=%fused_computation | convolution fusion | flops 2964324352 | bytes 27000832 | tf_op jit(solution)/shard_map/dot_general | solution.py:117
  438.8 3.8 constant_dynamic-slice_fusion.4
  445.8 15.5 %grad_normed.2 = (bf16[512,2048]{1,0:T(8,128)(2,1)}, f32[8,2048]{1,0:T(8,128)S(1)}, f32[8,2048]{1,0:T(8,128)S(1)}) custom-call(s32[4]{0:T(128)S(1)} %pad_add_fusion.s_ref, bf16[1024,1536]{1,0:T(8,128)(2,1)S(1)} %get-tuple-element.131.qkv_ref, bf16[512,2816]{1,0:T(8,128)(2,1)S(1)} %copy-done.48, bf16[512,2048]{1,0:T(8,128)(2,1)S(1)} %copy-done.52, ...), custom_call_target="tpu_custom_call" | custom-call | flops 9126805504 | bytes 28442624 | tf_op jit(solution)/shard_map/grad_normed/pallas_call | solution.py:293
  461.4 21.0 %collective-permute-done.18 = bf16[256,2816]{1,0:T(8,128)(2,1)} collective-permute-done((bf16[256,2816]{1,0:T(8,128)(2,1)}, bf16[256,2816]{1,0:T(8,128)(2,1)}, u32[]{:S(2)}, u32[]{:S(2)}) %collective-permute-start.18) | collective-permute-done | bytes 1441824 | tf_op jit(solution)/shard_map/ppermute | solution.py:768
  482.4 7.4 %convolution_convert_fusion = bf16[1024,1536]{1,0:T(8,128)(2,1)} fusion(bf16[1024,1536]{1,0:T(8,128)(2,1)} %copy-done.81, bf16[512,1024]{1,0:T(8,128)(2,1)} %copy-done.65, bf16[512,1024]{1,0:T(8,128)(2,1)S(1)} %copy-done.64), kind=kOutput, calls=%fused_computation.6 | convolution fusion | flops 3226992640 | bytes 8388608 | tf_op jit(solution)/shard_map/dot_general | solution.py:117
  492.7 2.7 constant_dynamic-slice_fusion.3
  496.9 1.9 copy-done.15
  500.4 1.9 copy-done.82
  502.3 15.8 %grad_normed.3 = (bf16[512,2048]{1,0:T(8,128)(2,1)}, f32[8,2048]{1,0:T(8,128)S(1)}, f32[8,2048]{1,0:T(8,128)S(1)}) custom-call(s32[4]{0:T(128)S(1)} %pad_add_fusion.s_ref, bf16[1024,1536]{1,0:T(8,128)(2,1)S(1)} %copy-done.82, bf16[512,2816]{1,0:T(8,128)(2,1)S(1)} %copy-done.46, bf16[512,2048]{1,0:T(8,128)(2,1)S(1)} %copy-done.50, ...), custom_call_target="tpu_custom_call" | custom-call | flops 9126805504 | bytes 28442624 | tf_op jit(solution)/shard_map/grad_normed/pallas_call | solution.py:293
  519.1 1.9 slice.213
  521.1 2.3 slice.216
  523.4 7.2 %collective-permute-done.19 = bf16[256,2816]{1,0:T(8,128)(2,1)} collective-permute-done((bf16[256,2816]{1,0:T(8,128)(2,1)}, bf16[256,2816]{1,0:T(8,128)(2,1)}, u32[]{:S(2)}, u32[]{:S(2)}) %collective-permute-start.19) | collective-permute-done | bytes 1441824 | tf_op jit(solution)/shard_map/ppermute | solution.py:768
  530.7 5.2 add_convert_fusion.4
  539.6 3.4 add_add_fusion
  543.0 13.6 %collective-permute-done.21 = bf16[256,1536]{1,0:T(8,128)(2,1)S(1)} collective-permute-done((bf16[256,1536]{1,0:T(8,128)(2,1)S(1)}, bf16[256,1536]{1,0:T(8,128)(2,1)S(1)}, u32[]{:S(2)}, u32[]{:S(2)}) %collective-permute-start.21) | collective-permute-done | bytes 786464 | tf_op jit(solution)/shard_map/ppermute | solution.py:768
  556.6 16.6 %collective-permute-done.23 = bf16[256,1536]{1,0:T(8,128)(2,1)S(1)} collective-permute-done((bf16[256,1536]{1,0:T(8,128)(2,1)S(1)}, bf16[256,1536]{1,0:T(8,128)(2,1)S(1)}, u32[]{:S(2)}, u32[]{:S(2)}) %collective-permute-start.23) | collective-permute-done | bytes 786464 | tf_op jit(solution)/shard_map/ppermute | solution.py:768
  580.7 2.5 last.2.old_ref
  587.0 2.5 collective-permute-start.27
  589.5 2.3 pad_maximum_fusion.3
  599.1 2.5 last.3
  (354 shorter events, 98.5 us)
Async XLA Ops:
  7.2 106.4 %all-gather.6.cloned.1.call-start = ((), (), s32[]{:S(2)}) async-start(), calls=%async_computation.5 | async-start | bytes 5242880 | tf_op jit(solution)/shard_map/all_gather | solution.py:800
  7.9 143.5 %all-gather.12.cloned.1.call-start = ((), (), s32[]{:S(2)}) async-start(), calls=%async_computation.13 | async-start | bytes 4915200 | tf_op jit(solution)/shard_map/all_gather | solution.py:806
  9.5 1.3 collective-permute-start
  10.8 4.5 collective-permute-start.1
  15.2 3.7 collective-permute-start.2
  19.0 31.9 %collective-permute-start.4 = (bf16[2,256,1408]{2,1,0:T(8,128)(2,1)}, bf16[2,256,1408]{2,1,0:T(8,128)(2,1)S(1)}, u32[]{:S(2)}, u32[]{:S(2)}) collective-permute-start(bf16[2,256,1408]{2,1,0:T(8,128)(2,1)} %param.20), channel_id=1, source_target_pairs={{0,16},{8,24},{16,0},{24,8},{1,17},{9,25},{17,1},{25,9},{2,18},{10... | collective-permute-start | bytes 4325384 | tf_op jit(solution)/shard_map/ppermute | solution.py:768
  21.1 31.6 %collective-permute-start.3 = (bf16[2,256,1408]{2,1,0:T(8,128)(2,1)}, bf16[2,256,1408]{2,1,0:T(8,128)(2,1)S(1)}, u32[]{:S(2)}, u32[]{:S(2)}) collective-permute-start(bf16[2,256,1408]{2,1,0:T(8,128)(2,1)} %param.20), channel_id=1, source_target_pairs={{0,8},{8,0},{16,24},{24,16},{1,9},{9,1},{17,25},{25,17},{2,10},{10... | collective-permute-start | bytes 4325384 | tf_op jit(solution)/shard_map/ppermute | solution.py:768
  24.8 197.3 %reduce-scatter.8.cloned.1.call-start = ((), (), s32[]{:S(2)}) async-start(), calls=%async_computation.7 | async-start | bytes 2621440 | tf_op jit(solution)/shard_map/reduce_scatter | solution.py:803
  24.9 6.1 %collective-permute-start.5 = (f32[1,8,128]{2,1,0:T(8,128)S(1)}, f32[1,8,128]{2,1,0:T(8,128)S(1)}, u32[]{:S(2)}, u32[]{:S(2)}) collective-permute-start(f32[1,8,128]{2,1,0:T(8,128)S(1)} %slice_bitcast_fusion.5), channel_id=1, source_target_pairs={{0,1},{1,0},{2,3},{3,2},{4,5},{5,4},{6,7},{7,6},{8,9},{9,8},{10,11... | collective-permute-start | bytes 12296 | tf_op jit(solution)/shard_map/ppermute | solution.py:35
  31.0 4.7 collective-permute-start.6
  36.0 53.8 %copy-start.100 = (bf16[3,256,512]{2,1,0:T(8,128)(2,1)S(1)}, bf16[3,256,512]{2,1,0:T(8,128)(2,1)}, u32[]{:S(2)}) copy-start(bf16[3,256,512]{2,1,0:T(8,128)(2,1)} %param.17) | copy-start | bytes 2359300
  50.9 38.8 %copy-start.95 = (bf16[2,256,1408]{2,1,0:T(8,128)(2,1)}, bf16[2,256,1408]{2,1,0:T(8,128)(2,1)S(1)}, u32[]{:S(2)}) copy-start(bf16[2,256,1408]{2,1,0:T(8,128)(2,1)S(1)} %collective-permute-done.4) | copy-start | bytes 4325380
  52.7 37.1 %copy-start.97 = (bf16[2,256,1408]{2,1,0:T(8,128)(2,1)}, bf16[2,256,1408]{2,1,0:T(8,128)(2,1)S(1)}, u32[]{:S(2)}) copy-start(bf16[2,256,1408]{2,1,0:T(8,128)(2,1)S(1)} %collective-permute-done.3) | copy-start | bytes 4325380
  52.7 21.6 %collective-permute-start.9 = (bf16[3,256,512]{2,1,0:T(8,128)(2,1)}, bf16[3,256,512]{2,1,0:T(8,128)(2,1)S(1)}, u32[]{:S(2)}, u32[]{:S(2)}) collective-permute-start(bf16[3,256,512]{2,1,0:T(8,128)(2,1)} %param.17), channel_id=1, source_target_pairs={{0,24},{8,16},{16,8},{24,0},{1,25},{9,17},{17,9},{25,1},{2,26},{10... | collective-permute-start | bytes 2359304 | tf_op jit(solution)/shard_map/ppermute | solution.py:768
  53.8 32.8 %collective-permute-start.8 = (bf16[3,256,512]{2,1,0:T(8,128)(2,1)}, bf16[3,256,512]{2,1,0:T(8,128)(2,1)S(1)}, u32[]{:S(2)}, u32[]{:S(2)}) collective-permute-start(bf16[3,256,512]{2,1,0:T(8,128)(2,1)} %param.17), channel_id=1, source_target_pairs={{0,16},{8,24},{16,0},{24,8},{1,17},{9,25},{17,1},{25,9},{2,18},{10... | collective-permute-start | bytes 2359304 | tf_op jit(solution)/shard_map/ppermute | solution.py:768
  55.6 34.1 %collective-permute-start.7 = (bf16[3,256,512]{2,1,0:T(8,128)(2,1)}, bf16[3,256,512]{2,1,0:T(8,128)(2,1)S(1)}, u32[]{:S(2)}, u32[]{:S(2)}) collective-permute-start(bf16[3,256,512]{2,1,0:T(8,128)(2,1)} %param.17), channel_id=1, source_target_pairs={{0,8},{8,0},{16,24},{24,16},{1,9},{9,1},{17,25},{25,17},{2,10},{10... | collective-permute-start | bytes 2359304 | tf_op jit(solution)/shard_map/ppermute | solution.py:768
  56.2 45.4 %collective-permute-start.12 = (bf16[1,256,1408]{2,1,0:T(8,128)(2,1)S(1)}, bf16[1,256,1408]{2,1,0:T(8,128)(2,1)S(1)}, u32[]{:S(2)}, u32[]{:S(2)}) collective-permute-start(bf16[1,256,1408]{2,1,0:T(8,128)(2,1)S(1)} %slice.188), channel_id=1, source_target_pairs={{0,8},{8,0},{16,24},{24,16},{1,9},{9,1},{17,25},{25,17},{2,10},{10... | collective-permute-start | bytes 2162696 | tf_op jit(solution)/shard_map/ppermute | solution.py:768
  57.9 44.2 %collective-permute-start.11 = (bf16[1,256,1408]{2,1,0:T(8,128)(2,1)S(1)}, bf16[1,256,1408]{2,1,0:T(8,128)(2,1)S(1)}, u32[]{:S(2)}, u32[]{:S(2)}) collective-permute-start(bf16[1,256,1408]{2,1,0:T(8,128)(2,1)S(1)} %slice.187), channel_id=1, source_target_pairs={{0,16},{8,24},{16,0},{24,8},{1,17},{9,25},{17,1},{25,9},{2,18},{10... | collective-permute-start | bytes 2162696 | tf_op jit(solution)/shard_map/ppermute | solution.py:768
  89.8 12.4 %copy-start.99 = (bf16[2,256,1408]{2,1,0:T(8,128)(2,1)S(1)}, bf16[2,256,1408]{2,1,0:T(8,128)(2,1)}, u32[]{:S(2)}) copy-start(bf16[2,256,1408]{2,1,0:T(8,128)(2,1)} %param.20) | copy-start | bytes 4325380
  90.2 43.4 %copy-start.13 = (bf16[4,3,256,512]{3,2,1,0:T(8,128)(2,1)}, bf16[4,3,256,512]{3,2,1,0:T(8,128)(2,1)S(1)}, u32[]{:S(2)}) copy-start(bf16[4,3,256,512]{3,2,1,0:T(8,128)(2,1)S(1)} %pad_maximum_fusion.1.w0_ref.refs_0_) | copy-start | bytes 9437188
  90.2 12.0 %copy-start.96 = (bf16[2,256,1408]{2,1,0:T(8,128)(2,1)S(1)}, bf16[2,256,1408]{2,1,0:T(8,128)(2,1)}, u32[]{:S(2)}) copy-start(bf16[2,256,1408]{2,1,0:T(8,128)(2,1)} %copy-done.95) | copy-start | bytes 4325380
  90.2 12.0 %copy-start.98 = (bf16[2,256,1408]{2,1,0:T(8,128)(2,1)S(1)}, bf16[2,256,1408]{2,1,0:T(8,128)(2,1)}, u32[]{:S(2)}) copy-start(bf16[2,256,1408]{2,1,0:T(8,128)(2,1)} %copy-done.97) | copy-start | bytes 4325380
  90.3 34.4 %collective-permute-start.10 = (bf16[4,3,256,512]{3,2,1,0:T(8,128)(2,1)S(1)}, bf16[4,3,256,512]{3,2,1,0:T(8,128)(2,1)}, u32[]{:S(2)}, u32[]{:S(2)}) collective-permute-start(bf16[4,3,256,512]{3,2,1,0:T(8,128)(2,1)S(1)} %pad_maximum_fusion.1.w0_ref.refs_0_), channel_id=1, source_target_pairs={{0,4},{4,0},{1,5},{5,1},{2,6},{6,2},{3,7},{7,3},{8,12},{12,8},{9,1... | collective-permute-start | bytes 9437192 | tf_op jit(solution)/shard_map/ppermute | solution.py:27
  105.4 46.5 %collective-permute-start.13 = (bf16[4,2,256,1408]{3,2,1,0:T(8,128)(2,1)}, bf16[4,2,256,1408]{3,2,1,0:T(8,128)(2,1)}, u32[]{:S(2)}, u32[]{:S(2)}) collective-permute-start(bf16[4,2,256,1408]{3,2,1,0:T(8,128)(2,1)} %pad_maximum_fusion.w0_ref.refs_2_), channel_id=1, source_target_pairs={{0,4},{4,0},{1,5},{5,1},{2,6},{6,2},{3,7},{7,3},{8,12},{12,8},{9,1... | collective-permute-start | bytes 17301512 | tf_op jit(solution)/shard_map/ppermute | solution.py:27
  120.6 13.0 %copy-start.53 = (bf16[512,1024]{1,0:T(8,128)(2,1)}, bf16[512,1024]{1,0:T(8,128)(2,1)S(1)}, u32[]{:S(2)}) copy-start(bf16[512,1024]{1,0:T(8,128)(2,1)S(1)} %get-tuple-element.78.own_ref) | copy-start | bytes 3145732
  120.6 13.0 %copy-start.61 = (bf16[512,1024]{1,0:T(8,128)(2,1)}, bf16[512,1024]{1,0:T(8,128)(2,1)S(1)}, u32[]{:S(2)}) copy-start(bf16[512,1024]{1,0:T(8,128)(2,1)S(1)} %get-tuple-element.79.other_ref) | copy-start | bytes 3145732
  151.4 15.2 %copy-start.2 = (bf16[7680,256]{1,0:T(8,128)(2,1)S(1)}, bf16[7680,256]{1,0:T(8,128)(2,1)}, u32[]{:S(2)}) copy-start(bf16[7680,256]{1,0:T(8,128)(2,1)} %all-gather.12.cloned.1.call-done) | copy-start | bytes 11796484
  151.4 15.2 %collective-permute-start.14 = (bf16[4,1920,256]{2,1,0:T(8,128)(2,1)}, bf16[4,1920,256]{2,1,0:T(8,128)(2,1)S(1)}, u32[]{:S(2)}, u32[]{:S(2)}) collective-permute-start(bf16[4,1920,256]{2,1,0:T(8,128)(2,1)} %bitcast.74), channel_id=1, source_target_pairs={{0,4},{4,0},{1,5},{5,1},{2,6},{6,2},{3,7},{7,3},{8,12},{12,8},{9,1... | collective-permute-start | bytes 11796488 | tf_op jit(solution)/shard_map/ppermute | solution.py:27
  177.6 12.3 %copy-start.58 = (bf16[512,1024]{1,0:T(8,128)(2,1)S(1)}, bf16[512,1024]{1,0:T(8,128)(2,1)}, u32[]{:S(2)}) copy-start(bf16[512,1024]{1,0:T(8,128)(2,1)} %copy-done.57) | copy-start | bytes 3145732
  177.6 12.3 %copy-start.66 = (bf16[512,1024]{1,0:T(8,128)(2,1)S(1)}, bf16[512,1024]{1,0:T(8,128)(2,1)}, u32[]{:S(2)}) copy-start(bf16[512,1024]{1,0:T(8,128)(2,1)} %copy-done.65) | copy-start | bytes 3145732
  177.6 89.9 %reduce-scatter.6.cloned.1.call-start = ((), (), s32[]{:S(2)}) async-start(), calls=%async_computation.6 | async-start | bytes 2621440 | tf_op jit(solution)/shard_map/reduce_scatter | solution.py:803
  189.9 15.0 %copy-start.3 = (bf16[7680,256]{1,0:T(8,128)(2,1)S(1)}, bf16[7680,256]{1,0:T(8,128)(2,1)}, u32[]{:S(2)}) copy-start(bf16[7680,256]{1,0:T(8,128)(2,1)} %all-gather.12.cloned.1.call-done) | copy-start | bytes 11796484
  190.0 14.9 %copy-start.7 = (bf16[4,1920,256]{2,1,0:T(8,128)(2,1)S(1)}, bf16[4,1920,256]{2,1,0:T(8,128)(2,1)}, u32[]{:S(2)}) copy-start(bf16[4,1920,256]{2,1,0:T(8,128)(2,1)} %copy-done.6) | copy-start | bytes 11796484
  204.9 17.2 %copy-start = (bf16[256,2048]{1,0:T(8,128)(2,1)S(1)}, bf16[256,2048]{1,0:T(8,128)(2,1)}, u32[]{:S(2)}) copy-start(bf16[256,2048]{1,0:T(8,128)(2,1)} %x_ref.7) | copy-start | bytes 3145732
  204.9 17.2 %copy-start.11 = (bf16[256,2048]{1,0:T(8,128)(2,1)S(1)}, bf16[256,2048]{1,0:T(8,128)(2,1)}, u32[]{:S(2)}) copy-start(bf16[256,2048]{1,0:T(8,128)(2,1)} %teach_ref.3) | copy-start | bytes 3145732
  204.9 17.2 %copy-start.12 = (bf16[256,2048]{1,0:T(8,128)(2,1)S(1)}, bf16[256,2048]{1,0:T(8,128)(2,1)}, u32[]{:S(2)}) copy-start(bf16[256,2048]{1,0:T(8,128)(2,1)} %cot_ref.3) | copy-start | bytes 3145732
  214.1 100.7 %all-gather.10.cloned.1.call-start = ((), (), s32[]{:S(2)}) async-start(), calls=%async_computation.9 | async-start | bytes 2621440 | tf_op jit(solution)/shard_map/all_gather | solution.py:800
  227.0 138.6 %all-gather.8.cloned.1.call-start = ((), (), s32[]{:S(2)}) async-start(), calls=%async_computation.8 | async-start | bytes 2621440 | tf_op jit(solution)/shard_map/all_gather | solution.py:800
  272.4 246.8 %reduce-scatter.14.cloned.1.call-start = ((), (), s32[]{:S(2)}) async-start(), calls=%async_computation.12 | async-start | bytes 4915200 | tf_op jit(solution)/shard_map/reduce_scatter | solution.py:851
  332.6 26.8 %copy-start.47 = (bf16[512,2816]{1,0:T(8,128)(2,1)}, bf16[512,2816]{1,0:T(8,128)(2,1)S(1)}, u32[]{:S(2)}) copy-start(bf16[512,2816]{1,0:T(8,128)(2,1)S(1)} %get-tuple-element.97.gu_ref) | copy-start | bytes 8650756
  371.6 13.0 %collective-permute-start.15 = (bf16[1920,1024]{1,0:T(8,128)(2,1)S(1)}, bf16[1920,1024]{1,0:T(8,128)(2,1)S(1)}, u32[]{:S(2)}, u32[]{:S(2)}) collective-permute-start(bf16[1920,1024]{1,0:T(8,128)(2,1)S(1)} %add_convert_fusion.3), channel_id=1, source_target_pairs={{0,4},{4,0},{1,5},{5,1},{2,6},{6,2},{3,7},{7,3},{8,12},{12,8},{9,1... | collective-permute-start | bytes 11796488 | tf_op jit(solution)/shard_map/ppermute | solution.py:27
  403.6 24.4 %collective-permute-start.16 = (bf16[1024,2816]{1,0:T(8,128)(2,1)}, bf16[1024,2816]{1,0:T(8,128)(2,1)}, u32[]{:S(2)}, u32[]{:S(2)}) collective-permute-start(bf16[1024,2816]{1,0:T(8,128)(2,1)} %add_convert_fusion.1), channel_id=1, source_target_pairs={{0,4},{4,0},{1,5},{5,1},{2,6},{6,2},{3,7},{7,3},{8,12},{12,8},{9,1... | collective-permute-start | bytes 17301512 | tf_op jit(solution)/shard_map/ppermute | solution.py:27
  403.6 176.0 %reduce-scatter.12.cloned.1.call-start = ((), (), s32[]{:S(2)}) async-start(), calls=%async_computation.11 | async-start | bytes 2621440 | tf_op jit(solution)/shard_map/reduce_scatter | solution.py:803
  415.0 13.0 %copy-start.45 = (bf16[512,2816]{1,0:T(8,128)(2,1)S(1)}, bf16[512,2816]{1,0:T(8,128)(2,1)}, u32[]{:S(2)}) copy-start(bf16[512,2816]{1,0:T(8,128)(2,1)} %copy-done.44) | copy-start | bytes 8650756
  415.0 13.0 %copy-start.59 = (bf16[512,1024]{1,0:T(8,128)(2,1)S(1)}, bf16[512,1024]{1,0:T(8,128)(2,1)}, u32[]{:S(2)}) copy-start(bf16[512,1024]{1,0:T(8,128)(2,1)} %copy-done.57) | copy-start | bytes 3145732
  428.0 17.8 %copy-start.81 = (bf16[1024,1536]{1,0:T(8,128)(2,1)}, bf16[1024,1536]{1,0:T(8,128)(2,1)S(1)}, u32[]{:S(2)}) copy-start(bf16[1024,1536]{1,0:T(8,128)(2,1)S(1)} %get-tuple-element.131.qkv_ref) | copy-start | bytes 9437188
  428.0 17.7 %copy-start.48 = (bf16[512,2816]{1,0:T(8,128)(2,1)S(1)}, bf16[512,2816]{1,0:T(8,128)(2,1)}, u32[]{:S(2)}) copy-start(bf16[512,2816]{1,0:T(8,128)(2,1)} %copy-done.47) | copy-start | bytes 8650756
  442.6 39.8 %collective-permute-start.18 = (bf16[256,2816]{1,0:T(8,128)(2,1)}, bf16[256,2816]{1,0:T(8,128)(2,1)}, u32[]{:S(2)}, u32[]{:S(2)}) collective-permute-start(bf16[256,2816]{1,0:T(8,128)(2,1)} %get-tuple-element.138), channel_id=1, source_target_pairs={{0,16},{8,24},{16,0},{24,8},{1,17},{9,25},{17,1},{25,9},{2,18},{10... | collective-permute-start | bytes 4325384 | tf_op jit(solution)/shard_map/ppermute | solution.py:768
  444.3 38.1 %collective-permute-start.17 = (bf16[256,2816]{1,0:T(8,128)(2,1)}, bf16[256,2816]{1,0:T(8,128)(2,1)}, u32[]{:S(2)}, u32[]{:S(2)}) collective-permute-start(bf16[256,2816]{1,0:T(8,128)(2,1)} %get-tuple-element.139), channel_id=1, source_target_pairs={{0,8},{8,0},{16,24},{24,16},{1,9},{9,1},{17,25},{25,17},{2,10},{10... | collective-permute-start | bytes 4325384 | tf_op jit(solution)/shard_map/ppermute | solution.py:768
  445.8 36.6 %copy-start.64 = (bf16[512,1024]{1,0:T(8,128)(2,1)S(1)}, bf16[512,1024]{1,0:T(8,128)(2,1)}, u32[]{:S(2)}) copy-start(bf16[512,1024]{1,0:T(8,128)(2,1)} %copy-done.61) | copy-start | bytes 3145732
  461.3 136.7 %reduce-scatter.10.cloned.1.call-start = ((), (), s32[]{:S(2)}) async-start(), calls=%async_computation.10 | async-start | bytes 2621440 | tf_op jit(solution)/shard_map/reduce_scatter | solution.py:803
  489.8 40.9 %collective-permute-start.20 = (bf16[1024,1536]{1,0:T(8,128)(2,1)}, bf16[1024,1536]{1,0:T(8,128)(2,1)}, u32[]{:S(2)}, u32[]{:S(2)}) collective-permute-start(bf16[1024,1536]{1,0:T(8,128)(2,1)} %convolution_convert_fusion), channel_id=1, source_target_pairs={{0,4},{4,0},{1,5},{5,1},{2,6},{6,2},{3,7},{7,3},{8,12},{12,8},{9,1... | collective-permute-start | bytes 9437192 | tf_op jit(solution)/shard_map/ppermute | solution.py:27
  495.4 35.2 %collective-permute-start.19 = (bf16[256,2816]{1,0:T(8,128)(2,1)}, bf16[256,2816]{1,0:T(8,128)(2,1)}, u32[]{:S(2)}, u32[]{:S(2)}) collective-permute-start(bf16[256,2816]{1,0:T(8,128)(2,1)} %constant_dynamic-slice_fusion.3), channel_id=1, source_target_pairs={{0,24},{8,16},{16,8},{24,0},{1,25},{9,17},{17,9},{25,1},{2,26},{10... | collective-permute-start | bytes 4325384 | tf_op jit(solution)/shard_map/ppermute | solution.py:768
  518.9 11.7 %copy-start.56 = (bf16[512,1024]{1,0:T(8,128)(2,1)S(1)}, bf16[512,1024]{1,0:T(8,128)(2,1)}, u32[]{:S(2)}) copy-start(bf16[512,1024]{1,0:T(8,128)(2,1)} %copy-done.53) | copy-start | bytes 3145732
  519.0 11.7 %copy-start.60 = (bf16[512,1024]{1,0:T(8,128)(2,1)S(1)}, bf16[512,1024]{1,0:T(8,128)(2,1)}, u32[]{:S(2)}) copy-start(bf16[512,1024]{1,0:T(8,128)(2,1)} %copy-done.57) | copy-start | bytes 3145732
  536.1 20.5 %collective-permute-start.21 = (bf16[256,1536]{1,0:T(8,128)(2,1)S(1)}, bf16[256,1536]{1,0:T(8,128)(2,1)S(1)}, u32[]{:S(2)}, u32[]{:S(2)}) collective-permute-start(bf16[256,1536]{1,0:T(8,128)(2,1)S(1)} %get-tuple-element.140), channel_id=1, source_target_pairs={{0,8},{8,0},{16,24},{24,16},{1,9},{9,1},{17,25},{25,17},{2,10},{10... | collective-permute-start | bytes 2359304 | tf_op jit(solution)/shard_map/ppermute | solution.py:768
  537.6 35.6 %collective-permute-start.23 = (bf16[256,1536]{1,0:T(8,128)(2,1)S(1)}, bf16[256,1536]{1,0:T(8,128)(2,1)S(1)}, u32[]{:S(2)}, u32[]{:S(2)}) collective-permute-start(bf16[256,1536]{1,0:T(8,128)(2,1)S(1)} %get-tuple-element.141), channel_id=1, source_target_pairs={{0,24},{8,16},{16,8},{24,0},{1,25},{9,17},{17,9},{25,1},{2,26},{10... | collective-permute-start | bytes 2359304 | tf_op jit(solution)/shard_map/ppermute | solution.py:768
  539.1 35.4 %collective-permute-start.22 = (bf16[256,1536]{1,0:T(8,128)(2,1)S(1)}, bf16[256,1536]{1,0:T(8,128)(2,1)S(1)}, u32[]{:S(2)}, u32[]{:S(2)}) collective-permute-start(bf16[256,1536]{1,0:T(8,128)(2,1)S(1)} %get-tuple-element.142), channel_id=1, source_target_pairs={{0,16},{8,24},{16,0},{24,8},{1,17},{9,25},{17,1},{25,9},{2,18},{10... | collective-permute-start | bytes 2359304 | tf_op jit(solution)/shard_map/ppermute | solution.py:768
  576.0 1.2 collective-permute-start.24
  577.2 5.9 collective-permute-start.25
  583.2 14.9 %copy-start.29 = (f32[128,2048]{1,0:T(8,128)S(1)}, f32[128,2048]{1,0:T(8,128)}, u32[]{:S(2)}) copy-start(f32[128,2048]{1,0:T(8,128)} %copy-done.28) | copy-start | bytes 3145732
  583.2 3.7 collective-permute-start.26
  587.0 4.9 collective-permute-start.27
  591.9 3.6 collective-permute-start.28
  (75 other events, 282.2 us)
Sparse Core Ops, SparseCore 0:
  9.6 83.7 all-gather.5
  95.8 48.9 all-gather.11
  177.7 44.3 reduce-scatter.7
  224.4 43.1 reduce-scatter.5
  269.5 45.2 all-gather.9
  316.8 44.6 all-gather.7
  403.7 54.9 reduce-scatter.13
  461.5 45.7 reduce-scatter.11
  519.1 43.8 reduce-scatter.9

commit v3 on v2

--- a/solution.py
+++ b/solution.py
@@ -41,40 +41,14 @@
     return buf
 
 
-def scatter_axis(a, axis, n):
+def direct_sum(a, axis, n):
     me = lax.axis_index(axis)
-    buf = a
-    k = n // 2
-    while k >= 1:
-        upper = (me // k) % 2 == 1
-        lo, hi = buf[:k], buf[k:]
-        sent = lax.ppermute(
-            jnp.where(upper, lo, hi), axis, [(j, j ^ k) for j in range(n)]
-        )
-        buf = jnp.where(upper, hi, lo) + sent
-        k //= 2
-    return buf[0]
-
-
-def line_scatter(part, n, holds=()):
-    me = lax.axis_index("tp")
-    rows = part.shape[0] // n
-
-    def chunk(j):
-        return lax.dynamic_slice_in_dim(part, jnp.clip(j, 0, n - 1) * rows, rows, 0)
-
-    def plus(a, b):
-        return a if b is None else (a.astype(f32) + b.astype(f32)).astype(bf16)
-
-    up = down = None
-    for s in range(n - 1):
-        up = plus(chunk(n - 1 - s + me), up)
-        down = plus(chunk(s - (n - 1) + me), down)
-        up = lax.ppermute(up, "tp", [(k, k + 1) for k in range(s + 1)])
-        down = lax.ppermute(down, "tp", [(k, k - 1) for k in range(n - 1 - s, n)])
-        if s < len(holds):
-            up, down = after(up, holds[s]), after(down, holds[s])
-    return chunk(me).astype(f32) + up.astype(f32) + down.astype(f32)
+
+    def row(k):
+        return lax.dynamic_index_in_dim(a, me ^ k, 0, keepdims=False)
+
+    sent = [lax.ppermute(row(k), axis, [(j, j ^ k) for j in range(n)]) for k in range(1, n)]
+    return row(0) + sum(sent)
 
 
 def rotary_tables(line):
@@ -185,7 +159,7 @@
             jax.ShapeDtypeStruct((half, width), bf16),
             jax.ShapeDtypeStruct((pairs, blocks, 2 * span), f32),
         ],
-        compiler_params=pltpu.CompilerParams(vmem_limit_bytes=30 << 20),
+        compiler_params=pltpu.CompilerParams(vmem_limit_bytes=(56 if part else 30) << 20),
         cost_estimate=pl.CostEstimate(
             flops=pairs * SEQ * SEQ * PAIR * 4,
             transcendentals=pairs * SEQ * SEQ,
@@ -277,7 +251,7 @@
         out_specs=out_specs,
         out_shape=out_shape,
         scratch_shapes=scratch,
-        compiler_params=pltpu.CompilerParams(vmem_limit_bytes=30 << 20),
+        compiler_params=pltpu.CompilerParams(vmem_limit_bytes=(56 if part else 30) << 20),
         cost_estimate=pl.CostEstimate(
             flops=pairs * SEQ * SEQ * PAIR * 10,
             transcendentals=pairs * SEQ * SEQ,
@@ -287,7 +261,7 @@
     )(qkv[part], qkv[0], qkv[0], qkv[1], qkv[1], grad, lse, *tables, *kept)
 
 
-def call(kernel, name, grid, in_specs, out_specs, out_shape, scalars, args, flops=0, scratch=()):
+def call(kernel, name, grid, in_specs, out_specs, out_shape, scalars, args, flops=0, scratch=(), vmem=30):
     moved = sum(a.size * a.dtype.itemsize for a in args)
     moved += sum(o.size * jnp.dtype(o.dtype).itemsize for o in out_shape)
     return pl.pallas_call(
@@ -300,7 +274,7 @@
             scratch_shapes=scratch,
         ),
         out_shape=out_shape,
-        compiler_params=pltpu.CompilerParams(vmem_limit_bytes=30 << 20),
+        compiler_params=pltpu.CompilerParams(vmem_limit_bytes=vmem << 20),
         cost_estimate=pl.CostEstimate(flops=flops, transcendentals=0, bytes_accessed=moved),
         name=name,
     )(scalars, *args)
@@ -690,6 +664,7 @@
         scalars,
         (grad_qkv, grad_gu, x, stats, *weights),
         flops=2 * rows * D * (3 * width + 2 * hid),
+        vmem=56 if part else 30,
     )
 
 
@@ -779,7 +754,8 @@
     def far_shard(near):
         if chips != 4:
             return []
-        return [cat([to_chip(near[0][:1], 2), to_chip(near[1][1:], 1)], 0)]
+        cut = feats // 2
+        return [cat([to_chip(near[0][:, :cut], 2), to_chip(near[1][:, cut:], 1)], 1)]
 
     def both_cores(own):
         return [own, swap_core(own)]
@@ -807,10 +783,10 @@
     shard = after(gate_up_weight, small)
     near = near_shards(shard)
     slot = after(slot, *near)
-    qkv_shard = after(qkv_weight, vectors, *near)
+    qkv_shard = after(qkv_weight, vectors, *tables, *near)
     w_gu = both_cores(jnp.stack([shard, *near, *far_shard(near)]))
-    near = near_shards(qkv_shard) + ([to_chip(qkv_shard, 3)] if chips == 4 else [])
-    w_qkv = both_cores(jnp.stack([qkv_shard, *near]))
+    near = near_shards(qkv_shard)
+    w_qkv = both_cores(jnp.stack([qkv_shard, *near, *far_shard(near)]))
     normed, stats, x, qkv = [None] * 2, [None] * 2, [None] * 2, [None] * 2
     for t in range(2):
         *normed[t], stats[t], x[t] = norm(scalars, t, span, slot, vectors, feats)
@@ -838,12 +814,6 @@
 
     half = D // 2
 
-    def seed_half(t, h):
-        return seed_all[t][:, h * half : (h + 1) * half]
-
-    def od_part(t, h, *hold):
-        return dot_tn(after(acts[t], *hold), seed_half(t, h))
-
     def with_other(mine, theirs):
         return (mine + theirs.astype(f32)).astype(bf16)
 
@@ -856,50 +826,47 @@
     def sent_rows(a, some):
         return [to_chip(rows_of(a, k), k) for k in some]
 
-    def gu_part(t, h, hold):
-        return dot_tn(normed[t][h], after(grad_gu[t], hold))
-
+    acts_all = cat(acts, 0)
+    normed_all = [cat([normed[0][h], normed[1][h]], 0) for h in range(2)]
     grad_attn, grad_gu = [None] * 2, [None] * 2
     grad_attn[0], grad_gu[0] = grad_acts(scalars, seed_all[0], w_od, gate[0], up[0])
     kept = attend_back(0, span, qkv, grad_attn[0], lse[0], tables)
-    od_early = [od_part(0, h, kept[0]) for h in range(2)]
-    gu_early = [gu_part(0, h, kept[0]) for h in range(2)]
-
-    seed_all[1] = after(seed_all[1], *od_early, *gu_early)
-    od_sent = (od_early[1] + od_part(1, 1)).astype(bf16)
+
+    seed_all[1] = after(seed_all[1], kept[0], acts_all, *normed_all)
+    seeds_all = cat(seed_all, 0)
+    od_sent = dot_tn(acts_all, seeds_all[:, half:]).astype(bf16)
     od_theirs = swap_core(od_sent)
     seed_all[1] = after(seed_all[1], od_sent)
     grad_attn[1], grad_gu[1] = grad_acts(scalars, seed_all[1], w_od, gate[1], up[1])
-    od_sum = with_other(od_early[0] + od_part(1, 0, grad_gu[1]), od_theirs)
+    od_sum = dot_tn(acts_all, after(seeds_all, grad_gu[1])[:, :half])
+    od_sum = with_other(od_sum, od_theirs)
     od_grad = scattered(od_sum, 1)
-    gu_sent = (gu_early[1] + gu_part(1, 1, od_sum)).astype(bf16)
+    gu_all = cat([grad_gu[0], after(grad_gu[1], od_sum)], 0)
+    gu_sent = dot_tn(normed_all[1], gu_all).astype(bf16)
     gu_theirs = swap_core(gu_sent)
     grad_qkv, grad_bias = attend_back(
         1, span, qkv, after(grad_attn[1], gu_sent), lse[1], tables, kept
     )
-    gu_sum = with_other(gu_early[0] + gu_part(1, 0, grad_qkv), gu_theirs)
-    normed_all = [cat([normed[0][h], normed[1][h]], 0) for h in range(2)]
+    gu_sum = with_other(dot_tn(normed_all[0], after(gu_all, grad_qkv)), gu_theirs)
     grads, gains, shifts, sums = [None] * 2, [None] * 2, [None] * 2, [None] * 2
 
-    def back(t, hold):
+    def back(t, *hold):
         grads[t], gain, shift = grad_normed(
-            scalars, t, after(grad_qkv, hold), grad_gu[t], w_qkv, w_gu, x[t], stats[t]
+            scalars, t, after(grad_qkv, *hold), grad_gu[t], w_qkv, w_gu, x[t], stats[t]
         )
         gains[t], shifts[t] = jnp.sum(gain, 0), jnp.sum(shift, 0)
         sums[t] = summed_line(grads[t])
 
-    back(0, gu_sum)
-    gu_got = sent_rows(gu_sum, (1, 2))
-    qkv_held = after(grad_qkv, grads[0], *gu_got)
+    qkv_held = after(grad_qkv, gu_sum)
     qkv_sent = dot_tn(normed_all[1], qkv_held).astype(bf16)
     qkv_theirs = swap_core(qkv_sent)
-    gu_got += sent_rows(after(gu_sum, *gu_got), range(3, chips))
-    back(1, qkv_sent)
+    gu_got = sent_rows(gu_sum, (1, 2))
+    back(0, qkv_sent)
+    qkv_back = after(grad_qkv, grads[0], *gu_got)
+    gu_got += sent_rows(after(gu_sum, qkv_back), range(3, chips))
+    back(1, qkv_back)
     qkv_held = after(qkv_held, grads[1], *gu_got)
     qkv_sum = with_other(dot_tn(normed_all[0], qkv_held), qkv_theirs)
-    qkv_got = sent_rows(qkv_sum, range(1, chips))
-    gu_grad = rows_of(gu_sum, 0).astype(f32) + sum(g.astype(f32) for g in gu_got)
-    qkv_grad = rows_of(qkv_sum, 0).astype(f32) + sum(g.astype(f32) for g in qkv_got)
     input_grad = None
     for t in range(2):
         input_grad = last(
@@ -918,11 +885,14 @@
         vector = jnp.stack([gains[h], shifts[h]]).reshape(2, chips, line, n)
         vector = cat([vector.transpose(1, 2, 0, 3).reshape(chips, line, 2 * n), scalar_sums], -1)
         small_sums.append(cat([vector.reshape(chips, -1), heads[h].reshape(chips, -1)], -1))
-    small_sums = [after(v, qkv_grad) for v in small_sums]
-    total = scatter_axis(small_sums[0] + swap_core(small_sums[1]), "chip", chips)
+    small_sums = [after(v, *gu_got) for v in small_sums]
+    total = direct_sum(small_sums[0] + swap_core(small_sums[1]), "chip", chips)
+    qkv_got = sent_rows(after(qkv_sum, total), range(1, chips))
+    gu_grad = rows_of(gu_sum, 0).astype(f32) + sum(g.astype(f32) for g in gu_got)
+    qkv_grad = rows_of(qkv_sum, 0).astype(f32) + sum(g.astype(f32) for g in qkv_got)
     cut = line * (2 * n + 2)
     qkv_b_grad = total[cut:].reshape(3, -1)
-    total = scatter_axis(total[:cut].reshape(line, -1), "tp", line)
+    total = direct_sum(total[:cut].reshape(line, -1), "tp", line)
     gain_grad, bias_grad = total[:n], total[n : 2 * n]
     loss_value = total[2 * n] / (total[2 * n + 1] * D)
     return (

time: 619 us -> 612 us (0.989)
  matrix products: 70.9 us -> 50.6 us
  starting transfers between devices: 32.1 us -> 50.2 us
  waiting for transfers between devices: 228 us -> 210 us
  Pallas kernels: 157 us -> 165 us
    dot_general x10 -> x6, matrix products: 70.9 us -> 50.6 us  [dot_tn(): lax.dot_general(a, b, (((0,), (0,)), ((), ())), preferred_element_type=f32)]
    reduce_scatter x4, starting transfers between devices: 0.63 us -> 12.9 us  [summed_line(): return lax.psum_scatter(a, 'tp', scatter_dimension=0, tiled=True)]
    reduce_scatter x4, waiting for transfers between devices: 48.5 us -> 39.3 us  [summed_line(): return lax.psum_scatter(a, 'tp', scatter_dimension=0, tiled=True)]
    ppermute x13 -> x14, waiting for transfers between devices: 120 us -> 111 us  [to_chip(): return lax.ppermute(a, 'chip', [(c, c ^ k) for c in range(chips)])]
    ppermute x5, waiting for transfers between devices: 13 us -> 6.26 us  [gather_axis(): other = lax.ppermute(buf, axis, [(j, j ^ k) for j in range(n)])]
    ppermute x13 -> x14, starting transfers between devices: 17.1 us -> 19.4 us  [to_chip(): return lax.ppermute(a, 'chip', [(c, c ^ k) for c in range(chips)])]
    unnamed x202 -> x176, local copies, waits for them, and re-layouts: 60.8 us -> 59.1 us
  transfers between devices with their start and end apart: 38 -> 41, of which waited for: 23 -> 21; matrix products, arithmetic and copies ran while one was open for 14% -> 12% of each run, Pallas kernels for 24% -> 26%
where the time goes in v3:
time: 612 us; the launch traced here: 604 us
  waiting for transfers between devices  210 us (34%)
  Pallas kernels  165 us (27%)
  local copies, waits for them, and re-layouts  85.4 us (14%)
  matrix products  50.6 us (8%)
  starting transfers between devices  50.2 us (8%)
  other arithmetic  23.4 us (4%)
  between operations  19.5 us (3%)
    pallas_call x12, Pallas kernels, call(): pl.pallas_call(kernel, grid_spec=pltpu.PrefetchScalarGridSpec(num_scalar_...  112 us
    ppermute x14, waiting for transfers between devices, to_chip(): return lax.ppermute(a, 'chip', [(c, c ^ k) for c in range(chips)])  111 us
    unnamed x176, local copies, waits for them, and re-layouts  59.1 us
    dot_general x6, matrix products, dot_tn(): lax.dot_general(a, b, (((0,), (0,)), ((), ())), preferred_element_type=f32)  50.6 us
    all_gather x3, waiting for transfers between devices, along_line(): return lax.all_gather(a, 'tp', axis=0, tiled=True)  46.4 us
    reduce_scatter x4, waiting for transfers between devices, summed_line(): return lax.psum_scatter(a, 'tp', scatter_dimension=0, tiled=True)  39.3 us
    pallas_call x2, Pallas kernels, attend_back(): pl.pallas_call(functools.partial(attend_back_kernel, part, span), grid=(p...  26.4 us
    ppermute x14, starting transfers between devices, to_chip(): return lax.ppermute(a, 'chip', [(c, c ^ k) for c in range(chips)])  19.4 us
  transfers between devices with their start and end apart: 41, of which 21 were waited for; matrix products, arithmetic and copies ran while one was open for 12% of the time, Pallas kernels for 26%

profile of v3, /device:TPU:0, one launch (start us, length us, event | category | flops | bytes accessed | tf_op | source)
XLA Modules:
  0.0 604.2 jit_solution(1657948651587408976)
XLA Ops:
  9.9 2.2 pad_maximum_fusion.4
  12.2 2.6 collective-permute-start.1
  16.4 2.1 collective-permute-start.2
  20.2 2.1 collective-permute-start.4
  28.1 2.5 collective-permute-start.6
  31.9 2.4 collective-permute-done.6
  34.5 18.0 %collective-permute-done.4 = bf16[2,256,1408]{2,1,0:T(8,128)(2,1)} collective-permute-done((bf16[2,256,1408]{2,1,0:T(8,128)(2,1)}, bf16[2,256,1408]{2,1,0:T(8,128)(2,1)}, u32[]{:S(2)}, u32[]{:S(2)}) %collective-permute-start.4) | collective-permute-done | bytes 1441824 | tf_op jit(solution)/shard_map/ppermute | solution.py:743
  56.0 14.4 %collective-permute-done.8 = bf16[3,256,512]{2,1,0:T(8,128)(2,1)S(1)} collective-permute-done((bf16[3,256,512]{2,1,0:T(8,128)(2,1)S(1)}, bf16[3,256,512]{2,1,0:T(8,128)(2,1)S(1)}, u32[]{:S(2)}, u32[]{:S(2)}) %collective-permute-start.8) | collective-permute-done | bytes 786464 | tf_op jit(solution)/shard_map/ppermute | solution.py:743
  70.5 2.3 collective-permute-start.10
  78.3 4.5 collective-permute-done.10
  82.8 2.1 collective-permute-done.9
  85.0 1.9 pad_maximum_fusion.1.w0_ref.refs_0_
  86.9 7.8 %collective-permute-done.13 = bf16[2,128,1408]{2,1,0:T(8,128)(2,1)S(1)} collective-permute-done((bf16[2,128,1408]{2,1,0:T(8,128)(2,1)S(1)}, bf16[2,128,1408]{2,1,0:T(8,128)(2,1)S(1)}, u32[]{:S(2)}, u32[]{:S(2)}) %collective-permute-start.13) | collective-permute-done | bytes 720928 | tf_op jit(solution)/shard_map/ppermute | solution.py:743
  94.8 5.6 pad_maximum_fusion.w0_ref.refs_2_
  101.3 2.6 copy-done.1
  103.9 2.7 norm.3
  107.9 2.7 norm.2
  112.7 9.3 %joined.3.q_ref.k0_ref.v0_ref = bf16[3,512,512]{2,1,0:T(8,128)(2,1)S(1)} custom-call(s32[4]{0:T(128)S(1)} %pad_add_fusion.s_ref, bf16[512,1024]{1,0:T(8,128)(2,1)S(1)} %get-tuple-element.78.own_ref, bf16[512,1024]{1,0:T(8,128)(2,1)S(1)} %get-tuple-element.79.other_ref, f32[3,1,512]{2,1,0:T(1,128)S(1)} %reshape.121.bias_ref, f32[3,512,128]{2,1,0:T(8,128)S(1)} %bitcast.78, ...), custom_call_target="tpu_custom_call" | custom-call | flops 3221225472 | bytes 10754048 | tf_op jit(solution)/shard_map/joined/pallas_call | solution.py:267
  122.1 8.9 %joined.2.k1_ref.v1_ref.q_ref = bf16[3,512,512]{2,1,0:T(8,128)(2,1)S(1)} custom-call(s32[4]{0:T(128)S(1)} %pad_add_fusion.s_ref, bf16[512,1024]{1,0:T(8,128)(2,1)S(1)} %get-tuple-element.75.own_ref, bf16[512,1024]{1,0:T(8,128)(2,1)S(1)} %get-tuple-element.76.other_ref, f32[3,1,512]{2,1,0:T(1,128)S(1)} %reshape.121.bias_ref, f32[3,512,128]{2,1,0:T(8,128)S(1)} %bitcast.81, ...), custom_call_target="tpu_custom_call" | custom-call | flops 3221225472 | bytes 10754048 | tf_op jit(solution)/shard_map/joined/pallas_call | solution.py:267
  131.1 8.1 %attend.2 = (bf16[512,512]{1,0:T(8,128)(2,1)S(1)}, f32[4,4,256]{2,1,0:T(4,128)S(1)}) custom-call(bf16[3,512,512]{2,1,0:T(8,128)(2,1)S(1)} %joined.3.q_ref.k0_ref.v0_ref, bf16[3,512,512]{2,1,0:T(8,128)(2,1)S(1)} %joined.3.q_ref.k0_ref.v0_ref, bf16[3,512,512]{2,1,0:T(8,128)(2,1)S(1)} %joined.3.q_ref.k0_ref.v0_ref, ...), custom_call_target="tpu_custom_call" | custom-call | flops 2147483648 | bytes 5242880 | tf_op jit(solution)/shard_map/attend/pallas_call | solution.py:153
  141.1 3.8 all-gather.12.cloned.1.call-done
  147.4 11.4 %gate_up.2 = (f32[512,1408]{1,0:T(8,128)S(1)}, f32[512,1408]{1,0:T(8,128)S(1)}, bf16[512,1920]{1,0:T(8,128)(2,1)S(1)}) custom-call(s32[4]{0:T(128)S(1)} %pad_add_fusion.s_ref, bf16[512,1024]{1,0:T(8,128)(2,1)S(1)} %get-tuple-element.78.own_ref, bf16[512,1024]{1,0:T(8,128)(2,1)S(1)} %copy-done.42, bf16[512,512]{1,0:T(8,128)(2,1)S(1)} %copy-done.65, ...), custom_call_target="tpu_custom_call" | custom-call | flops 5905580032 | bytes 21889024 | tf_op jit(solution)/shard_map/gate_up/pallas_call | solution.py:267
  162.2 7.7 %branch.2 = bf16[512,2048]{1,0:T(8,128)(2,1)} custom-call(s32[4]{0:T(128)S(1)} %pad_add_fusion.s_ref, bf16[512,1920]{1,0:T(8,128)(2,1)S(1)} %get-tuple-element.81.acts_ref, bf16[4,1920,256]{2,1,0:T(8,128)(2,1)S(1)} %bitcast.73, bf16[4,1920,256]{2,1,0:T(8,128)(2,1)S(1)} %collective-permute-done.15.w1_ref), custom_call_target="tpu_custom_call" | custom-call | flops 4026531840 | bytes 11927552 | tf_op jit(solution)/shard_map/branch/pallas_call | solution.py:267
  173.0 12.7 %reduce-scatter.6.cloned.1.call-start = ((), (), s32[]{:S(2)}) async-start(), calls=%async_computation.6 | async-start | bytes 2621440 | tf_op jit(solution)/shard_map/reduce_scatter | solution.py:779
  185.7 10.3 %attend.3 = (bf16[512,512]{1,0:T(8,128)(2,1)}, f32[4,4,256]{2,1,0:T(4,128)}) custom-call(bf16[3,512,512]{2,1,0:T(8,128)(2,1)} %copy-done.62, bf16[3,512,512]{2,1,0:T(8,128)(2,1)} %copy-done.60, bf16[3,512,512]{2,1,0:T(8,128)(2,1)} %copy-done.60, bf16[3,512,512]{2,1,0:T(8,128)(2,1)} %copy-done.62, bf16[3,512,512]{2,1,0:T(8,128)(2,1)} %copy-done.62), custom_call_target="tpu_custom_call" | custom-call | flops 2147483648 | bytes 5242880 | tf_op jit(solution)/shard_map/attend/pallas_call | solution.py:153
  197.1 11.7 %gate_up.3 = (f32[512,1408]{1,0:T(8,128)S(1)}, f32[512,1408]{1,0:T(8,128)S(1)}, bf16[512,1920]{1,0:T(8,128)(2,1)S(1)}) custom-call(s32[4]{0:T(128)S(1)} %pad_add_fusion.s_ref, bf16[512,1024]{1,0:T(8,128)(2,1)S(1)} %get-tuple-element.75.own_ref, bf16[512,1024]{1,0:T(8,128)(2,1)S(1)} %get-tuple-element.76.other_ref, bf16[512,512]{1,0:T(8,128)(2,1)S(1)} %copy-done.66, ...), custom_call_target="tpu_custom_call" | custom-call | flops 5905580032 | bytes 21889024 | tf_op jit(solution)/shard_map/gate_up/pallas_call | solution.py:267
  211.9 6.4 %branch.3 = bf16[512,2048]{1,0:T(8,128)(2,1)S(1)} custom-call(s32[4]{0:T(128)S(1)} %pad_add_fusion.s_ref, bf16[512,1920]{1,0:T(8,128)(2,1)S(1)} %get-tuple-element.85.acts_ref, bf16[4,1920,256]{2,1,0:T(8,128)(2,1)S(1)} %bitcast.74, bf16[4,1920,256]{2,1,0:T(8,128)(2,1)S(1)} %copy-done.7), custom_call_target="tpu_custom_call" | custom-call | flops 4026531840 | bytes 11927552 | tf_op jit(solution)/shard_map/branch/pallas_call | solution.py:267
  222.0 1.9 finish.2
  225.9 39.2 %reduce-scatter.6.cloned.1.call-done.branch_ref = bf16[128,2048]{1,0:T(8,128)(2,1)} async-done(((bf16[512,2048]{1,0:T(8,128)(2,1)}), bf16[128,2048]{1,0:T(8,128)(2,1)}) %reduce-scatter.6.cloned.1.call-update) | async-done | bytes 524304 | tf_op jit(solution)/shard_map/reduce_scatter | solution.py:779
  266.2 1.9 finish.3
  272.1 2.1 copy-done.29
  277.6 34.2 %all-gather.10.cloned.1.call-done.seed_ref = bf16[512,2048]{1,0:T(8,128)(2,1)} async-done(((bf16[128,2048]{1,0:T(8,128)(2,1)}), bf16[512,2048]{1,0:T(8,128)(2,1)}) %all-gather.10.cloned.1.call-update) | async-done | bytes 2097168 | tf_op jit(solution)/shard_map/all_gather | solution.py:776
  311.9 2.1 copy-done.4
  314.0 2.1 copy-done.8
  317.7 1.9 copy-done.24
  319.6 1.9 copy-done.26
  321.5 8.1 %grad_acts.2 = (bf16[512,512]{1,0:T(8,128)(2,1)S(1)}, bf16[512,2816]{1,0:T(8,128)(2,1)S(1)}) custom-call(s32[4]{0:T(128)S(1)} %pad_add_fusion.s_ref, bf16[512,2048]{1,0:T(8,128)(2,1)S(1)} %copy-done.10, f32[512,1408]{1,0:T(8,128)S(1)} %copy-done.24, f32[512,1408]{1,0:T(8,128)S(1)} %copy-done.26, bf16[4,1920,256]{2,1,0:T(8,128)(2,1)S(1)} %bitcast.75, ...), custom_call_target="tpu_custom_call" | custom-call | flops 4026531840 | bytes 19136512 | tf_op jit(solution)/shard_map/grad_acts/pallas_call | solution.py:267
  331.3 10.1 %attend_back.2 = (f32[512,512]{1,0:T(8,128)S(1)}, f32[512,512]{1,0:T(8,128)S(1)}, f32[512,512]{1,0:T(8,128)S(1)}, f32[512,512]{1,0:T(8,128)S(1)}, f32[512,512]{1,0:T(8,128)S(1)}) custom-call(bf16[3,512,512]{2,1,0:T(8,128)(2,1)S(1)} %copy-done.61, bf16[3,512,512]{2,1,0:T(8,128)(2,1)S(1)} %copy-done.61, bf16[3,512,512]{2,1,0:T(8,128)(2,1)S(1)} %copy-done.61, ...), custom_call_target="tpu_custom_call" | custom-call | flops 5368709120 | bytes 10485760 | tf_op jit(solution)/shard_map/attend_back/pallas_call | solution.py:245
  346.3 12.2 %all-gather.8.cloned.1.call-done.seed_ref = bf16[512,2048]{1,0:T(8,128)(2,1)} async-done(((bf16[128,2048]{1,0:T(8,128)(2,1)}), bf16[512,2048]{1,0:T(8,128)(2,1)}) %all-gather.8.cloned.1.call-update) | async-done | bytes 2097168 | tf_op jit(solution)/shard_map/all_gather | solution.py:776
  360.4 8.2 %convolution_convert_fusion.2 = bf16[1920,1024]{1,0:T(8,128)(2,1)} fusion(bf16[1024,1920]{1,0:T(8,128)(2,1)} %constant_dynamic-update-slice_fusion, bf16[1024,2048]{1,0:T(8,128)(2,1)S(1)} %constant_dynamic-update-slice_fusion.6), kind=kOutput, calls=%fused_computation.6 | convolution fusion | flops 4028497920 | bytes 9961472 | tf_op jit(solution)/shard_map/dot_general | solution.py:91
  368.6 8.3 %grad_acts.3 = (bf16[512,512]{1,0:T(8,128)(2,1)S(1)}, bf16[512,2816]{1,0:T(8,128)(2,1)S(1)}) custom-call(s32[4]{0:T(128)S(1)} %pad_add_fusion.s_ref, bf16[512,2048]{1,0:T(8,128)(2,1)S(1)} %copy-done.12, f32[512,1408]{1,0:T(8,128)S(1)} %copy-done.20, f32[512,1408]{1,0:T(8,128)S(1)} %copy-done.22, bf16[4,1920,256]{2,1,0:T(8,128)(2,1)S(1)} %bitcast.76, ...), custom_call_target="tpu_custom_call" | custom-call | flops 4026531840 | bytes 19136512 | tf_op jit(solution)/shard_map/grad_acts/pallas_call | solution.py:267
  377.0 2.0 constant_dynamic-update-slice_fusion.9
  379.6 8.1 %add_convert_fusion.1 = bf16[1920,1024]{1,0:T(8,128)(2,1)} fusion(bf16[1920,1024]{1,0:T(8,128)(2,1)S(1)} %collective-permute-done.16, bf16[1024,1920]{1,0:T(8,128)(2,1)} %constant_dynamic-update-slice_fusion, bf16[1024,2048]{1,0:T(8,128)(2,1)S(1)} %constant_dynamic-update-slice_fusion.6), kind=kOutput, calls=%fused_computation.1 | convolution fusion | flops 4032430080 | bytes 13893632 | tf_op jit(solution)/shard_map/dot_general | solution.py:91
  387.7 3.8 constant_dynamic-update-slice_fusion.8
  391.5 10.7 %convolution_convert_fusion = bf16[1024,2816]{1,0:T(8,128)(2,1)} fusion(bf16[1024,1024]{1,0:T(8,128)(2,1)S(1)} %copy-done.80, bf16[1024,2816]{1,0:T(8,128)(2,1)} %constant_dynamic-update-slice_fusion.8), kind=kOutput, calls=%fused_computation.4 | convolution fusion | flops 5908463616 | bytes 13631488 | tf_op jit(solution)/shard_map/dot_general | solution.py:91
  402.9 16.3 %attend_back.3 = (bf16[1024,1536]{1,0:T(8,128)(2,1)}, f32[8,1536]{1,0:T(8,128)}) custom-call(bf16[3,512,512]{2,1,0:T(8,128)(2,1)} %copy-done.62, bf16[3,512,512]{2,1,0:T(8,128)(2,1)} %copy-done.60, bf16[3,512,512]{2,1,0:T(8,128)(2,1)} %copy-done.60, bf16[3,512,512]{2,1,0:T(8,128)(2,1)} %copy-done.62, bf16[3,512,512]{2,1,0:T(8,128)(2,1)} %copy-done.62, ...), custom_call_target="tpu_custom_call" | custom-call | flops 5368709120 | bytes 10485760 | tf_op jit(solution)/shard_map/attend_back/pallas_call | solution.py:245
  419.2 11.5 %add_convert_fusion = bf16[1024,2816]{1,0:T(8,128)(2,1)} fusion(bf16[1024,2816]{1,0:T(8,128)(2,1)} %collective-permute-done.17, bf16[1024,1024]{1,0:T(8,128)(2,1)} %copy-done.82, bf16[1024,2816]{1,0:T(8,128)(2,1)S(1)} %bitcast.87), kind=kOutput, calls=%fused_computation | convolution fusion | flops 5914230784 | bytes 19398656 | tf_op jit(solution)/shard_map/dot_general | solution.py:91
  430.7 5.1 convolution_convert_fusion.1
  435.8 16.3 %grad_normed.2 = (bf16[512,2048]{1,0:T(8,128)(2,1)}, f32[8,2048]{1,0:T(8,128)S(1)}, f32[8,2048]{1,0:T(8,128)S(1)}) custom-call(s32[4]{0:T(128)S(1)} %pad_add_fusion.s_ref, bf16[1024,1536]{1,0:T(8,128)(2,1)S(1)} %copy-done.67, bf16[512,2816]{1,0:T(8,128)(2,1)S(1)} %copy-done.18, bf16[512,2048]{1,0:T(8,128)(2,1)S(1)} %copy-done.57, ...), custom_call_target="tpu_custom_call" | custom-call | flops 9126805504 | bytes 28442624 | tf_op jit(solution)/shard_map/grad_normed/pallas_call | solution.py:267
  452.2 3.6 constant_dynamic-slice_fusion.12
  461.0 27.9 %collective-permute-done.19 = bf16[256,2816]{1,0:T(8,128)(2,1)S(1)} collective-permute-done((bf16[256,2816]{1,0:T(8,128)(2,1)}, bf16[256,2816]{1,0:T(8,128)(2,1)S(1)}, u32[]{:S(2)}, u32[]{:S(2)}) %collective-permute-start.19) | collective-permute-done | bytes 1441824 | tf_op jit(solution)/shard_map/ppermute | solution.py:743
  491.5 2.5 collective-permute-start.20
  494.1 18.4 %grad_normed.3 = (bf16[512,2048]{1,0:T(8,128)(2,1)}, f32[8,2048]{1,0:T(8,128)}, f32[8,2048]{1,0:T(8,128)}) custom-call(s32[4]{0:T(128)} %copy-done.53, bf16[1024,1536]{1,0:T(8,128)(2,1)} %get-tuple-element.134.qkv_ref, bf16[512,2816]{1,0:T(8,128)(2,1)} %copy-done.15, bf16[512,2048]{1,0:T(8,128)(2,1)} %copy-done.55, f32[512,128]{1,0:T(8,128)} %copy-done.59, ...), custom_call_target="tpu_custom_call" | custom-call | flops 9126805504 | bytes 28442624 | tf_op jit(solution)/shard_map/grad_normed/pallas_call | solution.py:267
  517.0 2.4 slice.159
  519.4 6.0 collective-permute-done.20
  525.4 2.9 add_add_fusion
  536.7 2.7 collective-permute-start.25
  539.4 7.0 %add_convert_fusion.2 = bf16[1024,1536]{1,0:T(8,128)(2,1)S(1)} fusion(bf16[1024,1536]{1,0:T(8,128)(2,1)} %collective-permute-done.28, bf16[1024,1024]{1,0:T(8,128)(2,1)} %copy-done.82, bf16[1024,1536]{1,0:T(8,128)(2,1)} %get-tuple-element.134.qkv_ref), kind=kOutput, calls=%fused_computation.2 | convolution fusion | flops 3225944064 | bytes 11534336 | tf_op jit(solution)/shard_map/dot_general | solution.py:91
  549.1 2.0 collective-permute-start.31
  556.4 12.3 %collective-permute-done.29 = bf16[256,1536]{1,0:T(8,128)(2,1)} collective-permute-done((bf16[256,1536]{1,0:T(8,128)(2,1)}, bf16[256,1536]{1,0:T(8,128)(2,1)}, u32[]{:S(2)}, u32[]{:S(2)}) %collective-permute-start.29) | collective-permute-done | bytes 786464 | tf_op jit(solution)/shard_map/ppermute | solution.py:743
  568.7 15.5 %collective-permute-done.31 = bf16[256,1536]{1,0:T(8,128)(2,1)} collective-permute-done((bf16[256,1536]{1,0:T(8,128)(2,1)}, bf16[256,1536]{1,0:T(8,128)(2,1)}, u32[]{:S(2)}, u32[]{:S(2)}) %collective-permute-start.31) | collective-permute-done | bytes 786464 | tf_op jit(solution)/shard_map/ppermute | solution.py:743
  585.6 2.2 add_add_fusion.1
  590.3 2.5 last.2.old_ref
  593.8 2.5 last.3
  (334 shorter events, 97.4 us)
Async XLA Ops:
  7.2 94.2 %all-gather.6.cloned.1.call-start = ((), (), s32[]{:S(2)}) async-start(), calls=%async_computation.5 | async-start | bytes 5242880 | tf_op jit(solution)/shard_map/all_gather | solution.py:776
  7.9 137.0 %all-gather.12.cloned.1.call-start = ((), (), s32[]{:S(2)}) async-start(), calls=%async_computation.13 | async-start | bytes 4915200 | tf_op jit(solution)/shard_map/all_gather | solution.py:782
  9.5 2.7 collective-permute-start
  12.1 208.8 %reduce-scatter.8.cloned.1.call-start = ((), (), s32[]{:S(2)}) async-start(), calls=%async_computation.7 | async-start | bytes 2621440 | tf_op jit(solution)/shard_map/reduce_scatter | solution.py:779
  12.2 4.1 collective-permute-start.1
  16.4 3.7 collective-permute-start.2
  20.2 32.4 %collective-permute-start.4 = (bf16[2,256,1408]{2,1,0:T(8,128)(2,1)}, bf16[2,256,1408]{2,1,0:T(8,128)(2,1)}, u32[]{:S(2)}, u32[]{:S(2)}) collective-permute-start(bf16[2,256,1408]{2,1,0:T(8,128)(2,1)} %param.20), channel_id=1, source_target_pairs={{0,16},{8,24},{16,0},{24,8},{1,17},{9,25},{17,1},{25,9},{2,18},{10... | collective-permute-start | bytes 4325384 | tf_op jit(solution)/shard_map/ppermute | solution.py:743
  22.3 31.7 %collective-permute-start.3 = (bf16[2,256,1408]{2,1,0:T(8,128)(2,1)}, bf16[2,256,1408]{2,1,0:T(8,128)(2,1)}, u32[]{:S(2)}, u32[]{:S(2)}) collective-permute-start(bf16[2,256,1408]{2,1,0:T(8,128)(2,1)} %param.20), channel_id=1, source_target_pairs={{0,8},{8,0},{16,24},{24,16},{1,9},{9,1},{17,25},{25,17},{2,10},{10... | collective-permute-start | bytes 4325384 | tf_op jit(solution)/shard_map/ppermute | solution.py:743
  24.3 3.8 collective-permute-start.5
  26.0 28.0 %copy-start.77 = (bf16[3,256,512]{2,1,0:T(8,128)(2,1)S(1)}, bf16[3,256,512]{2,1,0:T(8,128)(2,1)}, u32[]{:S(2)}) copy-start(bf16[3,256,512]{2,1,0:T(8,128)(2,1)} %param.17) | copy-start | bytes 2359300
  28.1 6.2 %collective-permute-start.6 = (f32[2,8,128]{2,1,0:T(8,128)S(1)}, f32[2,8,128]{2,1,0:T(8,128)S(1)}, u32[]{:S(2)}, u32[]{:S(2)}) collective-permute-start(f32[2,8,128]{2,1,0:T(8,128)S(1)} %pad_maximum_fusion.11), channel_id=1, source_target_pairs={{0,2},{1,3},{2,0},{3,1},{4,6},{5,7},{6,4},{7,5},{8,10},{9,11},{10,... | collective-permute-start | bytes 24584 | tf_op jit(solution)/shard_map/ppermute | solution.py:35
  54.0 31.0 %copy-start.78 = (bf16[3,256,512]{2,1,0:T(8,128)(2,1)S(1)}, bf16[3,256,512]{2,1,0:T(8,128)(2,1)}, u32[]{:S(2)}) copy-start(bf16[3,256,512]{2,1,0:T(8,128)(2,1)} %param.17) | copy-start | bytes 2359300
  54.0 16.4 %collective-permute-start.8 = (bf16[3,256,512]{2,1,0:T(8,128)(2,1)S(1)}, bf16[3,256,512]{2,1,0:T(8,128)(2,1)S(1)}, u32[]{:S(2)}, u32[]{:S(2)}) collective-permute-start(bf16[3,256,512]{2,1,0:T(8,128)(2,1)S(1)} %copy-done.77), channel_id=1, source_target_pairs={{0,16},{8,24},{16,0},{24,8},{1,17},{9,25},{17,1},{25,9},{2,18},{10... | collective-permute-start | bytes 2359304 | tf_op jit(solution)/shard_map/ppermute | solution.py:743
  54.4 18.4 %collective-permute-start.7 = (bf16[3,256,512]{2,1,0:T(8,128)(2,1)S(1)}, bf16[3,256,512]{2,1,0:T(8,128)(2,1)S(1)}, u32[]{:S(2)}, u32[]{:S(2)}) collective-permute-start(bf16[3,256,512]{2,1,0:T(8,128)(2,1)S(1)} %copy-done.77), channel_id=1, source_target_pairs={{0,8},{8,0},{16,24},{24,16},{1,9},{9,1},{17,25},{25,17},{2,10},{10... | collective-permute-start | bytes 2359304 | tf_op jit(solution)/shard_map/ppermute | solution.py:743
  70.5 12.3 %collective-permute-start.10 = (bf16[3,128,512]{2,1,0:T(8,128)(2,1)S(1)}, bf16[3,128,512]{2,1,0:T(8,128)(2,1)S(1)}, u32[]{:S(2)}, u32[]{:S(2)}) collective-permute-start(bf16[3,128,512]{2,1,0:T(8,128)(2,1)S(1)} %slice.143), channel_id=1, source_target_pairs={{0,8},{8,0},{16,24},{24,16},{1,9},{9,1},{17,25},{25,17},{2,10},{10... | collective-permute-start | bytes 1179656 | tf_op jit(solution)/shard_map/ppermute | solution.py:743
  72.8 12.1 %collective-permute-start.9 = (bf16[3,128,512]{2,1,0:T(8,128)(2,1)S(1)}, bf16[3,128,512]{2,1,0:T(8,128)(2,1)S(1)}, u32[]{:S(2)}, u32[]{:S(2)}) collective-permute-start(bf16[3,128,512]{2,1,0:T(8,128)(2,1)S(1)} %slice.142), channel_id=1, source_target_pairs={{0,16},{8,24},{16,0},{24,8},{1,17},{9,25},{17,1},{25,9},{2,18},{10... | collective-permute-start | bytes 1179656 | tf_op jit(solution)/shard_map/ppermute | solution.py:743
  75.3 19.3 %collective-permute-start.13 = (bf16[2,128,1408]{2,1,0:T(8,128)(2,1)S(1)}, bf16[2,128,1408]{2,1,0:T(8,128)(2,1)S(1)}, u32[]{:S(2)}, u32[]{:S(2)}) collective-permute-start(bf16[2,128,1408]{2,1,0:T(8,128)(2,1)S(1)} %slice.145), channel_id=1, source_target_pairs={{0,8},{8,0},{16,24},{24,16},{1,9},{9,1},{17,25},{25,17},{2,10},{10... | collective-permute-start | bytes 2162696 | tf_op jit(solution)/shard_map/ppermute | solution.py:743
  78.2 16.4 %collective-permute-start.12 = (bf16[2,128,1408]{2,1,0:T(8,128)(2,1)S(1)}, bf16[2,128,1408]{2,1,0:T(8,128)(2,1)S(1)}, u32[]{:S(2)}, u32[]{:S(2)}) collective-permute-start(bf16[2,128,1408]{2,1,0:T(8,128)(2,1)S(1)} %slice.144), channel_id=1, source_target_pairs={{0,16},{8,24},{16,0},{24,8},{1,17},{9,25},{17,1},{25,9},{2,18},{10... | collective-permute-start | bytes 2162696 | tf_op jit(solution)/shard_map/ppermute | solution.py:743
  86.9 25.9 %collective-permute-start.11 = (bf16[4,3,256,512]{3,2,1,0:T(8,128)(2,1)}, bf16[4,3,256,512]{3,2,1,0:T(8,128)(2,1)}, u32[]{:S(2)}, u32[]{:S(2)}) collective-permute-start(bf16[4,3,256,512]{3,2,1,0:T(8,128)(2,1)} %pad_maximum_fusion.1.w0_ref.refs_0_), channel_id=1, source_target_pairs={{0,4},{4,0},{1,5},{5,1},{2,6},{6,2},{3,7},{7,3},{8,12},{12,8},{9,1... | collective-permute-start | bytes 9437192 | tf_op jit(solution)/shard_map/ppermute | solution.py:27
  100.4 44.5 %collective-permute-start.14 = (bf16[4,2,256,1408]{3,2,1,0:T(8,128)(2,1)}, bf16[4,2,256,1408]{3,2,1,0:T(8,128)(2,1)}, u32[]{:S(2)}, u32[]{:S(2)}) collective-permute-start(bf16[4,2,256,1408]{3,2,1,0:T(8,128)(2,1)} %pad_maximum_fusion.w0_ref.refs_2_), channel_id=1, source_target_pairs={{0,4},{4,0},{1,5},{5,1},{2,6},{6,2},{3,7},{7,3},{8,12},{12,8},{9,1... | collective-permute-start | bytes 17301512 | tf_op jit(solution)/shard_map/ppermute | solution.py:27
  101.2 334.6 %copy-start.53 = (s32[4]{0:T(128)}, s32[4]{0:T(128)S(1)}, u32[]{:S(2)}) copy-start(s32[4]{0:T(128)S(1)} %pad_add_fusion.s_ref) | copy-start | bytes 52
  107.9 14.1 %copy-start.41 = (bf16[512,1024]{1,0:T(8,128)(2,1)}, bf16[512,1024]{1,0:T(8,128)(2,1)S(1)}, u32[]{:S(2)}) copy-start(bf16[512,1024]{1,0:T(8,128)(2,1)S(1)} %get-tuple-element.79.other_ref) | copy-start | bytes 3145732
  107.9 37.0 %copy-start.40 = (bf16[512,1024]{1,0:T(8,128)(2,1)}, bf16[512,1024]{1,0:T(8,128)(2,1)S(1)}, u32[]{:S(2)}) copy-start(bf16[512,1024]{1,0:T(8,128)(2,1)S(1)} %get-tuple-element.78.own_ref) | copy-start | bytes 3145732
  112.7 83.3 %copy-start.36 = (bf16[512,1024]{1,0:T(8,128)(2,1)}, bf16[512,1024]{1,0:T(8,128)(2,1)S(1)}, u32[]{:S(2)}) copy-start(bf16[512,1024]{1,0:T(8,128)(2,1)S(1)} %get-tuple-element.76.other_ref) | copy-start | bytes 3145732
  112.7 83.3 %copy-start.38 = (bf16[512,1024]{1,0:T(8,128)(2,1)}, bf16[512,1024]{1,0:T(8,128)(2,1)S(1)}, u32[]{:S(2)}) copy-start(bf16[512,1024]{1,0:T(8,128)(2,1)S(1)} %get-tuple-element.75.own_ref) | copy-start | bytes 3145732
  112.7 9.4 %copy-start.45 = (f32[3,4,1,128,128]{4,3,2,1,0:T(8,128)S(1)}, f32[3,4,1,128,128]{4,3,2,1,0:T(8,128)}, u32[]{:S(2)}) copy-start(f32[3,4,1,128,128]{4,3,2,1,0:T(8,128)} %get-tuple-element.151) | copy-start | bytes 2359300
  144.9 17.3 %copy-start.2 = (bf16[7680,256]{1,0:T(8,128)(2,1)S(1)}, bf16[7680,256]{1,0:T(8,128)(2,1)}, u32[]{:S(2)}) copy-start(bf16[7680,256]{1,0:T(8,128)(2,1)} %all-gather.12.cloned.1.call-done) | copy-start | bytes 11796484
  144.9 17.2 %collective-permute-start.15 = (bf16[4,1920,256]{2,1,0:T(8,128)(2,1)}, bf16[4,1920,256]{2,1,0:T(8,128)(2,1)S(1)}, u32[]{:S(2)}, u32[]{:S(2)}) collective-permute-start(bf16[4,1920,256]{2,1,0:T(8,128)(2,1)} %bitcast.72), channel_id=1, source_target_pairs={{0,4},{4,0},{1,5},{5,1},{2,6},{6,2},{3,7},{7,3},{8,12},{12,8},{9,1... | collective-permute-start | bytes 11796488 | tf_op jit(solution)/shard_map/ppermute | solution.py:27
  173.0 92.1 %reduce-scatter.6.cloned.1.call-start = ((), (), s32[]{:S(2)}) async-start(), calls=%async_computation.6 | async-start | bytes 2621440 | tf_op jit(solution)/shard_map/reduce_scatter | solution.py:779
  197.1 14.8 %copy-start.3 = (bf16[7680,256]{1,0:T(8,128)(2,1)S(1)}, bf16[7680,256]{1,0:T(8,128)(2,1)}, u32[]{:S(2)}) copy-start(bf16[7680,256]{1,0:T(8,128)(2,1)} %all-gather.12.cloned.1.call-done) | copy-start | bytes 11796484
  197.1 14.8 %copy-start.7 = (bf16[4,1920,256]{2,1,0:T(8,128)(2,1)S(1)}, bf16[4,1920,256]{2,1,0:T(8,128)(2,1)}, u32[]{:S(2)}) copy-start(bf16[4,1920,256]{2,1,0:T(8,128)(2,1)} %copy-done.6) | copy-start | bytes 11796484
  211.9 9.0 %copy-start.13 = (bf16[256,2048]{1,0:T(8,128)(2,1)S(1)}, bf16[256,2048]{1,0:T(8,128)(2,1)}, u32[]{:S(2)}) copy-start(bf16[256,2048]{1,0:T(8,128)(2,1)} %teach_ref.3) | copy-start | bytes 3145732
  211.9 9.0 %copy-start.14 = (bf16[256,2048]{1,0:T(8,128)(2,1)S(1)}, bf16[256,2048]{1,0:T(8,128)(2,1)}, u32[]{:S(2)}) copy-start(bf16[256,2048]{1,0:T(8,128)(2,1)} %cot_ref.3) | copy-start | bytes 3145732
  220.9 91.0 %all-gather.10.cloned.1.call-start = ((), (), s32[]{:S(2)}) async-start(), calls=%async_computation.9 | async-start | bytes 2621440 | tf_op jit(solution)/shard_map/all_gather | solution.py:776
  225.8 132.7 %all-gather.8.cloned.1.call-start = ((), (), s32[]{:S(2)}) async-start(), calls=%async_computation.8 | async-start | bytes 2621440 | tf_op jit(solution)/shard_map/all_gather | solution.py:776
  269.9 245.2 %reduce-scatter.14.cloned.1.call-start = ((), (), s32[]{:S(2)}) async-start(), calls=%async_computation.12 | async-start | bytes 4915200 | tf_op jit(solution)/shard_map/reduce_scatter | solution.py:821
  321.5 9.7 %copy-start.44 = (f32[3,4,1,128,128]{4,3,2,1,0:T(8,128)S(1)}, f32[3,4,1,128,128]{4,3,2,1,0:T(8,128)}, u32[]{:S(2)}) copy-start(f32[3,4,1,128,128]{4,3,2,1,0:T(8,128)} %get-tuple-element.150) | copy-start | bytes 2359300
  321.5 9.7 %copy-start.46 = (f32[3,4,1,128,128]{4,3,2,1,0:T(8,128)S(1)}, f32[3,4,1,128,128]{4,3,2,1,0:T(8,128)}, u32[]{:S(2)}) copy-start(f32[3,4,1,128,128]{4,3,2,1,0:T(8,128)} %get-tuple-element.151) | copy-start | bytes 2359300
  321.5 9.7 %copy-start.61 = (bf16[3,512,512]{2,1,0:T(8,128)(2,1)S(1)}, bf16[3,512,512]{2,1,0:T(8,128)(2,1)}, u32[]{:S(2)}) copy-start(bf16[3,512,512]{2,1,0:T(8,128)(2,1)} %copy-done.60) | copy-start | bytes 4718596
  321.5 9.7 %copy-start.63 = (bf16[3,512,512]{2,1,0:T(8,128)(2,1)S(1)}, bf16[3,512,512]{2,1,0:T(8,128)(2,1)}, u32[]{:S(2)}) copy-start(bf16[3,512,512]{2,1,0:T(8,128)(2,1)} %copy-done.62) | copy-start | bytes 4718596
  331.3 27.3 %copy-start.11 = (bf16[512,2048]{1,0:T(8,128)(2,1)S(1)}, bf16[512,2048]{1,0:T(8,128)(2,1)}, u32[]{:S(2)}) copy-start(bf16[512,2048]{1,0:T(8,128)(2,1)} %all-gather.10.cloned.1.call-done.seed_ref) | copy-start | bytes 6291460
  368.6 11.1 %collective-permute-start.16 = (bf16[1920,1024]{1,0:T(8,128)(2,1)}, bf16[1920,1024]{1,0:T(8,128)(2,1)S(1)}, u32[]{:S(2)}, u32[]{:S(2)}) collective-permute-start(bf16[1920,1024]{1,0:T(8,128)(2,1)} %convolution_convert_fusion.2), channel_id=1, source_target_pairs={{0,4},{4,0},{1,5},{5,1},{2,6},{6,2},{3,7},{7,3},{8,12},{12,8},{9,1... | collective-permute-start | bytes 11796488 | tf_op jit(solution)/shard_map/ppermute | solution.py:27
  402.3 16.9 %collective-permute-start.17 = (bf16[1024,2816]{1,0:T(8,128)(2,1)}, bf16[1024,2816]{1,0:T(8,128)(2,1)}, u32[]{:S(2)}, u32[]{:S(2)}) collective-permute-start(bf16[1024,2816]{1,0:T(8,128)(2,1)} %convolution_convert_fusion), channel_id=1, source_target_pairs={{0,4},{4,0},{1,5},{5,1},{2,6},{6,2},{3,7},{7,3},{8,12},{12,8},{9,1... | collective-permute-start | bytes 17301512 | tf_op jit(solution)/shard_map/ppermute | solution.py:27
  402.8 16.4 %slice-start = ((s8[5767168]{0:T(1024)(128)(4,1)}), s8[1572864]{0:T(1024)(128)(4,1)S(1)}, s32[]{:S(2)}) async-start(s8[5767168]{0:T(1024)(128)(4,1)} %bitcast.86), calls=%async_computation.14 | async-start | bytes 3145728
  402.8 186.5 %reduce-scatter.12.cloned.1.call-start = ((), (), s32[]{:S(2)}) async-start(), calls=%async_computation.11 | async-start | bytes 2621440 | tf_op jit(solution)/shard_map/reduce_scatter | solution.py:779
  402.8 16.3 %slice-start.1 = ((s8[5767168]{0:T(1024)(128)(4,1)}), s8[4194304]{0:T(1024)(128)(4,1)S(1)}, s32[]{:S(2)}) async-start(s8[5767168]{0:T(1024)(128)(4,1)} %bitcast.86), calls=%async_computation.15 | async-start | bytes 8388608
  419.1 11.6 %copy-start.67 = (bf16[1024,1536]{1,0:T(8,128)(2,1)S(1)}, bf16[1024,1536]{1,0:T(8,128)(2,1)}, u32[]{:S(2)}) copy-start(bf16[1024,1536]{1,0:T(8,128)(2,1)} %get-tuple-element.134.qkv_ref) | copy-start | bytes 9437188
  419.1 11.6 %copy-start.81 = (bf16[1024,1024]{1,0:T(8,128)(2,1)S(1)}, bf16[1024,1024]{1,0:T(8,128)(2,1)}, u32[]{:S(2)}) copy-start(bf16[1024,1024]{1,0:T(8,128)(2,1)} %copy-done.79) | copy-start | bytes 6291460
  452.1 140.7 %reduce-scatter.10.cloned.1.call-start = ((), (), s32[]{:S(2)}) async-start(), calls=%async_computation.10 | async-start | bytes 2621440 | tf_op jit(solution)/shard_map/reduce_scatter | solution.py:779
  455.8 33.1 %collective-permute-start.19 = (bf16[256,2816]{1,0:T(8,128)(2,1)}, bf16[256,2816]{1,0:T(8,128)(2,1)S(1)}, u32[]{:S(2)}, u32[]{:S(2)}) collective-permute-start(bf16[256,2816]{1,0:T(8,128)(2,1)} %get-tuple-element.140), channel_id=1, source_target_pairs={{0,16},{8,24},{16,0},{24,8},{1,17},{9,25},{17,1},{25,9},{2,18},{10... | collective-permute-start | bytes 4325384 | tf_op jit(solution)/shard_map/ppermute | solution.py:743
  456.8 33.3 %collective-permute-start.18 = (bf16[256,2816]{1,0:T(8,128)(2,1)}, bf16[256,2816]{1,0:T(8,128)(2,1)}, u32[]{:S(2)}, u32[]{:S(2)}) collective-permute-start(bf16[256,2816]{1,0:T(8,128)(2,1)} %get-tuple-element.141), channel_id=1, source_target_pairs={{0,8},{8,0},{16,24},{24,16},{1,9},{9,1},{17,25},{25,17},{2,10},{10... | collective-permute-start | bytes 4325384 | tf_op jit(solution)/shard_map/ppermute | solution.py:743
  461.0 78.5 %collective-permute-start.28 = (bf16[1024,1536]{1,0:T(8,128)(2,1)}, bf16[1024,1536]{1,0:T(8,128)(2,1)}, u32[]{:S(2)}, u32[]{:S(2)}) collective-permute-start(bf16[1024,1536]{1,0:T(8,128)(2,1)} %convolution_convert_fusion.1), channel_id=1, source_target_pairs={{0,4},{4,0},{1,5},{5,1},{2,6},{6,2},{3,7},{7,3},{8,12},{12,8},{9,1... | collective-permute-start | bytes 9437192 | tf_op jit(solution)/shard_map/ppermute | solution.py:27
  491.5 33.8 %collective-permute-start.20 = (bf16[256,2816]{1,0:T(8,128)(2,1)S(1)}, bf16[256,2816]{1,0:T(8,128)(2,1)}, u32[]{:S(2)}, u32[]{:S(2)}) collective-permute-start(bf16[256,2816]{1,0:T(8,128)(2,1)S(1)} %constant_dynamic-slice_fusion.11), channel_id=1, source_target_pairs={{0,24},{8,16},{16,8},{24,0},{1,25},{9,17},{17,9},{25,1},{2,26},{10... | collective-permute-start | bytes 4325384 | tf_op jit(solution)/shard_map/ppermute | solution.py:743
  515.1 10.3 %copy-start.76 = (bf16[256,2816]{1,0:T(8,128)(2,1)S(1)}, bf16[256,2816]{1,0:T(8,128)(2,1)}, u32[]{:S(2)}) copy-start(bf16[256,2816]{1,0:T(8,128)(2,1)} %copy-done.75) | copy-start | bytes 4325380
  525.4 2.9 collective-permute-start.21
  528.3 4.8 collective-permute-start.23
  529.5 4.5 collective-permute-start.24
  531.3 3.6 collective-permute-start.22
  535.0 16.2 %collective-permute-start.27 = (f32[130]{0:T(256)S(1)}, f32[130]{0:T(256)S(1)}, u32[]{:S(2)}, u32[]{:S(2)}) collective-permute-start(f32[130]{0:T(256)S(1)} %bitcast.96), channel_id=1, source_target_pairs={{0,3},{1,2},{2,1},{3,0},{4,7},{5,6},{6,5},{7,4},{8,11},{9,10},{10,... | collective-permute-start | bytes 1568 | tf_op jit(solution)/shard_map/ppermute | solution.py:50
  536.3 17.6 %collective-permute-start.26 = (f32[130]{0:T(256)S(1)}, f32[130]{0:T(256)S(1)}, u32[]{:S(2)}, u32[]{:S(2)}) collective-permute-start(f32[130]{0:T(256)S(1)} %bitcast.95), channel_id=1, source_target_pairs={{0,2},{1,3},{2,0},{3,1},{4,6},{5,7},{6,4},{7,5},{8,10},{9,11},{10,... | collective-permute-start | bytes 1568 | tf_op jit(solution)/shard_map/ppermute | solution.py:50
  536.7 17.2 %collective-permute-start.25 = (f32[130]{0:T(256)S(1)}, f32[130]{0:T(256)S(1)}, u32[]{:S(2)}, u32[]{:S(2)}) collective-permute-start(f32[130]{0:T(256)S(1)} %bitcast.94), channel_id=1, source_target_pairs={{0,1},{1,0},{2,3},{3,2},{4,5},{5,4},{6,7},{7,6},{8,9},{9,8},{10,11... | collective-permute-start | bytes 1568 | tf_op jit(solution)/shard_map/ppermute | solution.py:50
  547.9 20.8 %collective-permute-start.29 = (bf16[256,1536]{1,0:T(8,128)(2,1)}, bf16[256,1536]{1,0:T(8,128)(2,1)}, u32[]{:S(2)}, u32[]{:S(2)}) collective-permute-start(bf16[256,1536]{1,0:T(8,128)(2,1)} %get-tuple-element.142), channel_id=1, source_target_pairs={{0,8},{8,0},{16,24},{24,16},{1,9},{9,1},{17,25},{25,17},{2,10},{10... | collective-permute-start | bytes 2359304 | tf_op jit(solution)/shard_map/ppermute | solution.py:743
  549.1 35.1 %collective-permute-start.31 = (bf16[256,1536]{1,0:T(8,128)(2,1)}, bf16[256,1536]{1,0:T(8,128)(2,1)}, u32[]{:S(2)}, u32[]{:S(2)}) collective-permute-start(bf16[256,1536]{1,0:T(8,128)(2,1)} %get-tuple-element.143), channel_id=1, source_target_pairs={{0,24},{8,16},{16,8},{24,0},{1,25},{9,17},{17,9},{25,1},{2,26},{10... | collective-permute-start | bytes 2359304 | tf_op jit(solution)/shard_map/ppermute | solution.py:743
  551.2 34.4 %collective-permute-start.30 = (bf16[256,1536]{1,0:T(8,128)(2,1)}, bf16[256,1536]{1,0:T(8,128)(2,1)}, u32[]{:S(2)}, u32[]{:S(2)}) collective-permute-start(bf16[256,1536]{1,0:T(8,128)(2,1)} %get-tuple-element.144), channel_id=1, source_target_pairs={{0,16},{8,24},{16,0},{24,8},{1,17},{9,25},{17,1},{25,9},{2,18},{10... | collective-permute-start | bytes 2359304 | tf_op jit(solution)/shard_map/ppermute | solution.py:743
  (63 other events, 177.9 us)
Sparse Core Ops, SparseCore 0:
  9.6 83.8 all-gather.5
  95.8 49.0 all-gather.11
  173.1 44.0 reduce-scatter.7
  221.0 44.0 reduce-scatter.5
  266.5 45.2 all-gather.9
  313.8 44.6 all-gather.7
  402.9 49.1 reduce-scatter.13
  454.4 43.8 reduce-scatter.11
  515.1 40.9 reduce-scatter.9

commit v4 on v3

--- a/solution.py
+++ b/solution.py
@@ -867,6 +867,9 @@
     back(1, qkv_back)
     qkv_held = after(qkv_held, grads[1], *gu_got)
     qkv_sum = with_other(dot_tn(normed_all[0], qkv_held), qkv_theirs)
+    qkv_got = sent_rows(qkv_sum, range(1, chips))
+    gu_grad = rows_of(gu_sum, 0).astype(f32) + sum(g.astype(f32) for g in gu_got)
+    qkv_grad = rows_of(qkv_sum, 0).astype(f32) + sum(g.astype(f32) for g in qkv_got)
     input_grad = None
     for t in range(2):
         input_grad = last(
@@ -885,14 +888,12 @@
         vector = jnp.stack([gains[h], shifts[h]]).reshape(2, chips, line, n)
         vector = cat([vector.transpose(1, 2, 0, 3).reshape(chips, line, 2 * n), scalar_sums], -1)
         small_sums.append(cat([vector.reshape(chips, -1), heads[h].reshape(chips, -1)], -1))
-    small_sums = [after(v, *gu_got) for v in small_sums]
+    small_sums = [after(v, qkv_got[0]) for v in small_sums]
     total = direct_sum(small_sums[0] + swap_core(small_sums[1]), "chip", chips)
-    qkv_got = sent_rows(after(qkv_sum, total), range(1, chips))
-    gu_grad = rows_of(gu_sum, 0).astype(f32) + sum(g.astype(f32) for g in gu_got)
-    qkv_grad = rows_of(qkv_sum, 0).astype(f32) + sum(g.astype(f32) for g in qkv_got)
     cut = line * (2 * n + 2)
     qkv_b_grad = total[cut:].reshape(3, -1)
-    total = direct_sum(total[:cut].reshape(line, -1), "tp", line)
+    total = after(total[:cut], input_grad).reshape(line, -1)
+    total = direct_sum(total, "tp", line)
     gain_grad, bias_grad = total[:n], total[n : 2 * n]
     loss_value = total[2 * n] / (total[2 * n + 1] * D)
     return (

time: 612 us -> 607 us (level)
  waiting for transfers between devices: 210 us -> 227 us
  starting transfers between devices: 50.2 us -> 38.2 us
  local copies, waits for them, and re-layouts: 85.4 us -> 79.2 us
    reduce_scatter x4, starting transfers between devices: 12.9 us -> 0.63 us  [summed_line(): return lax.psum_scatter(a, 'tp', scatter_dimension=0, tiled=True)]
    reduce_scatter x4, waiting for transfers between devices: 39.3 us -> 48.8 us  [summed_line(): return lax.psum_scatter(a, 'tp', scatter_dimension=0, tiled=True)]
    unnamed x176 -> x184, local copies, waits for them, and re-layouts: 59.1 us -> 55.3 us
  transfers between devices with their start and end apart: 41 -> 41, of which waited for: 21 -> 22; matrix products, arithmetic and copies ran while one was open for 12% -> 11% of each run, Pallas kernels for 26% -> 26%
where the time goes in v4:
time: 607 us; the launch traced here: 598 us
  waiting for transfers between devices  227 us (37%)
  Pallas kernels  164 us (27%)
  local copies, waits for them, and re-layouts  79.2 us (13%)
  matrix products  49.4 us (8%)
  starting transfers between devices  38.2 us (6%)
  other arithmetic  20 us (3%)
  between operations  19.6 us (3%)
    ppermute x14, waiting for transfers between devices, to_chip(): return lax.ppermute(a, 'chip', [(c, c ^ k) for c in range(chips)])  115 us
    pallas_call x12, Pallas kernels, call(): pl.pallas_call(kernel, grid_spec=pltpu.PrefetchScalarGridSpec(num_scalar_...  111 us
    unnamed x184, local copies, waits for them, and re-layouts  55.3 us
    dot_general x6, matrix products, dot_tn(): lax.dot_general(a, b, (((0,), (0,)), ((), ())), preferred_element_type=f32)  49.4 us
    reduce_scatter x4, waiting for transfers between devices, summed_line(): return lax.psum_scatter(a, 'tp', scatter_dimension=0, tiled=True)  48.8 us
    all_gather x3, waiting for transfers between devices, along_line(): return lax.all_gather(a, 'tp', axis=0, tiled=True)  46.4 us
    pallas_call x2, Pallas kernels, attend_back(): pl.pallas_call(functools.partial(attend_back_kernel, part, span), grid=(p...  25.9 us
    ppermute x14, starting transfers between devices, to_chip(): return lax.ppermute(a, 'chip', [(c, c ^ k) for c in range(chips)])  19.5 us
  transfers between devices with their start and end apart: 41, of which 22 were waited for; matrix products, arithmetic and copies ran while one was open for 11% of the time, Pallas kernels for 26%

profile of v4, /device:TPU:0, one launch (start us, length us, event | category | flops | bytes accessed | tf_op | source)
XLA Modules:
  0.0 597.8 jit_solution(16623521510139806009)
XLA Ops:
  9.9 2.2 pad_maximum_fusion.4
  12.2 2.6 collective-permute-start.1
  16.4 2.1 collective-permute-start.2
  20.2 2.1 collective-permute-start.4
  28.1 2.5 collective-permute-start.6
  31.9 2.4 collective-permute-done.6
  34.5 17.9 %collective-permute-done.4 = bf16[2,256,1408]{2,1,0:T(8,128)(2,1)S(1)} collective-permute-done((bf16[2,256,1408]{2,1,0:T(8,128)(2,1)}, bf16[2,256,1408]{2,1,0:T(8,128)(2,1)S(1)}, u32[]{:S(2)}, u32[]{:S(2)}) %collective-permute-start.4) | collective-permute-done | bytes 1441824 | tf_op jit(solution)/shard_map/ppermute | solution.py:743
  56.0 14.7 %collective-permute-done.8 = bf16[3,256,512]{2,1,0:T(8,128)(2,1)S(1)} collective-permute-done((bf16[3,256,512]{2,1,0:T(8,128)(2,1)}, bf16[3,256,512]{2,1,0:T(8,128)(2,1)S(1)}, u32[]{:S(2)}, u32[]{:S(2)}) %collective-permute-start.8) | collective-permute-done | bytes 786464 | tf_op jit(solution)/shard_map/ppermute | solution.py:743
  70.7 2.3 collective-permute-start.10
  77.4 5.6 collective-permute-done.10
  83.0 2.1 collective-permute-done.9
  85.7 9.1 %collective-permute-done.13 = bf16[2,128,1408]{2,1,0:T(8,128)(2,1)S(1)} collective-permute-done((bf16[2,128,1408]{2,1,0:T(8,128)(2,1)S(1)}, bf16[2,128,1408]{2,1,0:T(8,128)(2,1)S(1)}, u32[]{:S(2)}, u32[]{:S(2)}) %collective-permute-start.13) | collective-permute-done | bytes 720928 | tf_op jit(solution)/shard_map/ppermute | solution.py:743
  95.0 4.4 pad_maximum_fusion.w0_ref.refs_2_
  100.3 2.7 copy-done.1
  103.0 2.7 norm.3
  107.0 2.7 norm.2
  111.1 9.0 %joined.3.q_ref.k0_ref.v0_ref = bf16[3,512,512]{2,1,0:T(8,128)(2,1)S(1)} custom-call(s32[4]{0:T(128)S(1)} %pad_add_fusion.s_ref, bf16[512,1024]{1,0:T(8,128)(2,1)S(1)} %get-tuple-element.78.own_ref, bf16[512,1024]{1,0:T(8,128)(2,1)S(1)} %get-tuple-element.79.other_ref, f32[3,1,512]{2,1,0:T(1,128)S(1)} %reshape.121.bias_ref, f32[3,512,128]{2,1,0:T(8,128)S(1)} %bitcast.78, ...), custom_call_target="tpu_custom_call" | custom-call | flops 3221225472 | bytes 10754048 | tf_op jit(solution)/shard_map/joined/pallas_call | solution.py:267
  120.2 8.7 %joined.2.k1_ref.v1_ref.q_ref = bf16[3,512,512]{2,1,0:T(8,128)(2,1)S(1)} custom-call(s32[4]{0:T(128)S(1)} %pad_add_fusion.s_ref, bf16[512,1024]{1,0:T(8,128)(2,1)S(1)} %get-tuple-element.75.own_ref, bf16[512,1024]{1,0:T(8,128)(2,1)S(1)} %get-tuple-element.76.other_ref, f32[3,1,512]{2,1,0:T(1,128)S(1)} %reshape.121.bias_ref, f32[3,512,128]{2,1,0:T(8,128)S(1)} %bitcast.81, ...), custom_call_target="tpu_custom_call" | custom-call | flops 3221225472 | bytes 10754048 | tf_op jit(solution)/shard_map/joined/pallas_call | solution.py:267
  128.9 8.1 %attend.2 = (bf16[512,512]{1,0:T(8,128)(2,1)S(1)}, f32[4,4,256]{2,1,0:T(4,128)S(1)}) custom-call(bf16[3,512,512]{2,1,0:T(8,128)(2,1)S(1)} %joined.3.q_ref.k0_ref.v0_ref, bf16[3,512,512]{2,1,0:T(8,128)(2,1)S(1)} %joined.3.q_ref.k0_ref.v0_ref, bf16[3,512,512]{2,1,0:T(8,128)(2,1)S(1)} %joined.3.q_ref.k0_ref.v0_ref, ...), custom_call_target="tpu_custom_call" | custom-call | flops 2147483648 | bytes 5242880 | tf_op jit(solution)/shard_map/attend/pallas_call | solution.py:153
  138.2 6.7 %all-gather.12.cloned.1.call-done = bf16[7680,256]{1,0:T(8,128)(2,1)} async-done(((bf16[1920,256]{1,0:T(8,128)(2,1)}), bf16[7680,256]{1,0:T(8,128)(2,1)}) %all-gather.12.cloned.1.call-update) | async-done | bytes 3932176 | tf_op jit(solution)/shard_map/all_gather | solution.py:782
  144.9 11.7 %gate_up.2 = (f32[512,1408]{1,0:T(8,128)S(1)}, f32[512,1408]{1,0:T(8,128)S(1)}, bf16[512,1920]{1,0:T(8,128)(2,1)S(1)}) custom-call(s32[4]{0:T(128)S(1)} %pad_add_fusion.s_ref, bf16[512,1024]{1,0:T(8,128)(2,1)S(1)} %copy-done.45, bf16[512,1024]{1,0:T(8,128)(2,1)S(1)} %copy-done.47, bf16[512,512]{1,0:T(8,128)(2,1)S(1)} %get-tuple-element.80.attn_ref, ...), custom_call_target="tpu_custom_call" | custom-call | flops 5905580032 | bytes 21889024 | tf_op jit(solution)/shard_map/gate_up/pallas_call | solution.py:267
  159.9 7.7 %branch.2 = bf16[512,2048]{1,0:T(8,128)(2,1)} custom-call(s32[4]{0:T(128)S(1)} %pad_add_fusion.s_ref, bf16[512,1920]{1,0:T(8,128)(2,1)S(1)} %get-tuple-element.81.acts_ref, bf16[4,1920,256]{2,1,0:T(8,128)(2,1)S(1)} %bitcast.73, bf16[4,1920,256]{2,1,0:T(8,128)(2,1)S(1)} %collective-permute-done.15.w1_ref), custom_call_target="tpu_custom_call" | custom-call | flops 4026531840 | bytes 11927552 | tf_op jit(solution)/shard_map/branch/pallas_call | solution.py:267
  167.6 1.9 copy-done.6
  171.3 10.3 %attend.3 = (bf16[512,512]{1,0:T(8,128)(2,1)}, f32[4,4,256]{2,1,0:T(4,128)}) custom-call(bf16[3,512,512]{2,1,0:T(8,128)(2,1)} %copy-done.67, bf16[3,512,512]{2,1,0:T(8,128)(2,1)} %copy-done.65, bf16[3,512,512]{2,1,0:T(8,128)(2,1)} %copy-done.65, bf16[3,512,512]{2,1,0:T(8,128)(2,1)} %copy-done.67, bf16[3,512,512]{2,1,0:T(8,128)(2,1)} %copy-done.67), custom_call_target="tpu_custom_call" | custom-call | flops 2147483648 | bytes 5242880 | tf_op jit(solution)/shard_map/attend/pallas_call | solution.py:153
  182.7 11.7 %gate_up.3 = (f32[512,1408]{1,0:T(8,128)S(1)}, f32[512,1408]{1,0:T(8,128)S(1)}, bf16[512,1920]{1,0:T(8,128)(2,1)S(1)}) custom-call(s32[4]{0:T(128)S(1)} %pad_add_fusion.s_ref, bf16[512,1024]{1,0:T(8,128)(2,1)S(1)} %copy-done.42, bf16[512,1024]{1,0:T(8,128)(2,1)S(1)} %copy-done.39, bf16[512,512]{1,0:T(8,128)(2,1)S(1)} %copy-done.69, ...), custom_call_target="tpu_custom_call" | custom-call | flops 5905580032 | bytes 21889024 | tf_op jit(solution)/shard_map/gate_up/pallas_call | solution.py:267
  197.5 6.4 %branch.3 = bf16[512,2048]{1,0:T(8,128)(2,1)S(1)} custom-call(s32[4]{0:T(128)S(1)} %pad_add_fusion.s_ref, bf16[512,1920]{1,0:T(8,128)(2,1)S(1)} %get-tuple-element.85.acts_ref, bf16[4,1920,256]{2,1,0:T(8,128)(2,1)S(1)} %bitcast.74, bf16[4,1920,256]{2,1,0:T(8,128)(2,1)S(1)} %copy-done.7), custom_call_target="tpu_custom_call" | custom-call | flops 4026531840 | bytes 11927552 | tf_op jit(solution)/shard_map/branch/pallas_call | solution.py:267
  206.5 8.2 %reduce-scatter.8.cloned.1.call-done.branch_ref = bf16[128,2048]{1,0:T(8,128)(2,1)} async-done(((bf16[512,2048]{1,0:T(8,128)(2,1)}), bf16[128,2048]{1,0:T(8,128)(2,1)}) %reduce-scatter.8.cloned.1.call-update) | async-done | bytes 524304 | tf_op jit(solution)/shard_map/reduce_scatter | solution.py:779
  215.8 1.9 finish.2
  219.7 40.5 %reduce-scatter.6.cloned.1.call-done.branch_ref = bf16[128,2048]{1,0:T(8,128)(2,1)} async-done(((bf16[512,2048]{1,0:T(8,128)(2,1)}), bf16[128,2048]{1,0:T(8,128)(2,1)}) %reduce-scatter.6.cloned.1.call-update) | async-done | bytes 524304 | tf_op jit(solution)/shard_map/reduce_scatter | solution.py:779
  261.3 1.9 finish.3
  265.1 1.8 constant_dynamic-update-slice_fusion.3
  267.2 2.1 copy-done.31
  272.8 34.2 %all-gather.10.cloned.1.call-done.seed_ref = bf16[512,2048]{1,0:T(8,128)(2,1)} async-done(((bf16[128,2048]{1,0:T(8,128)(2,1)}), bf16[512,2048]{1,0:T(8,128)(2,1)}) %all-gather.10.cloned.1.call-update) | async-done | bytes 2097168 | tf_op jit(solution)/shard_map/all_gather | solution.py:776
  306.9 2.1 copy-done.4
  309.1 2.1 copy-done.8
  312.8 1.9 copy-done.26
  314.7 1.9 copy-done.28
  316.6 8.1 %grad_acts.2 = (bf16[512,512]{1,0:T(8,128)(2,1)S(1)}, bf16[512,2816]{1,0:T(8,128)(2,1)S(1)}) custom-call(s32[4]{0:T(128)S(1)} %pad_add_fusion.s_ref, bf16[512,2048]{1,0:T(8,128)(2,1)S(1)} %copy-done.10, f32[512,1408]{1,0:T(8,128)S(1)} %copy-done.26, f32[512,1408]{1,0:T(8,128)S(1)} %copy-done.28, bf16[4,1920,256]{2,1,0:T(8,128)(2,1)S(1)} %bitcast.75, ...), custom_call_target="tpu_custom_call" | custom-call | flops 4026531840 | bytes 19136512 | tf_op jit(solution)/shard_map/grad_acts/pallas_call | solution.py:267
  326.4 10.1 %attend_back.2 = (f32[512,512]{1,0:T(8,128)S(1)}, f32[512,512]{1,0:T(8,128)S(1)}, f32[512,512]{1,0:T(8,128)S(1)}, f32[512,512]{1,0:T(8,128)S(1)}, f32[512,512]{1,0:T(8,128)S(1)}) custom-call(bf16[3,512,512]{2,1,0:T(8,128)(2,1)S(1)} %copy-done.66, bf16[3,512,512]{2,1,0:T(8,128)(2,1)S(1)} %copy-done.66, bf16[3,512,512]{2,1,0:T(8,128)(2,1)S(1)} %copy-done.66, ...), custom_call_target="tpu_custom_call" | custom-call | flops 5368709120 | bytes 10485760 | tf_op jit(solution)/shard_map/attend_back/pallas_call | solution.py:245
  341.4 12.2 %all-gather.8.cloned.1.call-done.seed_ref = bf16[512,2048]{1,0:T(8,128)(2,1)} async-done(((bf16[128,2048]{1,0:T(8,128)(2,1)}), bf16[512,2048]{1,0:T(8,128)(2,1)}) %all-gather.8.cloned.1.call-update) | async-done | bytes 2097168 | tf_op jit(solution)/shard_map/all_gather | solution.py:776
  355.5 8.2 %convolution_convert_fusion.2 = bf16[1920,1024]{1,0:T(8,128)(2,1)} fusion(bf16[1024,1920]{1,0:T(8,128)(2,1)} %constant_dynamic-update-slice_fusion, bf16[1024,2048]{1,0:T(8,128)(2,1)S(1)} %constant_dynamic-update-slice_fusion.6), kind=kOutput, calls=%fused_computation.6 | convolution fusion | flops 4028497920 | bytes 9961472 | tf_op jit(solution)/shard_map/dot_general | solution.py:91
  363.7 8.3 %grad_acts.3 = (bf16[512,512]{1,0:T(8,128)(2,1)S(1)}, bf16[512,2816]{1,0:T(8,128)(2,1)S(1)}) custom-call(s32[4]{0:T(128)S(1)} %pad_add_fusion.s_ref, bf16[512,2048]{1,0:T(8,128)(2,1)S(1)} %copy-done.12, f32[512,1408]{1,0:T(8,128)S(1)} %copy-done.22, f32[512,1408]{1,0:T(8,128)S(1)} %copy-done.24, bf16[4,1920,256]{2,1,0:T(8,128)(2,1)S(1)} %bitcast.76, ...), custom_call_target="tpu_custom_call" | custom-call | flops 4026531840 | bytes 19136512 | tf_op jit(solution)/shard_map/grad_acts/pallas_call | solution.py:267
  372.1 2.0 constant_dynamic-update-slice_fusion.9
  374.7 8.1 %add_convert_fusion.1 = bf16[1920,1024]{1,0:T(8,128)(2,1)} fusion(bf16[1920,1024]{1,0:T(8,128)(2,1)S(1)} %collective-permute-done.16, bf16[1024,1920]{1,0:T(8,128)(2,1)} %constant_dynamic-update-slice_fusion, bf16[1024,2048]{1,0:T(8,128)(2,1)S(1)} %constant_dynamic-update-slice_fusion.6), kind=kOutput, calls=%fused_computation.1 | convolution fusion | flops 4032430080 | bytes 13893632 | tf_op jit(solution)/shard_map/dot_general | solution.py:91
  382.8 3.8 constant_dynamic-update-slice_fusion.8
  386.6 10.9 %convolution_convert_fusion = bf16[1024,2816]{1,0:T(8,128)(2,1)} fusion(bf16[1024,1024]{1,0:T(8,128)(2,1)S(1)} %copy-done.85, bf16[1024,2816]{1,0:T(8,128)(2,1)} %constant_dynamic-update-slice_fusion.8), kind=kOutput, calls=%fused_computation.4 | convolution fusion | flops 5908463616 | bytes 13631488 | tf_op jit(solution)/shard_map/dot_general | solution.py:91
  398.0 15.7 %attend_back.3 = (bf16[1024,1536]{1,0:T(8,128)(2,1)}, f32[8,1536]{1,0:T(8,128)}) custom-call(bf16[3,512,512]{2,1,0:T(8,128)(2,1)} %copy-done.67, bf16[3,512,512]{2,1,0:T(8,128)(2,1)} %copy-done.65, bf16[3,512,512]{2,1,0:T(8,128)(2,1)} %copy-done.65, bf16[3,512,512]{2,1,0:T(8,128)(2,1)} %copy-done.67, bf16[3,512,512]{2,1,0:T(8,128)(2,1)} %copy-done.67, ...), custom_call_target="tpu_custom_call" | custom-call | flops 5368709120 | bytes 10485760 | tf_op jit(solution)/shard_map/attend_back/pallas_call | solution.py:245
  413.8 12.0 %add_convert_fusion = bf16[1024,2816]{1,0:T(8,128)(2,1)} fusion(bf16[1024,2816]{1,0:T(8,128)(2,1)} %collective-permute-done.17, bf16[1024,1024]{1,0:T(8,128)(2,1)S(1)} %copy-done.87, bf16[1024,2816]{1,0:T(8,128)(2,1)} %constant_dynamic-update-slice_fusion.8), kind=kOutput, calls=%fused_computation | convolution fusion | flops 5914230784 | bytes 19398656 | tf_op jit(solution)/shard_map/dot_general | solution.py:91
  425.8 5.0 convolution_convert_fusion.1
  430.9 15.7 %grad_normed.2 = (bf16[512,2048]{1,0:T(8,128)(2,1)}, f32[8,2048]{1,0:T(8,128)S(1)}, f32[8,2048]{1,0:T(8,128)S(1)}) custom-call(s32[4]{0:T(128)S(1)} %pad_add_fusion.s_ref, bf16[1024,1536]{1,0:T(8,128)(2,1)S(1)} %copy-done.70, bf16[512,2816]{1,0:T(8,128)(2,1)S(1)} %copy-done.20, bf16[512,2048]{1,0:T(8,128)(2,1)S(1)} %copy-done.62, ...), custom_call_target="tpu_custom_call" | custom-call | flops 9126805504 | bytes 28442624 | tf_op jit(solution)/shard_map/grad_normed/pallas_call | solution.py:267
  446.7 3.6 constant_dynamic-slice_fusion.12
  455.9 27.9 %collective-permute-done.19 = bf16[256,2816]{1,0:T(8,128)(2,1)S(1)} collective-permute-done((bf16[256,2816]{1,0:T(8,128)(2,1)}, bf16[256,2816]{1,0:T(8,128)(2,1)S(1)}, u32[]{:S(2)}, u32[]{:S(2)}) %collective-permute-start.19) | collective-permute-done | bytes 1441824 | tf_op jit(solution)/shard_map/ppermute | solution.py:743
  486.6 2.2 collective-permute-start.20
  488.8 18.4 %grad_normed.3 = (bf16[512,2048]{1,0:T(8,128)(2,1)}, f32[8,2048]{1,0:T(8,128)}, f32[8,2048]{1,0:T(8,128)}) custom-call(s32[4]{0:T(128)} %copy-done.58, bf16[1024,1536]{1,0:T(8,128)(2,1)} %get-tuple-element.130.qkv_ref, bf16[512,2816]{1,0:T(8,128)(2,1)} %copy-done.17, bf16[512,2048]{1,0:T(8,128)(2,1)} %copy-done.60, f32[512,128]{1,0:T(8,128)} %copy-done.64, ...), custom_call_target="tpu_custom_call" | custom-call | flops 9126805504 | bytes 28442624 | tf_op jit(solution)/shard_map/grad_normed/pallas_call | solution.py:267
  509.9 1.9 slice.156
  511.8 2.4 slice.159
  514.2 6.0 %collective-permute-done.20 = bf16[256,2816]{1,0:T(8,128)(2,1)} collective-permute-done((bf16[256,2816]{1,0:T(8,128)(2,1)S(1)}, bf16[256,2816]{1,0:T(8,128)(2,1)}, u32[]{:S(2)}, u32[]{:S(2)}) %collective-permute-start.20) | collective-permute-done | bytes 1441824 | tf_op jit(solution)/shard_map/ppermute | solution.py:743
  520.2 2.9 add_add_fusion
  523.1 5.3 add_convert_fusion.2
  534.1 30.5 %collective-permute-done.22 = bf16[256,1536]{1,0:T(8,128)(2,1)S(1)} collective-permute-done((bf16[256,1536]{1,0:T(8,128)(2,1)S(1)}, bf16[256,1536]{1,0:T(8,128)(2,1)S(1)}, u32[]{:S(2)}, u32[]{:S(2)}) %collective-permute-start.22) | collective-permute-done | bytes 786464 | tf_op jit(solution)/shard_map/ppermute | solution.py:743
  573.7 2.5 last.2.old_ref
  577.2 2.5 last.3
  580.8 3.4 collective-permute-start.27
  584.2 2.5 pad_maximum_fusion.3
  (341 shorter events, 87.3 us)
Async XLA Ops:
  7.2 93.1 %all-gather.6.cloned.1.call-start = ((), (), s32[]{:S(2)}) async-start(), calls=%async_computation.5 | async-start | bytes 5242880 | tf_op jit(solution)/shard_map/all_gather | solution.py:776
  7.9 136.9 %all-gather.12.cloned.1.call-start = ((), (), s32[]{:S(2)}) async-start(), calls=%async_computation.13 | async-start | bytes 4915200 | tf_op jit(solution)/shard_map/all_gather | solution.py:782
  9.5 2.7 collective-permute-start
  12.1 202.7 %reduce-scatter.8.cloned.1.call-start = ((), (), s32[]{:S(2)}) async-start(), calls=%async_computation.7 | async-start | bytes 2621440 | tf_op jit(solution)/shard_map/reduce_scatter | solution.py:779
  12.2 4.1 collective-permute-start.1
  16.4 3.7 collective-permute-start.2
  20.2 32.3 %collective-permute-start.4 = (bf16[2,256,1408]{2,1,0:T(8,128)(2,1)}, bf16[2,256,1408]{2,1,0:T(8,128)(2,1)S(1)}, u32[]{:S(2)}, u32[]{:S(2)}) collective-permute-start(bf16[2,256,1408]{2,1,0:T(8,128)(2,1)} %param.20), channel_id=1, source_target_pairs={{0,16},{8,24},{16,0},{24,8},{1,17},{9,25},{17,1},{25,9},{2,18},{10... | collective-permute-start | bytes 4325384 | tf_op jit(solution)/shard_map/ppermute | solution.py:743
  22.3 31.7 %collective-permute-start.3 = (bf16[2,256,1408]{2,1,0:T(8,128)(2,1)}, bf16[2,256,1408]{2,1,0:T(8,128)(2,1)}, u32[]{:S(2)}, u32[]{:S(2)}) collective-permute-start(bf16[2,256,1408]{2,1,0:T(8,128)(2,1)} %param.20), channel_id=1, source_target_pairs={{0,8},{8,0},{16,24},{24,16},{1,9},{9,1},{17,25},{25,17},{2,10},{10... | collective-permute-start | bytes 4325384 | tf_op jit(solution)/shard_map/ppermute | solution.py:743
  24.3 3.8 collective-permute-start.5
  28.1 6.2 %collective-permute-start.6 = (f32[2,8,128]{2,1,0:T(8,128)S(1)}, f32[2,8,128]{2,1,0:T(8,128)S(1)}, u32[]{:S(2)}, u32[]{:S(2)}) collective-permute-start(f32[2,8,128]{2,1,0:T(8,128)S(1)} %pad_maximum_fusion.11), channel_id=1, source_target_pairs={{0,2},{1,3},{2,0},{3,1},{4,6},{5,7},{6,4},{7,5},{8,10},{9,11},{10,... | collective-permute-start | bytes 24584 | tf_op jit(solution)/shard_map/ppermute | solution.py:35
  52.4 32.7 %copy-start.77 = (bf16[2,256,1408]{2,1,0:T(8,128)(2,1)}, bf16[2,256,1408]{2,1,0:T(8,128)(2,1)S(1)}, u32[]{:S(2)}) copy-start(bf16[2,256,1408]{2,1,0:T(8,128)(2,1)S(1)} %collective-permute-done.4) | copy-start | bytes 4325380
  54.0 31.2 %copy-start.83 = (bf16[3,256,512]{2,1,0:T(8,128)(2,1)S(1)}, bf16[3,256,512]{2,1,0:T(8,128)(2,1)}, u32[]{:S(2)}) copy-start(bf16[3,256,512]{2,1,0:T(8,128)(2,1)} %param.17) | copy-start | bytes 2359300
  54.0 16.7 %collective-permute-start.8 = (bf16[3,256,512]{2,1,0:T(8,128)(2,1)}, bf16[3,256,512]{2,1,0:T(8,128)(2,1)S(1)}, u32[]{:S(2)}, u32[]{:S(2)}) collective-permute-start(bf16[3,256,512]{2,1,0:T(8,128)(2,1)} %param.17), channel_id=1, source_target_pairs={{0,16},{8,24},{16,0},{24,8},{1,17},{9,25},{17,1},{25,9},{2,18},{10... | collective-permute-start | bytes 2359304 | tf_op jit(solution)/shard_map/ppermute | solution.py:743
  54.4 18.6 %collective-permute-start.7 = (bf16[3,256,512]{2,1,0:T(8,128)(2,1)}, bf16[3,256,512]{2,1,0:T(8,128)(2,1)S(1)}, u32[]{:S(2)}, u32[]{:S(2)}) collective-permute-start(bf16[3,256,512]{2,1,0:T(8,128)(2,1)} %param.17), channel_id=1, source_target_pairs={{0,8},{8,0},{16,24},{24,16},{1,9},{9,1},{17,25},{25,17},{2,10},{10... | collective-permute-start | bytes 2359304 | tf_op jit(solution)/shard_map/ppermute | solution.py:743
  70.7 12.3 %collective-permute-start.10 = (bf16[3,128,512]{2,1,0:T(8,128)(2,1)S(1)}, bf16[3,128,512]{2,1,0:T(8,128)(2,1)S(1)}, u32[]{:S(2)}, u32[]{:S(2)}) collective-permute-start(bf16[3,128,512]{2,1,0:T(8,128)(2,1)S(1)} %slice.143), channel_id=1, source_target_pairs={{0,8},{8,0},{16,24},{24,16},{1,9},{9,1},{17,25},{25,17},{2,10},{10... | collective-permute-start | bytes 1179656 | tf_op jit(solution)/shard_map/ppermute | solution.py:743
  73.0 12.1 %collective-permute-start.9 = (bf16[3,128,512]{2,1,0:T(8,128)(2,1)S(1)}, bf16[3,128,512]{2,1,0:T(8,128)(2,1)S(1)}, u32[]{:S(2)}, u32[]{:S(2)}) collective-permute-start(bf16[3,128,512]{2,1,0:T(8,128)(2,1)S(1)} %slice.142), channel_id=1, source_target_pairs={{0,16},{8,24},{16,0},{24,8},{1,17},{9,25},{17,1},{25,9},{2,18},{10... | collective-permute-start | bytes 1179656 | tf_op jit(solution)/shard_map/ppermute | solution.py:743
  74.4 20.4 %collective-permute-start.13 = (bf16[2,128,1408]{2,1,0:T(8,128)(2,1)S(1)}, bf16[2,128,1408]{2,1,0:T(8,128)(2,1)S(1)}, u32[]{:S(2)}, u32[]{:S(2)}) collective-permute-start(bf16[2,128,1408]{2,1,0:T(8,128)(2,1)S(1)} %slice.145), channel_id=1, source_target_pairs={{0,8},{8,0},{16,24},{24,16},{1,9},{9,1},{17,25},{25,17},{2,10},{10... | collective-permute-start | bytes 2162696 | tf_op jit(solution)/shard_map/ppermute | solution.py:743
  77.3 17.5 %collective-permute-start.12 = (bf16[2,128,1408]{2,1,0:T(8,128)(2,1)S(1)}, bf16[2,128,1408]{2,1,0:T(8,128)(2,1)S(1)}, u32[]{:S(2)}, u32[]{:S(2)}) collective-permute-start(bf16[2,128,1408]{2,1,0:T(8,128)(2,1)S(1)} %slice.144), channel_id=1, source_target_pairs={{0,16},{8,24},{16,0},{24,8},{1,17},{9,25},{17,1},{25,9},{2,18},{10... | collective-permute-start | bytes 2162696 | tf_op jit(solution)/shard_map/ppermute | solution.py:743
  85.6 34.5 %copy-start.15 = (bf16[4,3,256,512]{3,2,1,0:T(8,128)(2,1)}, bf16[4,3,256,512]{3,2,1,0:T(8,128)(2,1)S(1)}, u32[]{:S(2)}) copy-start(bf16[4,3,256,512]{3,2,1,0:T(8,128)(2,1)S(1)} %pad_maximum_fusion.1.w0_ref.refs_0_) | copy-start | bytes 9437188
  85.7 25.5 %collective-permute-start.11 = (bf16[4,3,256,512]{3,2,1,0:T(8,128)(2,1)S(1)}, bf16[4,3,256,512]{3,2,1,0:T(8,128)(2,1)}, u32[]{:S(2)}, u32[]{:S(2)}) collective-permute-start(bf16[4,3,256,512]{3,2,1,0:T(8,128)(2,1)S(1)} %pad_maximum_fusion.1.w0_ref.refs_0_), channel_id=1, source_target_pairs={{0,4},{4,0},{1,5},{5,1},{2,6},{6,2},{3,7},{7,3},{8,12},{12,8},{9,1... | collective-permute-start | bytes 9437192 | tf_op jit(solution)/shard_map/ppermute | solution.py:27
  99.4 45.5 %collective-permute-start.14 = (bf16[4,2,256,1408]{3,2,1,0:T(8,128)(2,1)}, bf16[4,2,256,1408]{3,2,1,0:T(8,128)(2,1)}, u32[]{:S(2)}, u32[]{:S(2)}) collective-permute-start(bf16[4,2,256,1408]{3,2,1,0:T(8,128)(2,1)} %pad_maximum_fusion.w0_ref.refs_2_), channel_id=1, source_target_pairs={{0,4},{4,0},{1,5},{5,1},{2,6},{6,2},{3,7},{7,3},{8,12},{12,8},{9,1... | collective-permute-start | bytes 17301512 | tf_op jit(solution)/shard_map/ppermute | solution.py:27
  100.1 330.7 %copy-start.58 = (s32[4]{0:T(128)}, s32[4]{0:T(128)S(1)}, u32[]{:S(2)}) copy-start(s32[4]{0:T(128)S(1)} %pad_add_fusion.s_ref) | copy-start | bytes 52
  107.0 13.1 %copy-start.44 = (bf16[512,1024]{1,0:T(8,128)(2,1)}, bf16[512,1024]{1,0:T(8,128)(2,1)S(1)}, u32[]{:S(2)}) copy-start(bf16[512,1024]{1,0:T(8,128)(2,1)S(1)} %get-tuple-element.78.own_ref) | copy-start | bytes 3145732
  107.0 13.1 %copy-start.46 = (bf16[512,1024]{1,0:T(8,128)(2,1)}, bf16[512,1024]{1,0:T(8,128)(2,1)S(1)}, u32[]{:S(2)}) copy-start(bf16[512,1024]{1,0:T(8,128)(2,1)S(1)} %get-tuple-element.79.other_ref) | copy-start | bytes 3145732
  128.9 16.0 %copy-start.45 = (bf16[512,1024]{1,0:T(8,128)(2,1)S(1)}, bf16[512,1024]{1,0:T(8,128)(2,1)}, u32[]{:S(2)}) copy-start(bf16[512,1024]{1,0:T(8,128)(2,1)} %copy-done.44) | copy-start | bytes 3145732
  128.9 16.0 %copy-start.47 = (bf16[512,1024]{1,0:T(8,128)(2,1)S(1)}, bf16[512,1024]{1,0:T(8,128)(2,1)}, u32[]{:S(2)}) copy-start(bf16[512,1024]{1,0:T(8,128)(2,1)} %copy-done.46) | copy-start | bytes 3145732
  144.9 15.0 %copy-start.2 = (bf16[7680,256]{1,0:T(8,128)(2,1)S(1)}, bf16[7680,256]{1,0:T(8,128)(2,1)}, u32[]{:S(2)}) copy-start(bf16[7680,256]{1,0:T(8,128)(2,1)} %all-gather.12.cloned.1.call-done) | copy-start | bytes 11796484
  144.9 15.0 %collective-permute-start.15 = (bf16[4,1920,256]{2,1,0:T(8,128)(2,1)}, bf16[4,1920,256]{2,1,0:T(8,128)(2,1)S(1)}, u32[]{:S(2)}, u32[]{:S(2)}) collective-permute-start(bf16[4,1920,256]{2,1,0:T(8,128)(2,1)} %bitcast.72), channel_id=1, source_target_pairs={{0,4},{4,0},{1,5},{5,1},{2,6},{6,2},{3,7},{7,3},{8,12},{12,8},{9,1... | collective-permute-start | bytes 11796488 | tf_op jit(solution)/shard_map/ppermute | solution.py:27
  170.7 10.9 %copy-start.39 = (bf16[512,1024]{1,0:T(8,128)(2,1)S(1)}, bf16[512,1024]{1,0:T(8,128)(2,1)}, u32[]{:S(2)}) copy-start(bf16[512,1024]{1,0:T(8,128)(2,1)} %copy-done.38) | copy-start | bytes 3145732
  170.7 10.8 %copy-start.42 = (bf16[512,1024]{1,0:T(8,128)(2,1)S(1)}, bf16[512,1024]{1,0:T(8,128)(2,1)}, u32[]{:S(2)}) copy-start(bf16[512,1024]{1,0:T(8,128)(2,1)} %copy-done.41) | copy-start | bytes 3145732
  170.8 89.5 %reduce-scatter.6.cloned.1.call-start = ((), (), s32[]{:S(2)}) async-start(), calls=%async_computation.6 | async-start | bytes 2621440 | tf_op jit(solution)/shard_map/reduce_scatter | solution.py:779
  182.7 14.9 %copy-start.3 = (bf16[7680,256]{1,0:T(8,128)(2,1)S(1)}, bf16[7680,256]{1,0:T(8,128)(2,1)}, u32[]{:S(2)}) copy-start(bf16[7680,256]{1,0:T(8,128)(2,1)} %all-gather.12.cloned.1.call-done) | copy-start | bytes 11796484
  182.7 14.9 %copy-start.7 = (bf16[4,1920,256]{2,1,0:T(8,128)(2,1)S(1)}, bf16[4,1920,256]{2,1,0:T(8,128)(2,1)}, u32[]{:S(2)}) copy-start(bf16[4,1920,256]{2,1,0:T(8,128)(2,1)} %copy-done.6) | copy-start | bytes 11796484
  197.5 17.3 %copy-start = (bf16[256,2048]{1,0:T(8,128)(2,1)S(1)}, bf16[256,2048]{1,0:T(8,128)(2,1)}, u32[]{:S(2)}) copy-start(bf16[256,2048]{1,0:T(8,128)(2,1)} %x_ref.7) | copy-start | bytes 3145732
  197.5 17.3 %copy-start.13 = (bf16[256,2048]{1,0:T(8,128)(2,1)S(1)}, bf16[256,2048]{1,0:T(8,128)(2,1)}, u32[]{:S(2)}) copy-start(bf16[256,2048]{1,0:T(8,128)(2,1)} %teach_ref.3) | copy-start | bytes 3145732
  197.5 17.3 %copy-start.14 = (bf16[256,2048]{1,0:T(8,128)(2,1)S(1)}, bf16[256,2048]{1,0:T(8,128)(2,1)}, u32[]{:S(2)}) copy-start(bf16[256,2048]{1,0:T(8,128)(2,1)} %cot_ref.3) | copy-start | bytes 3145732
  206.5 100.5 %all-gather.10.cloned.1.call-start = ((), (), s32[]{:S(2)}) async-start(), calls=%async_computation.9 | async-start | bytes 2621440 | tf_op jit(solution)/shard_map/all_gather | solution.py:776
  219.6 134.0 %all-gather.8.cloned.1.call-start = ((), (), s32[]{:S(2)}) async-start(), calls=%async_computation.8 | async-start | bytes 2621440 | tf_op jit(solution)/shard_map/all_gather | solution.py:776
  265.0 244.9 %reduce-scatter.14.cloned.1.call-start = ((), (), s32[]{:S(2)}) async-start(), calls=%async_computation.12 | async-start | bytes 4915200 | tf_op jit(solution)/shard_map/reduce_scatter | solution.py:821
  316.6 9.7 %copy-start.68 = (bf16[3,512,512]{2,1,0:T(8,128)(2,1)S(1)}, bf16[3,512,512]{2,1,0:T(8,128)(2,1)}, u32[]{:S(2)}) copy-start(bf16[3,512,512]{2,1,0:T(8,128)(2,1)} %copy-done.67) | copy-start | bytes 4718596
  326.4 27.3 %copy-start.11 = (bf16[512,2048]{1,0:T(8,128)(2,1)S(1)}, bf16[512,2048]{1,0:T(8,128)(2,1)}, u32[]{:S(2)}) copy-start(bf16[512,2048]{1,0:T(8,128)(2,1)} %all-gather.10.cloned.1.call-done.seed_ref) | copy-start | bytes 6291460
  363.6 11.1 %collective-permute-start.16 = (bf16[1920,1024]{1,0:T(8,128)(2,1)}, bf16[1920,1024]{1,0:T(8,128)(2,1)S(1)}, u32[]{:S(2)}, u32[]{:S(2)}) collective-permute-start(bf16[1920,1024]{1,0:T(8,128)(2,1)} %convolution_convert_fusion.2), channel_id=1, source_target_pairs={{0,4},{4,0},{1,5},{5,1},{2,6},{6,2},{3,7},{7,3},{8,12},{12,8},{9,1... | collective-permute-start | bytes 11796488 | tf_op jit(solution)/shard_map/ppermute | solution.py:27
  397.5 16.3 %collective-permute-start.17 = (bf16[1024,2816]{1,0:T(8,128)(2,1)}, bf16[1024,2816]{1,0:T(8,128)(2,1)}, u32[]{:S(2)}, u32[]{:S(2)}) collective-permute-start(bf16[1024,2816]{1,0:T(8,128)(2,1)} %convolution_convert_fusion), channel_id=1, source_target_pairs={{0,4},{4,0},{1,5},{5,1},{2,6},{6,2},{3,7},{7,3},{8,12},{12,8},{9,1... | collective-permute-start | bytes 17301512 | tf_op jit(solution)/shard_map/ppermute | solution.py:27
  398.0 174.6 %reduce-scatter.12.cloned.1.call-start = ((), (), s32[]{:S(2)}) async-start(), calls=%async_computation.11 | async-start | bytes 2621440 | tf_op jit(solution)/shard_map/reduce_scatter | solution.py:779
  398.0 15.8 %copy-start.87 = (bf16[1024,1024]{1,0:T(8,128)(2,1)S(1)}, bf16[1024,1024]{1,0:T(8,128)(2,1)}, u32[]{:S(2)}) copy-start(bf16[1024,1024]{1,0:T(8,128)(2,1)} %copy-done.86) | copy-start | bytes 6291460
  413.8 12.0 %copy-start.70 = (bf16[1024,1536]{1,0:T(8,128)(2,1)S(1)}, bf16[1024,1536]{1,0:T(8,128)(2,1)}, u32[]{:S(2)}) copy-start(bf16[1024,1536]{1,0:T(8,128)(2,1)} %get-tuple-element.130.qkv_ref) | copy-start | bytes 9437188
  446.6 129.5 %reduce-scatter.10.cloned.1.call-start = ((), (), s32[]{:S(2)}) async-start(), calls=%async_computation.10 | async-start | bytes 2621440 | tf_op jit(solution)/shard_map/reduce_scatter | solution.py:779
  450.3 33.6 %collective-permute-start.19 = (bf16[256,2816]{1,0:T(8,128)(2,1)}, bf16[256,2816]{1,0:T(8,128)(2,1)S(1)}, u32[]{:S(2)}, u32[]{:S(2)}) collective-permute-start(bf16[256,2816]{1,0:T(8,128)(2,1)} %get-tuple-element.140), channel_id=1, source_target_pairs={{0,16},{8,24},{16,0},{24,8},{1,17},{9,25},{17,1},{25,9},{2,18},{10... | collective-permute-start | bytes 4325384 | tf_op jit(solution)/shard_map/ppermute | solution.py:743
  451.6 33.6 %collective-permute-start.18 = (bf16[256,2816]{1,0:T(8,128)(2,1)}, bf16[256,2816]{1,0:T(8,128)(2,1)}, u32[]{:S(2)}, u32[]{:S(2)}) collective-permute-start(bf16[256,2816]{1,0:T(8,128)(2,1)} %get-tuple-element.141), channel_id=1, source_target_pairs={{0,8},{8,0},{16,24},{24,16},{1,9},{9,1},{17,25},{25,17},{2,10},{10... | collective-permute-start | bytes 4325384 | tf_op jit(solution)/shard_map/ppermute | solution.py:743
  455.9 67.2 %collective-permute-start.21 = (bf16[1024,1536]{1,0:T(8,128)(2,1)}, bf16[1024,1536]{1,0:T(8,128)(2,1)}, u32[]{:S(2)}, u32[]{:S(2)}) collective-permute-start(bf16[1024,1536]{1,0:T(8,128)(2,1)} %convolution_convert_fusion.1), channel_id=1, source_target_pairs={{0,4},{4,0},{1,5},{5,1},{2,6},{6,2},{3,7},{7,3},{8,12},{12,8},{9,1... | collective-permute-start | bytes 9437192 | tf_op jit(solution)/shard_map/ppermute | solution.py:27
  486.6 33.6 %collective-permute-start.20 = (bf16[256,2816]{1,0:T(8,128)(2,1)S(1)}, bf16[256,2816]{1,0:T(8,128)(2,1)}, u32[]{:S(2)}, u32[]{:S(2)}) collective-permute-start(bf16[256,2816]{1,0:T(8,128)(2,1)S(1)} %constant_dynamic-slice_fusion.11), channel_id=1, source_target_pairs={{0,24},{8,16},{16,8},{24,0},{1,25},{9,17},{17,9},{25,1},{2,26},{10... | collective-permute-start | bytes 4325384 | tf_op jit(solution)/shard_map/ppermute | solution.py:743
  509.9 10.3 %copy-start.82 = (bf16[256,2816]{1,0:T(8,128)(2,1)S(1)}, bf16[256,2816]{1,0:T(8,128)(2,1)}, u32[]{:S(2)}) copy-start(bf16[256,2816]{1,0:T(8,128)(2,1)} %copy-done.81) | copy-start | bytes 4325380
  528.6 36.0 %collective-permute-start.30 = (bf16[256,1536]{1,0:T(8,128)(2,1)S(1)}, bf16[256,1536]{1,0:T(8,128)(2,1)S(1)}, u32[]{:S(2)}, u32[]{:S(2)}) collective-permute-start(bf16[256,1536]{1,0:T(8,128)(2,1)S(1)} %get-tuple-element.142), channel_id=1, source_target_pairs={{0,16},{8,24},{16,0},{24,8},{1,17},{9,25},{17,1},{25,9},{2,18},{10... | collective-permute-start | bytes 2359304 | tf_op jit(solution)/shard_map/ppermute | solution.py:743
  530.2 34.3 %collective-permute-start.31 = (bf16[256,1536]{1,0:T(8,128)(2,1)S(1)}, bf16[256,1536]{1,0:T(8,128)(2,1)S(1)}, u32[]{:S(2)}, u32[]{:S(2)}) collective-permute-start(bf16[256,1536]{1,0:T(8,128)(2,1)S(1)} %get-tuple-element.143), channel_id=1, source_target_pairs={{0,24},{8,16},{16,8},{24,0},{1,25},{9,17},{17,9},{25,1},{2,26},{10... | collective-permute-start | bytes 2359304 | tf_op jit(solution)/shard_map/ppermute | solution.py:743
  531.7 32.8 %collective-permute-start.22 = (bf16[256,1536]{1,0:T(8,128)(2,1)S(1)}, bf16[256,1536]{1,0:T(8,128)(2,1)S(1)}, u32[]{:S(2)}, u32[]{:S(2)}) collective-permute-start(bf16[256,1536]{1,0:T(8,128)(2,1)S(1)} %get-tuple-element.144), channel_id=1, source_target_pairs={{0,8},{8,0},{16,24},{24,16},{1,9},{9,1},{17,25},{25,17},{2,10},{10... | collective-permute-start | bytes 2359304 | tf_op jit(solution)/shard_map/ppermute | solution.py:743
  534.1 38.5 %copy-start.35 = (f32[128,2048]{1,0:T(8,128)S(1)}, f32[128,2048]{1,0:T(8,128)}, u32[]{:S(2)}) copy-start(f32[128,2048]{1,0:T(8,128)} %copy-done.34) | copy-start | bytes 3145732
  534.1 38.5 %copy-start.59 = (s32[4]{0:T(128)S(1)}, s32[4]{0:T(128)}, u32[]{:S(2)}) copy-start(s32[4]{0:T(128)} %copy-done.58) | copy-start | bytes 52
  564.5 1.2 collective-permute-start.23
  565.8 4.8 collective-permute-start.25
  567.5 4.5 collective-permute-start.26
  569.0 3.6 collective-permute-start.24
  579.8 7.7 %collective-permute-start.29 = (f32[130]{0:T(256)S(1)}, f32[130]{0:T(256)S(1)}, u32[]{:S(2)}, u32[]{:S(2)}) collective-permute-start(f32[130]{0:T(256)S(1)} %bitcast.96), channel_id=1, source_target_pairs={{0,3},{1,2},{2,1},{3,0},{4,7},{5,6},{6,5},{7,4},{8,11},{9,10},{10,... | collective-permute-start | bytes 1568 | tf_op jit(solution)/shard_map/ppermute | solution.py:50
  580.6 6.8 %collective-permute-start.28 = (f32[130]{0:T(256)S(1)}, f32[130]{0:T(256)S(1)}, u32[]{:S(2)}, u32[]{:S(2)}) collective-permute-start(f32[130]{0:T(256)S(1)} %bitcast.95), channel_id=1, source_target_pairs={{0,2},{1,3},{2,0},{3,1},{4,6},{5,7},{6,4},{7,5},{8,10},{9,11},{10,... | collective-permute-start | bytes 1568 | tf_op jit(solution)/shard_map/ppermute | solution.py:50
  580.8 6.6 %collective-permute-start.27 = (f32[130]{0:T(256)S(1)}, f32[130]{0:T(256)S(1)}, u32[]{:S(2)}, u32[]{:S(2)}) collective-permute-start(f32[130]{0:T(256)S(1)} %bitcast.94), channel_id=1, source_target_pairs={{0,1},{1,0},{2,3},{3,2},{4,5},{5,4},{6,7},{7,6},{8,9},{9,8},{10,11... | collective-permute-start | bytes 1568 | tf_op jit(solution)/shard_map/ppermute | solution.py:50
  (67 other events, 266.2 us)
Sparse Core Ops, SparseCore 0:
  9.6 83.8 all-gather.5
  95.8 48.9 all-gather.11
  170.9 43.8 reduce-scatter.7
  217.0 43.1 reduce-scatter.5
  261.6 45.2 all-gather.9
  308.9 44.6 all-gather.7
  398.1 49.1 reduce-scatter.13
  449.6 43.8 reduce-scatter.11
  509.9 40.8 reduce-scatter.9
